TPU v7x, 32 devices: a whole 2x2x4 slice. The times are simulated.
32 devices in a mesh: grp: 2 (over y), seq: 4 (over z), head: 2 (over x), rep: 2 (over core).
Axes of the slice: x: 2, y: 2, z: 4, core: 2. Of those that a mesh axis runs over, the one named last changes fastest.
Arguments:
- spectrum: float32 [4, 3, 128, 4096], P('grp', None, ('seq', 'head', 'rep')), parts along dimension 0, may hold values from -6 to 6
- src_amp: float32 [32, 3], P('grp'), parts along dimension 0, may hold values from -6 to 6
- src_phase: float32 [32], P('grp'), parts along dimension 0, may hold values from -3.140625 to 3.140625
- src_mode: int32 [32], P('grp'), parts along dimension 0, may hold values from 1 to 4
- src_delay: int32 [32], P('grp'), parts along dimension 0, may hold values from 0 to 511
- src_bins: int32 [32, 2], P('grp'), parts along dimension 0, may hold values from 0 to 524287, as said below
- w_embed: bfloat16 [384, 1024], replicated, may hold values from -0.3125 to 0.3125
- norm_in: bfloat16 [1024], replicated, may hold values from 0.5 to 1.5
- w_z: bfloat16 [1024, 2048], P(None, ('head', 'rep')), may hold values from -0.1875 to 0.1875
- w_x: bfloat16 [1024, 2048], P(None, ('head', 'rep')), may hold values from -0.1875 to 0.1875
- w_bc: bfloat16 [1024, 256], replicated, may hold values from -0.1875 to 0.1875
- w_dt: bfloat16 [1024, 32], P(None, ('head', 'rep')), may hold values from -0.5625 to 0.5625
- dt_bias: float32 [32], P(('head', 'rep')), may hold values from -4 to -2
- a_log: float32 [32], P(('head', 'rep')), may hold values from -11 to -1.5
- conv_x: float32 [4, 2048], P(None, ('head', 'rep')), may hold values from -3 to 3
- conv_bc: float32 [4, 256], replicated, may hold values from -3 to 3
- norm_out: bfloat16 [2048], replicated, may hold values from 0.5 to 1.5
- w_out: bfloat16 [2048, 1024], replicated, may hold values from -0.125 to 0.125
Outputs:
- summary: bfloat16 [16384, 1024], P(('grp', 'seq', 'head', 'rep')), parts along dimension 0
There are 2 independent parts, one for each index of `grp`. A program takes and returns all parts, laid end to end along the dimension named above; an argument that names none is the same for every part. Nothing has to cross between parts.
Inputs may be any that keep to these rules, and one draw needn't show every extreme that they name: src_bins[s, 0] is the first frequency bin of source s and src_bins[s, 1] one past its last; the first is smaller than the second; some source starts at bin 0 and some has src_bins[s, 1] = 524287.
All inputs are finite; a program needn't handle non-finite values.
Results may differ from a plain program's by a relative error of at most 0.0065.
Values may be sent and summed in bfloat16 or wider, within the bound.
No kernel may reach another device: no remote copies, remote signals or barrier semaphores. Data moves between devices by JAX's collectives and lax.ppermute only.
A program may use at most 128 MiB of HBM per device.

v0:
```python
import math

import jax
import jax.numpy as jnp
from jax import lax
from jax.sharding import PartitionSpec as P

SPAN = 256


EPSILON = 1e-05
HIGHEST_MODE = lax.Precision.HIGHEST


def passed_along(shard, axis, by):
    devices = lax.axis_size(axis)
    pairs = [(i, i + by) for i in range(devices) if 0 <= i + by < devices]
    return lax.ppermute(shard, axis, pairs)


def carried_in(shard, axis, combine, identity):
    devices, place = (lax.axis_size(axis), lax.axis_index(axis))
    everything = jax.tree.map(
        lambda part, kind: lax.all_gather(part.astype(kind), axis),
        shard,
        (jnp.bfloat16, jnp.bfloat16),
    )
    start = jax.tree.map(
        lambda part, zero: jnp.broadcast_to(jnp.asarray(zero, part.dtype), part.shape),
        shard,
        identity,
    )

    def hop(k, before):
        reached = k < place
        new = combine(
            before, jax.tree.map(lambda part, own: part[k].astype(own.dtype), everything, shard)
        )
        return jax.tree.map(lambda a, b: jnp.where(reached, a, b), new, before)

    return lax.fori_loop(0, devices, hop, start)


def harmonic_angle(position, harmonic, lag_bins, phase_shift, length):
    turn_count = position * lag_bins % length * harmonic % length
    return harmonic.astype(phase_shift.dtype) * phase_shift + turn_count.astype(
        phase_shift.dtype
    ) * (2.0 * math.pi / length)


def rms_scale(values):
    return lax.rsqrt(jnp.mean(values * values, axis=-1, keepdims=True) + EPSILON)


def causal_conv(padded, kernel, row_count):
    accumulated = kernel[0][None, :] * padded[0:row_count].astype(jnp.float32)
    for tap_index in range(1, kernel.shape[0]):
        accumulated = accumulated + kernel[tap_index][None, :] * padded[
            tap_index : tap_index + row_count
        ].astype(jnp.float32)
    return jax.nn.silu(accumulated).astype(jnp.bfloat16)


def dft_table(order):
    counter = jnp.arange(order, dtype=jnp.int32)
    turn_count = counter[:, None] * counter[None, :] % order
    radians = turn_count.astype(jnp.float32) * (2.0 * math.pi / order)
    return (jnp.cos(radians), jnp.sin(radians))


def link_states(earlier_part, later_part):
    return (
        earlier_part[0] * later_part[0],
        later_part[0][:, None, None] * earlier_part[1] + later_part[1],
    )


def on_device(
    spectrum,
    src_amp,
    src_phase,
    src_mode,
    src_delay,
    src_bins,
    w_embed,
    norm_in,
    w_z,
    w_x,
    w_bc,
    w_dt,
    dt_bias,
    a_log,
    conv_x,
    conv_bc,
    norm_out,
    w_out,
):
    devices = lax.axis_size(("seq", "head", "rep"))
    position = lax.axis_index(("seq", "head", "rep"))
    _, channels, row_block, columns = spectrum.shape
    rows_all = row_block * devices
    length = rows_all * columns
    row_ids = position * row_block + jnp.arange(row_block, dtype=jnp.int32)
    column_ids = jnp.arange(columns, dtype=jnp.int32)
    freq_index = row_ids[:, None] + rows_all * column_ids[None, :]
    lower_bin = src_bins[:, 0][:, None, None]
    upper_bin = src_bins[:, 1][:, None, None]
    inside = jnp.where(
        (freq_index[None] >= lower_bin) & (freq_index[None] < upper_bin), 1.0, 0.0
    ).astype(jnp.float32)
    angle_now = harmonic_angle(
        freq_index[None],
        src_mode[:, None, None],
        src_delay[:, None, None],
        src_phase[:, None, None],
        length,
    )
    wave_pair = jnp.stack([inside * jnp.cos(angle_now), inside * jnp.sin(angle_now)])
    spectra = spectrum + jnp.einsum("sc,rsuv->rcuv", src_amp, wave_pair, precision=HIGHEST_MODE)
    cos_cols, sin_cols = dft_table(columns)
    flat_rows = spectra.reshape(2 * channels * row_block, columns)
    along_cos = jnp.dot(flat_rows, cos_cols, precision=HIGHEST_MODE).reshape(
        2, channels, row_block, columns
    )
    along_sin = jnp.dot(flat_rows, sin_cols, precision=HIGHEST_MODE).reshape(
        2, channels, row_block, columns
    )
    part_re = along_cos[0] - along_sin[1]
    part_im = along_sin[0] + along_cos[1]
    twist = (row_ids[:, None] * column_ids[None, :] % length).astype(jnp.float32) * (
        2.0 * math.pi / length
    )
    twist_cos = jnp.cos(twist)
    twist_sin = jnp.sin(twist)
    section_one = jnp.stack(
        [part_re * twist_cos - part_im * twist_sin, part_re * twist_sin + part_im * twist_cos]
    )
    section_one = lax.all_to_all(
        section_one, ("seq", "head", "rep"), split_axis=3, concat_axis=2, tiled=True
    )
    cos_rows, sin_rows = dft_table(rows_all)
    tables = jnp.stack([cos_rows, sin_rows])
    mixed_ft = jnp.einsum("rcuq,kum->krcqm", section_one, tables, precision=HIGHEST_MODE)
    series = (
        jnp.stack([mixed_ft[0, 0] - mixed_ft[1, 1], mixed_ft[1, 0] + mixed_ft[0, 1]])
        * (1.0 / math.sqrt(length))
    ).astype(jnp.bfloat16)
    series = lax.all_to_all(series, ("seq", "head", "rep"), split_axis=3, concat_axis=2, tiled=True)
    series = jnp.transpose(series, (0, 1, 3, 2)).reshape(2, channels, row_block * columns)
    patch_len = w_embed.shape[0] // (2 * channels)
    tok_own = row_block * columns // patch_len
    patches = (
        series.reshape(2, channels, tok_own, patch_len)
        .transpose(2, 0, 1, 3)
        .reshape(tok_own, 2 * channels * patch_len)
    )
    share_count = lax.axis_size(("head", "rep"))
    tok_all = tok_own * share_count
    w_joined = jnp.concatenate([w_z, w_x, w_bc, w_dt], axis=1)
    embedded = jnp.dot(patches, w_embed, preferred_element_type=jnp.float32).astype(jnp.bfloat16)
    embedded_f = embedded.astype(jnp.float32)
    normed_mine = (embedded_f * rms_scale(embedded_f) * norm_in.astype(jnp.float32)).astype(
        jnp.bfloat16
    )
    projected = jnp.dot(
        lax.all_gather(normed_mine, ("head", "rep"), axis=0, tiled=True),
        w_joined,
        preferred_element_type=jnp.float32,
    )
    inner_width = w_z.shape[1]
    state_size = w_bc.shape[1] // 2
    gate_in = projected[:, :inner_width].astype(jnp.bfloat16)
    x_raw = projected[:, inner_width : 2 * inner_width].astype(jnp.bfloat16)
    bc_raw = projected[:, 2 * inner_width : 2 * inner_width + 2 * state_size].astype(jnp.bfloat16)
    dt_raw = projected[:, 2 * inner_width + 2 * state_size :]
    kernel_len = conv_x.shape[0]
    rim_x, rim_bc = passed_along(
        (x_raw[tok_all - kernel_len + 1 :], bc_raw[tok_all - kernel_len + 1 :]), "seq", 1
    )
    x_conv = causal_conv(jnp.concatenate([rim_x, x_raw], 0), conv_x, tok_all)
    bc_conv = causal_conv(jnp.concatenate([rim_bc, bc_raw], 0), conv_bc, tok_all)
    head_count = dt_bias.shape[0]
    head_dim = inner_width // head_count
    blocks = tok_all // SPAN
    x_blocks = x_conv.reshape(blocks, SPAN, head_count, head_dim)
    b_blocks = bc_conv[:, :state_size].reshape(blocks, SPAN, state_size)
    c_blocks = bc_conv[:, state_size:].reshape(blocks, SPAN, state_size)
    step_size = jax.nn.softplus(dt_raw + dt_bias[None, :])
    step_blocks = step_size.reshape(blocks, SPAN, head_count)
    cumulative = jnp.cumsum(step_blocks * (-jnp.exp(a_log))[None, None, :], axis=1)
    by_head = jnp.transpose(cumulative, (0, 2, 1))
    causal_mask = jnp.arange(SPAN)[:, None] >= jnp.arange(SPAN)[None, :]
    spread = by_head[:, :, :, None] - by_head[:, :, None, :]
    segment = jnp.exp(jnp.where(causal_mask[None, None], spread, -jnp.inf))
    gram_matrix = jnp.einsum("nts,nks->ntk", c_blocks, b_blocks, preferred_element_type=jnp.float32)
    step_by_head = jnp.transpose(step_blocks, (0, 2, 1))
    scores = (gram_matrix[:, None] * segment * step_by_head[:, :, None, :]).astype(jnp.bfloat16)
    y_diag = jnp.einsum("nhtk,nkhp->nthp", scores, x_blocks, preferred_element_type=jnp.float32)
    block_end = cumulative[:, -1, :]
    weights_in = jnp.exp(block_end[:, None, :] - cumulative) * step_blocks
    weighted = (b_blocks.astype(jnp.float32)[:, :, None, :] * weights_in[..., None]).astype(
        jnp.bfloat16
    )
    states = jnp.einsum("nkhs,nkhp->nhsp", weighted, x_blocks, preferred_element_type=jnp.float32)
    block_decay = jnp.exp(block_end)

    def advance(carried, inputs):
        decay_now, state_now = inputs
        return (decay_now[:, None, None] * carried + state_now, carried)

    local_final, entering_local = lax.scan(
        advance, jnp.zeros((head_count, state_size, head_dim), jnp.float32), (block_decay, states)
    )
    through = jnp.cumprod(block_decay, axis=0)
    before = jnp.concatenate([jnp.ones((1, head_count), jnp.float32), through[:-1]], 0)
    identity_pair = (
        jnp.ones((head_count,), jnp.float32),
        jnp.zeros((head_count, state_size, head_dim), jnp.float32),
    )
    incoming = carried_in((through[-1], local_final), "seq", link_states, identity_pair)
    in_state = incoming[1]
    c_float = c_blocks.astype(jnp.float32)
    entering = entering_local + before[:, :, None, None] * in_state[None]
    y_off = jnp.einsum("nts,nhsp->nthp", c_float, entering, precision=HIGHEST_MODE)
    y_off = y_off * jnp.exp(cumulative)[..., None]
    y_all = (y_diag + y_off).reshape(tok_all, inner_width)
    gated_out = (y_all * jax.nn.silu(gate_in.astype(jnp.float32))).astype(jnp.bfloat16)
    mine_rows = lax.all_to_all(gated_out, ("head", "rep"), split_axis=0, concat_axis=1, tiled=True)
    mine_f = mine_rows.astype(jnp.float32)
    normed = (mine_f * rms_scale(mine_f) * norm_out.astype(jnp.float32)).astype(jnp.bfloat16)
    mixed_out = jnp.dot(normed, w_out, preferred_element_type=jnp.float32)
    return (embedded.astype(jnp.float32) + mixed_out).astype(jnp.bfloat16)


def solution(mesh):
    in_specs = (
        P("grp", None, ("seq", "head", "rep"), None),
        P("grp", None),
        P("grp"),
        P("grp"),
        P("grp"),
        P("grp", None),
        P(),
        P(),
        P(None, ("head", "rep")),
        P(None, ("head", "rep")),
        P(),
        P(None, ("head", "rep")),
        P(("head", "rep")),
        P(("head", "rep")),
        P(None, ("head", "rep")),
        P(),
        P(),
        P(),
    )
    out_specs = P(("grp", "seq", "head", "rep"), None)
    return jax.shard_map(
        on_device, mesh=mesh, in_specs=in_specs, out_specs=out_specs, check_vma=False
    )
```

profile of v0, /device:TPU:17, one launch (start us, length us, event | category | flops | bytes accessed | tf_op | source)
XLA Modules:
  0.0 919.0 jit_solution(11118588031213412508)
XLA Ops:
  9.4 10.2 %select_multiply_fusion.1 = (f32[1,16,8,4096]{3,1,2,0:T(8,128)S(1)}, f32[1,16,8,4096]{3,1,2,0:T(8,128)S(1)}) fusion(s32[8,4096]{1,0:T(8,128)S(1)} %broadcast_add_fusion, s32[16]{0:T(128)} %param.25, s32[16]{0:T(128)} %param.26, f32[16]{0:T(128)S(1)} %convert_multiply_fusion.3, s32[16]{0:T(128)S(1)} %get-tuple-element.250, s32[16]{0:T(128)S(1)} %get-tuple-element.249), kind=kLoop, calls=%fused_computation.73 | loop fusion | flops 17301504 | bytes 4325696 | tf_op jit(solution)/shard_map/mul | solution.py:118
  22.4 294.4 %fusion.5 = f32[48,4096]{1,0:T(8,128)S(1)} fusion(f32[48,4096]{1,0:T(8,128)S(1)} %bitcast.177), kind=kOutput, calls=%fused_computation.14 | convolution fusion | flops 9898557440 | bytes 1572864 | tf_op jit(solution)/shard_map/dot_general | solution.py:125
  316.8 280.0 %fusion.7 = f32[48,4096]{1,0:T(8,128)S(1)} fusion(f32[48,4096]{1,0:T(8,128)S(1)} %bitcast.178), kind=kOutput, calls=%fused_computation.16 | convolution fusion | flops 9898557440 | bytes 1572864 | tf_op jit(solution)/shard_map/dot_general | solution.py:122
  597.0 12.4 %copy.115 = f32[2,3,8,4096]{2,0,1,3:T(2,128)} copy(f32[2,3,8,4096]{3,2,1,0:T(8,128)S(1)} %pad_maximum_fusion.2) | data formatting | bytes 1572864 | tf_op jit(solution)/shard_map/stack | solution.py:135
  609.4 19.4 %reshape.519 = f32[16,1,12288]{2,1,0:T(1,128)} reshape(f32[4096,3,2,8]{3,2,1,0:T(2,128)} %bitcast.159) | data formatting | bytes 1572864
  628.9 6.5 all-to-all-start
  635.6 18.8 %all-to-all-done = f32[16,1,12288]{2,1,0:T(1,128)S(1)} async-done(((f32[16,1,12288]{2,1,0:T(1,128)}), f32[16,1,12288]{2,1,0:T(1,128)S(1)}, u32[]{:S(2)}, u32[]{:S(2)}) %all-to-all-start) | async-done | bytes 786464 | tf_op jit(solution)/shard_map/all_to_all | solution.py:138
  657.4 24.5 %reshape.520 = f32[4096,3,2,8]{3,2,1,0:T(2,128)} reshape(f32[16,12288]{1,0:T(8,128)S(1)} %reduce.4) | data formatting | bytes 1572864
  681.9 15.1 %copy.116 = f32[2,3,8,16,256]{4,2,3,1,0:T(8,128)S(1)} copy(f32[2,3,8,16,256]{2,0,1,4,3:T(2,128)} %bitcast.160) | data formatting | bytes 1572864 | tf_op jit(solution)/shard_map/all_to_all | solution.py:138
  699.8 5.1 all-to-all-start.1
  705.1 10.2 %all-to-all-done.1 = bf16[2,3,256,128]{2,0,1,3:T(2,128)(2,1)S(1)} async-done(((bf16[2,3,256,128]{2,0,1,3:T(2,128)(2,1)}), bf16[2,3,256,128]{2,0,1,3:T(2,128)(2,1)S(1)}, u32[]{:S(2)}, u32[]{:S(2)}) %all-to-all-start.1) | async-done | bytes 393248 | tf_op jit(solution)/shard_map/all_to_all | solution.py:148
  721.2 33.5 %all-gather.4.cloned.1.call-done = bf16[2048,1024]{1,0:T(8,128)(2,1)} async-done(((bf16[512,1024]{1,0:T(8,128)(2,1)}), bf16[2048,1024]{1,0:T(8,128)(2,1)}) %all-gather.4.cloned.1.call-update) | async-done | bytes 4194320 | tf_op jit(solution)/shard_map/all_gather | solution.py:166
  754.6 11.1 %fusion.105 = (bf16[2048,1288]{0,1:T(8,128)(2,1)}, f32[2048,1288]{0,1:T(8,128)S(1)}) fusion(bf16[2048,1024]{1,0:T(8,128)(2,1)} %all-gather.4.cloned.1.call-done, bf16[1024,8]{1,0:T(8,128)(2,1)S(1)} %copy.120, bf16[1024,256]{1,0:T(8,128)(2,1)} %param.32, bf16[1024,512]{1,0:T(8,128)(2,1)S(1)} %copy-done.21, bf16[1024,512]{1,0:T(8,128)(2,1)} %param.30), kind=kOutput, calls=%fused_computation.181 | convolution fusion | flops 5415452672 | bytes 22659072 | tf_op jit(solution)/shard_map/dot_general | solution.py:165
  766.0 4.5 reduce-window.6
  784.6 6.2 all-gather.1
  798.3 9.7 %multiply_convert_fusion.4 = bf16[2048,512]{0,1:T(8,128)(2,1)S(1)} fusion(bf16[2048,512]{0,1:T(8,128)(2,1)} %slice.167, bf16[3,512]{0,1:T(8,128)(2,1)} %collective-permute-done, f32[512]{0:T(512)} %bitcast.186, f32[512]{0:T(512)} %bitcast.187, f32[512]{0:T(512)S(1)} %bitcast.185, f32[512]{0:T(512)S(1)} %bitcast.184), kind=kLoop, calls=%fused_computation.49 | loop fusion | flops 26214400 | bytes 4205568 | tf_op jit(solution)/shard_map/convert_element_type | solution.py:61
  810.0 6.5 fusion.25
  816.4 16.3 %while.27 = (s32[]{:T(128)}, f32[8,128,64]{2,1,0:T(8,128)S(1)}, f32[8,8,128,64]{3,2,1,0:T(8,128)}, f32[8,8]{1,0:T(8,128)S(1)}, f32[8,8,128,64]{3,2,1,0:T(8,128)}, /*index=5*/s32[]{:T(128)}, s32[]{:T(128)}) while((s32[]{:T(128)}, f32[8,128,64]{2,1,0:T(8,128)S(1)}, f32[8,8,128,64]{3,2,1,0:T(8,128)}, f32[8,8]{1,0:T(8,128)S(1)}, ...), condition=%wide.region_4.5_spmd.clone, body=%wide.region_3.4_spmd.clone.sunk | while | flops 262147 | bytes 1573068 | solution.py:211
  832.9 14.2 %all-gather = bf16[32,128,64]{1,2,0:T(8,128)(2,1)S(1)} all-gather(bf16[8,128,64]{1,2,0:T(8,128)(2,1)S(1)} %copy.129), channel_id=2, replica_groups=mesh['grp'=2,'seq'=4,'head'=2,'rep'=2] {'seq'}, dimensions={0}, use_global_device_ids=true | all-gather | bytes 655360 | tf_op jit(solution)/shard_map/all_gather | solution.py:24
  848.6 4.7 multiply_add_fusion
  858.6 4.8 bitcast_add_fusion.1
  867.8 3.4 fusion.34
  872.7 8.2 all-to-all-start.2
  880.9 24.8 %all-to-all-done.2 = bf16[4,512,512]{1,2,0:T(8,128)(2,1)S(1)} async-done(((bf16[4,512,512]{1,2,0:T(8,128)(2,1)}), bf16[4,512,512]{1,2,0:T(8,128)(2,1)S(1)}, u32[]{:S(2)}, u32[]{:S(2)}) %all-to-all-start.2) | async-done | bytes 2097184 | tf_op jit(solution)/shard_map/all_to_all | solution.py:228
  (165 shorter events, 77.6 us)
Async XLA Ops:
  6.5 710.0 %copy-start = (bf16[384,1024]{1,0:T(8,128)(2,1)S(1)}, bf16[384,1024]{1,0:T(8,128)(2,1)}, u32[]{:S(2)}) copy-start(bf16[384,1024]{1,0:T(8,128)(2,1)} %param.28) | copy-start | bytes 2359300
  6.5 13.0 %copy-start.16 = (f32[16,3]{0,1:T(4,128)S(1)}, f32[16,3]{0,1:T(4,128)}, u32[]{:S(2)}) copy-start(f32[16,3]{0,1:T(4,128)} %param.23) | copy-start | bytes 580
  9.4 12.5 %copy-start.6 = (f32[2,3,8,4096]{3,2,1,0:T(8,128)S(1)}, f32[2,3,8,4096]{3,2,1,0:T(8,128)}, u32[]{:S(2)}) copy-start(f32[2,3,8,4096]{3,2,1,0:T(8,128)} %param.22) | copy-start | bytes 2359300
  316.8 280.0 %copy-start.7 = (f32[8,4096]{1,0:T(8,128)S(1)}, f32[8,4096]{1,0:T(8,128)}, u32[]{:S(2)}) copy-start(f32[8,4096]{1,0:T(8,128)} %get-tuple-element.251) | copy-start | bytes 393220
  316.8 280.0 %copy-start.8 = (f32[8,4096]{1,0:T(8,128)S(1)}, f32[8,4096]{1,0:T(8,128)}, u32[]{:S(2)}) copy-start(f32[8,4096]{1,0:T(8,128)} %get-tuple-element.252) | copy-start | bytes 393220
  628.9 25.5 %all-to-all-start = ((f32[16,1,12288]{2,1,0:T(1,128)}), f32[16,1,12288]{2,1,0:T(1,128)S(1)}, u32[]{:S(2)}, u32[]{:S(2)}) async-start(f32[16,1,12288]{2,1,0:T(1,128)} %reshape.519), calls=%async_computation | async-start | bytes 1572864 | tf_op jit(solution)/shard_map/all_to_all | solution.py:138
  697.0 8.1 copy-start.17
  699.8 15.6 %all-to-all-start.1 = ((bf16[2,3,256,128]{2,0,1,3:T(2,128)(2,1)}), bf16[2,3,256,128]{2,0,1,3:T(2,128)(2,1)S(1)}, u32[]{:S(2)}, u32[]{:S(2)}) async-start(bf16[2,3,256,128]{2,0,1,3:T(2,128)(2,1)} %copy.117), calls=%async_computation.1 | async-start | bytes 786432 | tf_op jit(solution)/shard_map/all_to_all | solution.py:148
  704.9 49.7 %all-gather.4.cloned.1.call-start = ((), (), s32[]{:S(2)}) async-start(), calls=%async_computation.3 | async-start | bytes 5242880 | tf_op jit(solution)/shard_map/all_gather | solution.py:166
  715.4 4.4 copy-start.12
  715.4 5.2 copy-start.22
  715.4 5.2 copy-start.15
  715.4 5.2 copy-start.13
  716.3 38.3 %copy-start.21 = (bf16[1024,512]{1,0:T(8,128)(2,1)S(1)}, bf16[1024,512]{1,0:T(8,128)(2,1)}, u32[]{:S(2)}) copy-start(bf16[1024,512]{1,0:T(8,128)(2,1)} %param.31) | copy-start | bytes 3145732
  721.2 44.6 %copy-start.19 = (f32[8]{0:T(128)S(1)}, f32[8]{0:T(128)}, u32[]{:S(2)}) copy-start(f32[8]{0:T(128)} %param.34) | copy-start | bytes 100
  773.4 17.9 %collective-permute-start.1 = (bf16[3,256]{0,1:T(8,128)(2,1)S(1)}, bf16[3,256]{0,1:T(8,128)(2,1)S(1)}, u32[]{:S(2)}, u32[]{:S(2)}) collective-permute-start(bf16[3,256]{0,1:T(8,128)(2,1)S(1)} %slice.172), channel_id=1, source_target_pairs={{0,4},{4,8},{8,12},{1,5},{5,9},{9,13},{2,6},{6,10},{10,14},{3,7},{... | collective-permute-start | bytes 4616 | tf_op jit(solution)/shard_map/ppermute | solution.py:18
  782.6 15.6 %collective-permute-start = (bf16[3,512]{0,1:T(8,128)(2,1)}, bf16[3,512]{0,1:T(8,128)(2,1)}, u32[]{:S(2)}, u32[]{:S(2)}) collective-permute-start(bf16[3,512]{0,1:T(8,128)(2,1)} %slice.166), channel_id=1, source_target_pairs={{0,4},{4,8},{8,12},{1,5},{5,9},{9,13},{2,6},{6,10},{10,14},{3,7},{... | collective-permute-start | bytes 9224 | tf_op jit(solution)/shard_map/ppermute | solution.py:18
  816.4 30.6 %copy-start.18 = (bf16[4,1,8]{2,0,1:T(4,128)(2,1)S(1)}, bf16[4,1,8]{2,0,1:T(4,128)(2,1)}, u32[]{:S(2)}) copy-start(bf16[4,1,8]{2,0,1:T(4,128)(2,1)} %copy.158) | copy-start | bytes 196
  856.4 2.2 copy-start.3
  856.4 2.2 copy-start.9
  856.4 2.2 copy-start.10
  871.2 9.7 %copy-start.14 = (bf16[2048]{0:T(1024)(128)(2,1)S(1)}, bf16[2048]{0:T(1024)(128)(2,1)}, u32[]{:S(2)}) copy-start(bf16[2048]{0:T(1024)(128)(2,1)} %param.38) | copy-start | bytes 12292
  872.7 33.0 %all-to-all-start.2 = ((bf16[4,512,512]{1,2,0:T(8,128)(2,1)}), bf16[4,512,512]{1,2,0:T(8,128)(2,1)S(1)}, u32[]{:S(2)}, u32[]{:S(2)}) async-start(bf16[4,512,512]{1,2,0:T(8,128)(2,1)} %bitcast.167), calls=%async_computation.2 | async-start | bytes 4194304 | tf_op jit(solution)/shard_map/all_to_all | solution.py:228
  905.7 2.5 copy-start.20
  (5 other events, 7.6 us)
Sparse Core Ops, SparseCore 0:
  719.8 34.7 all-gather.3
where the time goes:
time: 933 us; the launch traced here: 919 us
  matrix products  608 us (65%)
  local copies, waits for them, and re-layouts  100 us (11%)
  waiting for transfers between devices  87.3 us (9%)
  other arithmetic  62.8 us (7%)
  starting transfers between devices  25 us (3%)
  blocking collectives  20.3 us (2%)
  between operations  14.5 us (2%)
    dot_general x1, matrix products, on_device(): jnp.dot(flat_rows, sin_cols, precision=HIGHEST_MODE)  294 us
    dot_general x1, matrix products, on_device(): jnp.dot(flat_rows, cos_cols, precision=HIGHEST_MODE)  280 us
    unnamed x54, local copies, waits for them, and re-layouts  51.6 us
    all_gather x1, waiting for transfers between devices, on_device(): lax.all_gather(normed_mine, ('head', 'rep'), axis=0, tiled=True)  33.5 us
    all_to_all x1, waiting for transfers between devices, on_device(): lax.all_to_all(gated_out, ('head', 'rep'), split_axis=0, concat_axis=1, t...  24.8 us
    all_gather x2, blocking collectives, carried_in(): lax.all_gather(part.astype(kind), axis)  20.3 us
    all_to_all x1, waiting for transfers between devices, on_device(): lax.all_to_all(section_one, ('seq', 'head', 'rep'), split_axis=3, concat_...  18.8 us
  transfers between devices with their start and end apart: 6, of which 4 were waited for; matrix products, arithmetic and copies ran while one was open for 2% of the time, Pallas kernels for 0%

commit v1 on v0

v1 whole, which is shorter than its diff:
```python
import functools
import math

import jax
import jax.numpy as jnp
import ml_dtypes
import numpy as np
from jax import lax
from jax.experimental import pallas as pl
from jax.experimental.pallas import tpu as pltpu
from jax.sharding import PartitionSpec as P

SPAN = 256
EPSILON = 1e-05
LANES = 128
PATCH = 64
ALL = ("seq", "head", "rep")
HR = ("head", "rep")
F32 = jnp.float32
BF16 = jnp.bfloat16
VMEM = pl.BlockSpec(memory_space=pltpu.VMEM)
SMEM = pl.BlockSpec(memory_space=pltpu.SMEM)
PARAMS = pltpu.CompilerParams(vmem_limit_bytes=56 * 1024 * 1024)


def two_halves(table):
    high = table.astype(ml_dtypes.bfloat16)
    return high, (table - high.astype(np.float64)).astype(ml_dtypes.bfloat16)


def mm(a, b):
    return jnp.dot(a, b, preferred_element_type=F32)


def split(a):
    high = a.astype(BF16)
    return high, (a - high.astype(F32)).astype(BF16)


def lane_bins(inner):
    parts = PATCH // inner
    lane = np.arange(LANES)
    width = LANES // parts
    return lane // width + parts * (lane % width)


def inverse_fft(real, imag):
    count = len(real)
    if count == 1:
        return real, imag
    even_r, even_i = inverse_fft(real[0::2], imag[0::2])
    odd_r, odd_i = inverse_fft(real[1::2], imag[1::2])
    half = count // 2
    out_r, out_i = [None] * count, [None] * count
    for k in range(half):
        angle = 2.0 * math.pi * k / count
        c, s = math.cos(angle), math.sin(angle)
        if k == 0:
            r, i = odd_r[k], odd_i[k]
        elif 4 * k == count:
            r, i = -odd_i[k], odd_r[k]
        else:
            r = odd_r[k] * c - odd_i[k] * s
            i = odd_r[k] * s + odd_i[k] * c
        out_r[k], out_i[k] = even_r[k] + r, even_i[k] + i
        out_r[k + half], out_i[k + half] = even_r[k] - r, even_i[k] - i
    return out_r, out_i


def first_section(
    rows_all, length, pos, amp, phase, mode, delay, bins, turn_ref, x_ref, twist_ref, high_ref, low_ref,
    out_ref, base, acc, lhs,
):
    channels = amp.shape[1]
    sources = amp.shape[0]
    inner = x_ref.shape[2]
    row_block = x_ref.shape[3]
    shape = (row_block, LANES)
    row = pos[0] * row_block + lax.broadcasted_iota(jnp.int32, shape, 0)
    lane = lax.broadcasted_iota(jnp.int32, shape, 1)
    first_bin = row + rows_all * lane
    unit = 2.0 * math.pi / length

    def make_base(s, _):
        turn = ((((first_bin * delay[s]) & (length - 1)) * mode[s]) & (length - 1)).astype(F32)
        angle = mode[s].astype(F32) * phase[s] + turn * unit
        base[0, s] = jnp.cos(angle)
        base[1, s] = jnp.sin(angle)
        return 0

    lax.fori_loop(0, sources, make_base, 0)

    def add_sources(v, _):
        here = first_bin + (rows_all * LANES) * v
        total = [x_ref[r, c, v] for r in range(2) for c in range(channels)]
        for s in range(sources):
            which = (delay[s] * mode[s] * v) & (inner - 1)
            tr, ti = turn_ref[0, which], turn_ref[1, which]
            inside = (here >= bins[s, 0]) & (here < bins[s, 1])
            br, bi = base[0, s], base[1, s]
            real = jnp.where(inside, br * tr - bi * ti, 0.0)
            imag = jnp.where(inside, br * ti + bi * tr, 0.0)
            for c in range(channels):
                total[c] = total[c] + amp[s, c] * real
                total[channels + c] = total[channels + c] + amp[s, c] * imag
        for n in range(2 * channels):
            acc[n, v] = total[n]
        return 0

    lax.fori_loop(0, inner, add_sources, 0)

    def transform(c, _):
        real, imag = inverse_fft(
            [acc[c, v] for v in range(inner)], [acc[channels + c, v] for v in range(inner)]
        )
        for q in range(inner):
            tc, ts = twist_ref[0, q : q + 1, :], twist_ref[1, q : q + 1, :]
            lhs[c, q, :, 0:LANES] = real[q] * tc - imag[q] * ts
            lhs[c, q, :, LANES : 2 * LANES] = real[q] * ts + imag[q] * tc
        return 0

    lax.fori_loop(0, channels, transform, 0)

    wide = (inner, row_block, LANES)
    parts = PATCH // inner
    width = LANES // parts
    lanes = lax.broadcasted_iota(jnp.int32, wide, 2)
    outer = lax.div(lanes, width) + parts * lax.rem(lanes, width)
    column = lax.broadcasted_iota(jnp.int32, wide, 0) + inner * outer
    rows = pos[0] * row_block + lax.broadcasted_iota(jnp.int32, wide, 1)
    angle = ((rows * column) & (length - 1)).astype(F32) * unit
    cos, sin = jnp.cos(angle), jnp.sin(angle)
    for c in range(channels):
        high, low = split(lhs[c].reshape(inner * row_block, 2 * LANES))
        got = mm(high, high_ref[...]) + mm(low, high_ref[...]) + mm(high, low_ref[...])
        real = got[:, 0:LANES].reshape(wide)
        imag = got[:, LANES : 2 * LANES].reshape(wide)
        out_ref[:, c] = (real * cos - imag * sin).astype(BF16)
        out_ref[:, channels + c] = (real * sin + imag * cos).astype(BF16)


def run_first(spectrum, amp, phase, mode, delay, bins, pos, rows_all, length):
    _, channels, row_block, columns = spectrum.shape
    inner = columns // LANES
    grid_in = spectrum.reshape(2, channels, row_block, inner, LANES).transpose(0, 1, 3, 2, 4)
    steps = np.arange(inner)
    turn = 2.0 * np.pi * steps / inner
    turns = np.stack([np.cos(turn), np.sin(turn)]).astype(np.float32)
    lane = np.arange(LANES)
    twist = 2.0 * np.pi * (steps[:, None] * lane[None, :] % columns) / columns
    twists = np.stack([np.cos(twist), np.sin(twist)]).astype(np.float32)
    angle = 2.0 * np.pi * (lane[:, None] * lane_bins(inner)[None, :] % LANES) / LANES
    cos, sin = np.cos(angle), np.sin(angle)
    high, low = two_halves(np.block([[cos, sin], [-sin, cos]]))
    return pl.pallas_call(
        functools.partial(first_section, rows_all, length),
        out_shape=jax.ShapeDtypeStruct((inner, 2 * channels, row_block, LANES), BF16),
        in_specs=[SMEM] * 7 + [VMEM] * 4,
        out_specs=VMEM,
        scratch_shapes=[
            pltpu.VMEM((2, amp.shape[0], row_block, LANES), F32),
            pltpu.VMEM((2 * channels, inner, row_block, LANES), F32),
            pltpu.VMEM((channels, inner, row_block, 2 * LANES), F32),
        ],
        compiler_params=PARAMS,
        name="first_section",
    )(pos, amp, phase, mode, delay, bins, turns, grid_in, twists, high, low)


def second_section(z_ref, high_ref, low_ref, out_ref):
    devices, own, pairs, row_block, _ = z_ref.shape
    channels = pairs // 2
    rows = devices * row_block
    for q in range(own):
        for c in range(channels):
            right = jnp.concatenate(
                [z_ref[:, q, r * channels + c].astype(F32).reshape(rows, LANES) for r in range(2)], axis=0
            ).astype(BF16)
            got = mm(high_ref[...], right) + mm(low_ref[...], right)
            for r in range(2):
                out_ref[:, q * pairs + r * channels + c] = (
                    got[r * rows : (r + 1) * rows].reshape(devices, row_block, LANES).astype(BF16)
                )


def run_second(z, length):
    devices, own, pairs, row_block, _ = z.shape
    rows = devices * row_block
    counter = np.arange(rows)
    angle = 2.0 * np.pi * (counter[:, None] * counter[None, :] % rows) / rows
    cos, sin = np.cos(angle), np.sin(angle)
    high, low = two_halves(np.block([[cos, -sin], [sin, cos]]) / math.sqrt(length))
    return pl.pallas_call(
        second_section,
        out_shape=jax.ShapeDtypeStruct((devices, own * pairs, row_block, LANES), BF16),
        in_specs=[VMEM] * 3,
        out_specs=VMEM,
        compiler_params=PARAMS,
        name="second_section",
    )(z, high, low)


def order_patches(x_ref, perm_ref, out_ref, wide):
    devices, own, row_block, _ = x_ref.shape
    parts = perm_ref.shape[0]
    width = LANES // parts
    wide[...] = x_ref[...].astype(F32).reshape(devices * own * row_block, LANES)
    for m in range(row_block):
        rows = wide[pl.ds(m, devices * own, stride=row_block), :]
        across = rows.T.astype(BF16)
        total = mm(across[0:width], perm_ref[0])
        for n in range(1, parts):
            total = total + mm(across[n * width : (n + 1) * width], perm_ref[n])
        out_ref[m * width : (m + 1) * width, :] = total.astype(BF16)


def run_order(x, inner, channels):
    devices, own, row_block, _ = x.shape
    parts = PATCH // inner
    each = own // (2 * channels)
    perm = np.zeros((parts, devices * own, 2 * channels * PATCH), ml_dtypes.bfloat16)
    for n in range(parts):
        for j in range(devices):
            for q in range(each):
                for rc in range(2 * channels):
                    perm[n, j * own + q * 2 * channels + rc, rc * PATCH + n * inner + j * each + q] = 1
    return pl.pallas_call(
        order_patches,
        out_shape=jax.ShapeDtypeStruct((row_block * LANES // parts, 2 * channels * PATCH), BF16),
        in_specs=[VMEM] * 2,
        out_specs=VMEM,
        scratch_shapes=[pltpu.VMEM((devices * own * row_block, LANES), F32)],
        compiler_params=PARAMS,
        name="order_patches",
    )(x, perm)


def dft_table(order):
    counter = jnp.arange(order, dtype=jnp.int32)
    turn_count = counter[:, None] * counter[None, :] % order
    radians = turn_count.astype(F32) * (2.0 * math.pi / order)
    return jnp.stack([jnp.cos(radians), jnp.sin(radians)])


def make_patches(first, length):
    devices = lax.axis_size(ALL)
    inner, pairs, row_block, _ = first.shape
    channels = pairs // 2
    if inner % devices == 0:
        own = inner // devices
        moved = lax.all_to_all(
            first.reshape(devices, own, pairs, row_block, LANES), ALL, 0, 0, tiled=True
        )
        moved = lax.all_to_all(run_second(moved, length), ALL, 0, 0, tiled=True)
        return run_order(moved, inner, channels)
    flat = first.transpose(1, 2, 0, 3).reshape(2, channels, row_block, inner * LANES)
    flat = lax.all_to_all(flat, ALL, split_axis=3, concat_axis=2, tiled=True).astype(F32)
    mixed = jnp.einsum(
        "rcuq,kum->krcqm", flat, dft_table(row_block * devices), precision=lax.Precision.HIGHEST
    )
    series = jnp.stack([mixed[0, 0] - mixed[1, 1], mixed[1, 0] + mixed[0, 1]])
    series = (series * (1.0 / math.sqrt(length))).astype(BF16)
    series = lax.all_to_all(series, ALL, split_axis=4 - 1, concat_axis=2, tiled=True)
    parts = PATCH // inner
    series = series.reshape(2, channels, inner, parts, LANES // parts, row_block)
    return series.transpose(5, 4, 0, 1, 3, 2).reshape(
        row_block * LANES // parts, 2 * channels * PATCH
    )


def norm_rows(values, total):
    return lax.rsqrt(jnp.sum(values * values, axis=-1, keepdims=True) * (1.0 / total) + EPSILON)


def silu(values):
    return values * (1.0 / (1.0 + jnp.exp(-values)))


def scan_tokens(
    heads, per, me_ref, *refs,
):
    count = len(refs) - 23
    pats = refs[:count]
    (halo, we, nin, wz, wx, wbc, wdt, dtb, alog, cx, cbc, spread, yg_ref, fac_ref, c_ref, st_ref,
     xs, bcs, carried, total, y_acc, low_tri, pad) = refs[count:]
    block = pl.program_id(0)
    inner = wx.shape[1]
    head_dim = inner // heads
    state = wbc.shape[1] // 2
    taps = cx.shape[0]

    def features(p):
        embedded = mm(p, we[...]).astype(BF16).astype(F32)
        scale = norm_rows(embedded, embedded.shape[-1])
        return (embedded * scale * nin[...].astype(F32)).astype(BF16)

    @pl.when(block == 0)
    def _():
        carried[...] = jnp.zeros_like(carried)
        total[...] = jnp.zeros_like(total)
        before = features(halo[...])
        xs[0:8] = mm(before, wx[...]).astype(BF16).astype(F32)
        bcs[0:8] = mm(before, wbc[...]).astype(BF16).astype(F32)
        ri = lax.broadcasted_iota(jnp.int32, (SPAN, SPAN), 0)
        ci = lax.broadcasted_iota(jnp.int32, (SPAN, SPAN), 1)
        low_tri[...] = jnp.where(ri >= ci, 1.0, 0.0)

    @pl.when(block > 0)
    def _():
        xs[0:8] = xs[SPAN : SPAN + 8]
        bcs[0:8] = bcs[SPAN : SPAN + 8]

    which = (block // per) ^ me_ref[0]
    patch = pats[0][...]
    for d in range(1, count):
        patch = jnp.where(which == d, pats[d][...], patch)
    normed = features(patch)
    xs[8 : SPAN + 8] = mm(normed, wx[...]).astype(BF16).astype(F32)
    bcs[8 : SPAN + 8] = mm(normed, wbc[...]).astype(BF16).astype(F32)
    gate = silu(mm(normed, wz[...]).astype(BF16).astype(F32))
    step = mm(normed, wdt[...]) + dtb[...]
    step = jnp.maximum(step, 0.0) + jnp.log1p(jnp.exp(-jnp.abs(step)))

    def conv(buffer, kernel):
        out = kernel[0:1] * buffer[9 - taps : 9 - taps + SPAN]
        for i in range(1, taps):
            out = out + kernel[i : i + 1] * buffer[9 - taps + i : 9 - taps + i + SPAN]
        return silu(out)

    xc = conv(xs, cx).astype(BF16)
    bc = conv(bcs, cbc)
    bt = bc[:, :state].T.astype(BF16)
    cm = bc[:, state:].astype(BF16)
    c_ref[...] = cm
    cum = jnp.dot(
        low_tri[...], step * (-jnp.exp(alog[...])), precision=lax.Precision.HIGHEST,
        preferred_element_type=F32,
    )
    last = cum[SPAN - 1 : SPAN]
    cum_t = cum.T
    step_t = step.T
    gram = mm(cm, bt)
    inside = low_tri[...] > 0.5

    def expand(values):
        high, low = split(values)
        return mm(jnp.concatenate([high, low], axis=1), spread[...])

    for h in range(heads):
        gap = cum[:, h : h + 1] - cum_t[h : h + 1, :]
        seg = jnp.exp(jnp.where(inside, gap, -jnp.inf))
        scores = (gram * seg * step_t[h : h + 1, :]).astype(BF16)
        cols = slice(h * head_dim, (h + 1) * head_dim)
        y_acc[:, cols] = mm(scores, xc[:, cols])
    grown = expand(jnp.exp(cum))
    weights = expand(jnp.exp(last - cum) * step)
    rows8 = expand(jnp.concatenate(
        [jnp.exp(jnp.broadcast_to(last, (8, LANES))), jnp.exp(total[...])], axis=0))
    c_twice = jnp.concatenate([cm, cm], axis=1)
    high, low = split(carried[...])
    off = mm(c_twice, jnp.concatenate([high, low], axis=0))
    y = y_acc[...] + off * grown
    yg_ref[...] = (y * gate).astype(BF16)
    fac_ref[...] = (grown * rows8[8:9] * gate).astype(BF16)
    weighted = (xc.astype(F32) * weights).astype(BF16)
    carried[...] = carried[...] * rows8[0:1] + mm(bt, weighted)
    total[...] = total[...] + last

    @pl.when(block == pl.num_programs(0) - 1)
    def _():
        st_ref[0:state] = carried[...].astype(BF16)
        st_ref[state : state + 8] = (rows8[8:16] * rows8[0:8]).astype(BF16)


def run_scan(pats, halo, me, we, nin, wz, wx, wbc, wdt, dtb, alog, cx, cbc):
    own, width = pats[0].shape
    heads = dtb.shape[0]
    inner = wx.shape[1]
    state = wbc.shape[1] // 2
    tokens = own * len(pats)
    per = own // SPAN
    spread = np.zeros((2 * LANES, inner), ml_dtypes.bfloat16)
    for h in range(heads):
        spread[h, h * (inner // heads) : (h + 1) * (inner // heads)] = 1
    spread[LANES:] = spread[:LANES]
    more = LANES - heads
    wdt = jnp.pad(wdt, ((0, 0), (0, more)))
    dtb = jnp.pad(dtb, (0, more))[None]
    alog = jnp.pad(alog, (0, more))[None]
    consts = [halo, we, nin[None], wz, wx, wbc, wdt, dtb, alog, cx, cbc, spread]
    rows = lambda n: pl.BlockSpec((SPAN, n), lambda b, me: (b, 0))
    return pl.pallas_call(
        functools.partial(scan_tokens, heads, per),
        grid_spec=pltpu.PrefetchScalarGridSpec(
            num_scalar_prefetch=1,
            grid=(tokens // SPAN,),
            in_specs=[pl.BlockSpec((SPAN, width), lambda b, me: (b % per, 0))] * len(pats)
            + [VMEM] * len(consts),
            out_specs=[rows(inner), rows(inner), rows(state),
                       pl.BlockSpec((state + 8, inner), lambda b, me: (0, 0))],
            scratch_shapes=[
                pltpu.VMEM((SPAN + 8, inner), F32),
                pltpu.VMEM((SPAN + 8, 2 * state), F32),
                pltpu.VMEM((state, inner), F32),
                pltpu.VMEM((8, LANES), F32),
                pltpu.VMEM((SPAN, inner), F32),
                pltpu.VMEM((SPAN, SPAN), F32),
                pltpu.VMEM((8, LANES), F32),
            ],
        ),
        out_shape=[
            jax.ShapeDtypeStruct((tokens, inner), BF16),
            jax.ShapeDtypeStruct((tokens, inner), BF16),
            jax.ShapeDtypeStruct((tokens, state), BF16),
            jax.ShapeDtypeStruct((state + 8, inner), BF16),
        ],
        compiler_params=PARAMS,
        name="scan_tokens",
    )(me, *pats, *consts)


def correct(steps, me_ref, yg_ref, fac_ref, c_ref, *refs):
    earlier = refs[: len(refs) - steps - 1]
    outs = refs[len(earlier) : -1]
    start = refs[-1]
    step = pl.program_id(0)
    state = c_ref.shape[1]

    @pl.when(step == 0)
    def _():
        entering = jnp.zeros((state, yg_ref.shape[1]), F32)
        for part in reversed(earlier):
            entering = part[0:state].astype(F32) + part[state : state + 1].astype(F32) * entering
        high, low = split(entering)
        start[0:state] = high
        start[state : 2 * state] = low

    cm = c_ref[...]
    added = mm(jnp.concatenate([cm, cm], axis=1), start[...])
    value = (yg_ref[...].astype(F32) + fac_ref[...].astype(F32) * added).astype(BF16)
    for n in range(steps):
        @pl.when(step == n)
        def _(n=n):
            outs[n][...] = value


def run_correct(which, me, yg, fac, cm, earlier, own):
    inner, state = yg.shape[1], cm.shape[1]
    steps = len(which)
    first, stride = which[0], (which[1] - which[0] if steps > 1 else 0)
    block = lambda d, me: (me[0] ^ (first + stride * d), 0)
    return pl.pallas_call(
        functools.partial(correct, steps),
        grid_spec=pltpu.PrefetchScalarGridSpec(
            num_scalar_prefetch=1,
            grid=(steps,),
            in_specs=[pl.BlockSpec((own, inner), block)] * 2 + [pl.BlockSpec((own, state), block)]
            + [VMEM] * len(earlier),
            out_specs=[pl.BlockSpec((own, inner), lambda d, me: (0, 0))] * steps,
            scratch_shapes=[pltpu.VMEM((2 * state, inner), BF16)],
        ),
        out_shape=[jax.ShapeDtypeStruct((own, inner), BF16)] * steps,
        compiler_params=PARAMS,
        name="correct",
    )(me, yg, fac, cm, *earlier)


def finish(count, me_ref, pat_ref, we_ref, *refs):
    parts, norms, weights, out_ref = refs[:count], refs[count : 2 * count], refs[2 * count : -1], refs[-1]
    values = [p[...].astype(F32) for p in parts]
    square = values[0] * values[0]
    for v in values[1:]:
        square = square + v * v
    inner = values[0].shape[1]
    scale = lax.rsqrt(
        jnp.sum(square, axis=-1, keepdims=True) * (1.0 / (count * inner)) + EPSILON
    )
    out = mm(pat_ref[...], we_ref[...]).astype(BF16).astype(F32)
    mixed = None
    for v, n, w in zip(values, norms, weights):
        part = mm((v * scale * n[0].astype(F32)).astype(BF16), w[0])
        mixed = part if mixed is None else mixed + part
    out_ref[...] = (out + mixed).astype(BF16)


def run_finish(me, patches, we, parts, norm_out, w_out):
    count = len(parts)
    own, inner = parts[0].shape
    width = w_out.shape[1]
    tile = min(own, SPAN)
    norms = norm_out.reshape(count, 1, inner)
    weights = w_out.reshape(count, inner, width)
    pick = lambda shape: [
        pl.BlockSpec((1,) + shape, lambda i, me, d=d: (me[0] ^ d, 0, 0)) for d in range(count)
    ]
    return pl.pallas_call(
        functools.partial(finish, count),
        grid_spec=pltpu.PrefetchScalarGridSpec(
            num_scalar_prefetch=1,
            grid=(own // tile,),
            in_specs=[pl.BlockSpec((tile, patches.shape[1]), lambda i, me: (i, 0)), VMEM]
            + [pl.BlockSpec((tile, inner), lambda i, me: (i, 0))] * count
            + pick((1, inner)) + pick((inner, width)),
            out_specs=pl.BlockSpec((tile, width), lambda i, me: (i, 0)),
        ),
        out_shape=jax.ShapeDtypeStruct((own, width), BF16),
        compiler_params=PARAMS,
        name="finish",
    )(me, patches, we, *parts, *([norms] * count), *([weights] * count))


def swap(value, flip):
    count = lax.axis_size(HR)
    return lax.ppermute(value, HR, [(i, i ^ flip) for i in range(count)])


def shift(value, by):
    count = lax.axis_size("seq")
    return lax.ppermute(value, "seq", [(i, i + by) for i in range(count - by)])


def on_device(
    spectrum, src_amp, src_phase, src_mode, src_delay, src_bins, w_embed, norm_in, w_z, w_x, w_bc, w_dt,
    dt_bias, a_log, conv_x, conv_bc, norm_out, w_out,
):
    devices = lax.axis_size(ALL)
    share = lax.axis_size(HR)
    rows_all = spectrum.shape[2] * devices
    length = rows_all * spectrum.shape[3]
    pos = lax.axis_index(ALL).astype(jnp.int32).reshape(1)
    me = lax.axis_index(HR).astype(jnp.int32).reshape(1)
    first = run_first(
        spectrum, src_amp, src_phase, src_mode, src_delay, src_bins, pos, rows_all, length
    )
    patches = make_patches(first, length)
    own = patches.shape[0]
    pats = [patches]
    for d in range(1, share):
        pats.append(swap(pats[2], 1) if d == 3 else swap(patches, d))
    tail = pats[0][own - 8 :]
    for d in range(1, share):
        tail = jnp.where(me[0] ^ d == share - 1, pats[d][own - 8 :], tail)
    halo = shift(tail, 1)
    yg, fac, cm, ends = run_scan(
        pats, halo, me, w_embed, norm_in, w_z, w_x, w_bc, w_dt, dt_bias, a_log, conv_x, conv_bc
    )
    earlier = [shift(ends, d) for d in range(1, lax.axis_size("seq"))]
    far = run_correct(list(range(share // 2, share)), me, yg, fac, cm, earlier, own)
    near = run_correct(list(range(share // 2)), me, yg, fac, cm, earlier, own)
    gated = list(near) + list(far)
    parts = [gated[0]] + [swap(gated[d], d) for d in range(1, share)]
    return run_finish(me, patches, w_embed, parts, norm_out, w_out)


def solution(mesh):
    in_specs = (
        P("grp", None, ("seq", "head", "rep"), None),
        P("grp", None),
        P("grp"),
        P("grp"),
        P("grp"),
        P("grp", None),
        P(),
        P(),
        P(None, ("head", "rep")),
        P(None, ("head", "rep")),
        P(),
        P(None, ("head", "rep")),
        P(("head", "rep")),
        P(("head", "rep")),
        P(None, ("head", "rep")),
        P(),
        P(),
        P(),
    )
    out_specs = P(("grp", "seq", "head", "rep"), None)
    return jax.shard_map(
        on_device, mesh=mesh, in_specs=in_specs, out_specs=out_specs, check_vma=False
    )
```

time: 933 us -> 154 us (0.17)
  the two profiles are of different devices: /device:TPU:17 before, /device:TPU:27 now
where the time goes in v1:
time: 154 us; the launch traced here: 153 us
  Pallas kernels  58.9 us (38%)
  waiting for transfers between devices  42.8 us (28%)
  blocking collectives  32.8 us (21%)
  starting transfers between devices  10.1 us (7%)
  local copies, waits for them, and re-layouts  7.75 us (5%)
    pallas_call x1, Pallas kernels, run_scan(): pl.pallas_call(functools.partial(scan_tokens, heads, per), grid_spec=pltp...  32.6 us
    ppermute x6, waiting for transfers between devices, swap(): return lax.ppermute(value, HR, [(i, i ^ flip) for i in range(count)])  29.2 us
    all_to_all x1, blocking collectives, make_patches(): lax.all_to_all(first.reshape(devices, own, pairs, row_block, LANES), ALL,...  16.4 us
    all_to_all x1, blocking collectives, make_patches(): moved = lax.all_to_all(run_second(moved, length), ALL, 0, 0, tiled=True)  16.4 us
    ppermute x4, waiting for transfers between devices, shift(): return lax.ppermute(value, 'seq', [(i, i + by) for i in range(count - by)])  13.5 us
    pallas_call x1, Pallas kernels, run_first(): pl.pallas_call(functools.partial(first_section, rows_all, length), out_sh...  7.4 us
    pallas_call x1, Pallas kernels, run_finish(): pl.pallas_call(functools.partial(finish, count), grid_spec=pltpu.Prefetch...  7.18 us
    pallas_call x2, Pallas kernels, run_correct(): pl.pallas_call(functools.partial(correct, steps), grid_spec=pltpu.Prefetc...  6.71 us
  transfers between devices with their start and end apart: 10, of which 7 were waited for; matrix products, arithmetic and copies ran while one was open for 2% of the time, Pallas kernels for 2%

profile of v1, /device:TPU:27, one launch (start us, length us, event | category | flops | bytes accessed | tf_op | source)
XLA Modules:
  0.0 153.1 jit_solution(2880055394815738502)
XLA Ops:
  0.0 1.3 copy.30.amp
  1.3 1.3 copy.31.bins
  2.7 7.4 %first_section.1 = bf16[32,6,8,128]{3,2,1,0:T(8,128)(2,1)} custom-call(s32[1]{0:T(128)} %bitcast.1.pos, f32[16,3]{1,0:T(8,128)} %copy.30.amp, f32[16]{0:T(128)} %phase.1, s32[16]{0:T(128)} %mode.1, s32[16]{0:T(128)} %delay.1, s32[16,2]{1,0:T(8,128)} %copy.31.bins, f32[2,32]{1,0:T(2,128)} %constant.40.clone.turn_ref, f32[2,3,32,8,128]{4,3,2,1,0:T(8,128)} %bitcast.16, ...), custom_call_target="tpu_custom_call" | custom-call | tf_op jit(solution)/shard_map/first_section/pallas_call | solution.py:155
  10.1 16.4 %all_to_all.10.z_ref = bf16[16,2,6,8,128]{4,3,2,1,0:T(8,128)(2,1)} all-to-all(bf16[16,2,6,8,128]{4,3,2,1,0:T(8,128)(2,1)} %bitcast.15), channel_id=1, replica_groups=mesh['grp'=2,'seq'=4,'head'=2,'rep'=2] {'seq','head','rep'}, dimensions={0} | all-to-all | bytes 786432 | tf_op jit(solution)/shard_map/all_to_all | solution.py:251
  26.5 2.4 %second_section.1 = bf16[16,12,8,128]{3,2,1,0:T(8,128)(2,1)} custom-call(bf16[16,2,6,8,128]{4,3,2,1,0:T(8,128)(2,1)} %all_to_all.10.z_ref, bf16[256,256]{1,0:T(8,128)(2,1)} %constant.44.clone.high_ref, bf16[256,256]{1,0:T(8,128)(2,1)} %constant.45.clone.low_ref), custom_call_target="tpu_custom_call" | custom-call | tf_op jit(solution)/shard_map/second_section/pallas_call | solution.py:193
  28.9 16.4 %all_to_all.11.x_ref = bf16[16,12,8,128]{3,2,1,0:T(8,128)(2,1)} all-to-all(bf16[16,12,8,128]{3,2,1,0:T(8,128)(2,1)} %second_section.1), channel_id=1, replica_groups=mesh['grp'=2,'seq'=4,'head'=2,'rep'=2] {'seq','head','rep'}, dimensions={0} | all-to-all | bytes 786432 | tf_op jit(solution)/shard_map/all_to_all | solution.py:254
  45.3 2.6 %order_patches.1.refs_0_.pat_ref = bf16[512,384]{1,0:T(8,128)(2,1)} custom-call(bf16[16,12,8,128]{3,2,1,0:T(8,128)(2,1)} %all_to_all.11.x_ref, bf16[2,192,384]{2,1,0:T(8,128)(2,1)} %constant.46.clone.perm_ref), custom_call_target="tpu_custom_call" | custom-call | tf_op jit(solution)/shard_map/order_patches/pallas_call | solution.py:227
  48.7 9.9 %collective-permute-done.1.refs_2_ = bf16[512,384]{1,0:T(8,128)(2,1)S(1)} collective-permute-done((bf16[512,384]{1,0:T(8,128)(2,1)}, bf16[512,384]{1,0:T(8,128)(2,1)S(1)}, u32[]{:S(2)}, u32[]{:S(2)}) %collective-permute-start.1) | collective-permute-done | bytes 393248 | tf_op jit(solution)/shard_map/ppermute | solution.py:514
  58.7 1.0 collective-permute-start.2
  59.7 1.3 collective-permute-done.2.refs_3_
  61.7 1.3 collective-permute-start.3
  65.2 0.9 collective-permute-done.3.refs_4_
  66.7 32.6 %scan_tokens.1 = (bf16[2048,512]{1,0:T(8,128)(2,1)}, bf16[2048,512]{1,0:T(8,128)(2,1)}, bf16[2048,128]{1,0:T(8,128)(2,1)}, bf16[136,512]{1,0:T(8,128)(2,1)}) custom-call(s32[1]{0:T(128)} %bitcast.me_ref, bf16[512,384]{1,0:T(8,128)(2,1)} %order_patches.1.refs_0_.pat_ref, bf16[512,384]{1,0:T(8,128)(2,1)} %copy-done.7, bf16[512,384]{1,0:T(8,128)(2,1)} %copy-done.6, ...), custom_call_target="tpu_custom_call" | custom-call | tf_op jit(solution)/shard_map/scan_tokens/pallas_call | solution.py:392
  99.3 1.3 collective-permute-start.4
  100.6 1.3 collective-permute-start.5
  101.9 1.3 collective-permute-start.6
  103.2 2.1 %collective-permute-done.4.refs_0_ = bf16[136,512]{1,0:T(8,128)(2,1)S(1)} collective-permute-done((bf16[136,512]{1,0:T(8,128)(2,1)}, bf16[136,512]{1,0:T(8,128)(2,1)S(1)}, u32[]{:S(2)}, u32[]{:S(2)}) %collective-permute-start.4) | collective-permute-done | bytes 139296 | tf_op jit(solution)/shard_map/ppermute | solution.py:519
  105.3 10.5 %collective-permute-done.5.refs_1_ = bf16[136,512]{1,0:T(8,128)(2,1)S(1)} collective-permute-done((bf16[136,512]{1,0:T(8,128)(2,1)}, bf16[136,512]{1,0:T(8,128)(2,1)S(1)}, u32[]{:S(2)}, u32[]{:S(2)}) %collective-permute-start.5) | collective-permute-done | bytes 139296 | tf_op jit(solution)/shard_map/ppermute | solution.py:519
  116.5 3.3 %correct.3 = (bf16[512,512]{1,0:T(8,128)(2,1)}, bf16[512,512]{1,0:T(8,128)(2,1)}) custom-call(s32[1]{0:T(128)} %bitcast.me_ref, bf16[2048,512]{1,0:T(8,128)(2,1)} %get-tuple-element.13.yg_ref, bf16[2048,512]{1,0:T(8,128)(2,1)} %get-tuple-element.14.fac_ref, bf16[2048,128]{1,0:T(8,128)(2,1)} %get-tuple-element.15.c_ref, bf16[136,512]{1,0:T(8,128)(2,1)} %copy-done, ...), custom_call_target="tpu_custom_call" | custom-call | tf_op jit(solution)/shard_map/correct/pallas_call | solution.py:452
  119.8 3.2 %collective-permute-start.9 = (bf16[512,512]{1,0:T(8,128)(2,1)}, bf16[512,512]{1,0:T(8,128)(2,1)S(1)}, u32[]{:S(2)}, u32[]{:S(2)}) collective-permute-start(bf16[512,512]{1,0:T(8,128)(2,1)} %get-tuple-element.20), channel_id=1, source_target_pairs={{0,3},{1,2},{2,1},{3,0},{4,7},{5,6},{6,5},{7,4},{8,11},{9,10},{10,... | collective-permute-start | bytes 1572872 | tf_op jit(solution)/shard_map/ppermute | solution.py:514
  123.0 3.4 %correct.2 = (bf16[512,512]{1,0:T(8,128)(2,1)}, bf16[512,512]{1,0:T(8,128)(2,1)}) custom-call(s32[1]{0:T(128)} %bitcast.me_ref, bf16[2048,512]{1,0:T(8,128)(2,1)} %get-tuple-element.13.yg_ref, bf16[2048,512]{1,0:T(8,128)(2,1)} %get-tuple-element.14.fac_ref, bf16[2048,128]{1,0:T(8,128)(2,1)} %get-tuple-element.15.c_ref, bf16[136,512]{1,0:T(8,128)(2,1)} %copy-done, ...), custom_call_target="tpu_custom_call" | custom-call | tf_op jit(solution)/shard_map/correct/pallas_call | solution.py:452
  127.0 5.0 %collective-permute-done.8.refs_2_ = bf16[512,512]{1,0:T(8,128)(2,1)S(1)} collective-permute-done((bf16[512,512]{1,0:T(8,128)(2,1)}, bf16[512,512]{1,0:T(8,128)(2,1)S(1)}, u32[]{:S(2)}, u32[]{:S(2)}) %collective-permute-start.8) | collective-permute-done | bytes 524320 | tf_op jit(solution)/shard_map/ppermute | solution.py:514
  131.9 13.0 %collective-permute-done.9.refs_3_ = bf16[512,512]{1,0:T(8,128)(2,1)S(1)} collective-permute-done((bf16[512,512]{1,0:T(8,128)(2,1)}, bf16[512,512]{1,0:T(8,128)(2,1)S(1)}, u32[]{:S(2)}, u32[]{:S(2)}) %collective-permute-start.9) | collective-permute-done | bytes 524320 | tf_op jit(solution)/shard_map/ppermute | solution.py:514
  145.9 7.2 %finish.1 = bf16[512,1024]{1,0:T(8,128)(2,1)} custom-call(s32[1]{0:T(128)} %bitcast.me_ref, bf16[512,384]{1,0:T(8,128)(2,1)} %order_patches.1.refs_0_.pat_ref, bf16[384,1024]{1,0:T(8,128)(2,1)} %we_ref.1, bf16[512,512]{1,0:T(8,128)(2,1)} %get-tuple-element.17.refs_0_, bf16[512,512]{1,0:T(8,128)(2,1)} %copy-done.5, bf16[512,512]{1,0:T(8,128)(2,1)} %copy-done.3, ...), custom_call_target="tpu_custom_call" | custom-call | tf_op jit(solution)/shard_map/finish/pallas_call | solution.py:496
  (43 shorter events, 6.5 us)
Async XLA Ops:
  10.1 52.9 %copy-start.13 = (f32[8]{0:T(128)S(1)}, f32[8]{0:T(128)}, u32[]{:S(2)}) copy-start(f32[8]{0:T(128)} %param.39) | copy-start | bytes 100
  10.1 52.9 %copy-start.14 = (f32[8]{0:T(128)S(1)}, f32[8]{0:T(128)}, u32[]{:S(2)}) copy-start(f32[8]{0:T(128)} %param.38) | copy-start | bytes 100
  10.1 53.5 %copy-start.9 = (bf16[1024,8]{0,1:T(8,128)(2,1)S(1)}, bf16[1024,8]{0,1:T(8,128)(2,1)}, u32[]{:S(2)}) copy-start(bf16[1024,8]{0,1:T(8,128)(2,1)} %param.37) | copy-start | bytes 49156
  10.1 53.7 %copy-start.12 = (bf16[1024]{0:T(1024)(128)(2,1)S(1)}, bf16[1024]{0:T(1024)(128)(2,1)}, u32[]{:S(2)}) copy-start(bf16[1024]{0:T(1024)(128)(2,1)} %param.33) | copy-start | bytes 6148
  47.9 10.7 %collective-permute-start.1 = (bf16[512,384]{1,0:T(8,128)(2,1)}, bf16[512,384]{1,0:T(8,128)(2,1)S(1)}, u32[]{:S(2)}, u32[]{:S(2)}) collective-permute-start(bf16[512,384]{1,0:T(8,128)(2,1)} %order_patches.1.refs_0_.pat_ref), channel_id=1, source_target_pairs={{0,2},{1,3},{2,0},{3,1},{4,6},{5,7},{6,4},{7,5},{8,10},{9,11},{10,... | collective-permute-start | bytes 1179656 | tf_op jit(solution)/shard_map/ppermute | solution.py:514
  48.4 11.3 %collective-permute-start = (bf16[512,384]{1,0:T(8,128)(2,1)}, bf16[512,384]{1,0:T(8,128)(2,1)S(1)}, u32[]{:S(2)}, u32[]{:S(2)}) collective-permute-start(bf16[512,384]{1,0:T(8,128)(2,1)} %order_patches.1.refs_0_.pat_ref), channel_id=1, source_target_pairs={{0,1},{1,0},{2,3},{3,2},{4,5},{5,4},{6,7},{7,6},{8,9},{9,8},{10,11... | collective-permute-start | bytes 1179656 | tf_op jit(solution)/shard_map/ppermute | solution.py:514
  58.7 7.4 %copy-start.6 = (bf16[512,384]{1,0:T(8,128)(2,1)}, bf16[512,384]{1,0:T(8,128)(2,1)S(1)}, u32[]{:S(2)}) copy-start(bf16[512,384]{1,0:T(8,128)(2,1)S(1)} %collective-permute-done.1.refs_2_) | copy-start | bytes 1179652
  58.7 2.4 %collective-permute-start.2 = (bf16[512,384]{1,0:T(8,128)(2,1)S(1)}, bf16[512,384]{1,0:T(8,128)(2,1)S(1)}, u32[]{:S(2)}, u32[]{:S(2)}) collective-permute-start(bf16[512,384]{1,0:T(8,128)(2,1)S(1)} %collective-permute-done.1.refs_2_), channel_id=1, source_target_pairs={{0,1},{1,0},{2,3},{3,2},{4,5},{5,4},{6,7},{7,6},{8,9},{9,8},{10,11... | collective-permute-start | bytes 1179656 | tf_op jit(solution)/shard_map/ppermute | solution.py:514
  59.7 6.4 %copy-start.7 = (bf16[512,384]{1,0:T(8,128)(2,1)}, bf16[512,384]{1,0:T(8,128)(2,1)S(1)}, u32[]{:S(2)}) copy-start(bf16[512,384]{1,0:T(8,128)(2,1)S(1)} %collective-permute-done.refs_1_) | copy-start | bytes 1179652
  61.0 5.1 %copy-start.8 = (bf16[512,384]{1,0:T(8,128)(2,1)}, bf16[512,384]{1,0:T(8,128)(2,1)S(1)}, u32[]{:S(2)}) copy-start(bf16[512,384]{1,0:T(8,128)(2,1)S(1)} %collective-permute-done.2.refs_3_) | copy-start | bytes 1179652
  61.7 4.4 %collective-permute-start.3 = (bf16[8,384]{1,0:T(8,128)(2,1)S(1)}, bf16[8,384]{1,0:T(8,128)(2,1)S(1)}, u32[]{:S(2)}, u32[]{:S(2)}) collective-permute-start(bf16[8,384]{1,0:T(8,128)(2,1)S(1)} %fusion.1), channel_id=1, source_target_pairs={{0,4},{4,8},{8,12},{1,5},{5,9},{9,13},{2,6},{6,10},{10,14},{3,7},{... | collective-permute-start | bytes 18440 | tf_op jit(solution)/shard_map/ppermute | solution.py:519
  99.3 6.0 %collective-permute-start.4 = (bf16[136,512]{1,0:T(8,128)(2,1)}, bf16[136,512]{1,0:T(8,128)(2,1)S(1)}, u32[]{:S(2)}, u32[]{:S(2)}) collective-permute-start(bf16[136,512]{1,0:T(8,128)(2,1)} %get-tuple-element.16), channel_id=1, source_target_pairs={{0,4},{4,8},{8,12},{1,5},{5,9},{9,13},{2,6},{6,10},{10,14},{3,7},{... | collective-permute-start | bytes 417800 | tf_op jit(solution)/shard_map/ppermute | solution.py:519
  100.6 15.2 %collective-permute-start.5 = (bf16[136,512]{1,0:T(8,128)(2,1)}, bf16[136,512]{1,0:T(8,128)(2,1)S(1)}, u32[]{:S(2)}, u32[]{:S(2)}) collective-permute-start(bf16[136,512]{1,0:T(8,128)(2,1)} %get-tuple-element.16), channel_id=1, source_target_pairs={{0,8},{4,12},{1,9},{5,13},{2,10},{6,14},{3,11},{7,15},{16,24},{20,... | collective-permute-start | bytes 417800 | tf_op jit(solution)/shard_map/ppermute | solution.py:519
  101.9 13.9 %collective-permute-start.6 = (bf16[136,512]{1,0:T(8,128)(2,1)}, bf16[136,512]{1,0:T(8,128)(2,1)S(1)}, u32[]{:S(2)}, u32[]{:S(2)}) collective-permute-start(bf16[136,512]{1,0:T(8,128)(2,1)} %get-tuple-element.16), channel_id=1, source_target_pairs={{0,12},{1,13},{2,14},{3,15},{16,28},{17,29},{18,30},{19,31}} | collective-permute-start | bytes 417800 | tf_op jit(solution)/shard_map/ppermute | solution.py:519
  105.3 10.5 %copy-start = (bf16[136,512]{1,0:T(8,128)(2,1)}, bf16[136,512]{1,0:T(8,128)(2,1)S(1)}, u32[]{:S(2)}) copy-start(bf16[136,512]{1,0:T(8,128)(2,1)S(1)} %collective-permute-done.4.refs_0_) | copy-start | bytes 417796
  115.8 0.7 copy-start.1
  115.8 0.7 copy-start.2
  119.8 12.1 %collective-permute-start.8 = (bf16[512,512]{1,0:T(8,128)(2,1)}, bf16[512,512]{1,0:T(8,128)(2,1)S(1)}, u32[]{:S(2)}, u32[]{:S(2)}) collective-permute-start(bf16[512,512]{1,0:T(8,128)(2,1)} %get-tuple-element.19), channel_id=1, source_target_pairs={{0,2},{1,3},{2,0},{3,1},{4,6},{5,7},{6,4},{7,5},{8,10},{9,11},{10,... | collective-permute-start | bytes 1572872 | tf_op jit(solution)/shard_map/ppermute | solution.py:514
  119.8 6.5 %copy-start.11 = (bf16[2048]{0:T(1024)(128)(2,1)S(1)}, bf16[2048]{0:T(1024)(128)(2,1)}, u32[]{:S(2)}) copy-start(bf16[2048]{0:T(1024)(128)(2,1)} %param.42) | copy-start | bytes 12292
  119.8 25.1 %collective-permute-start.9 = (bf16[512,512]{1,0:T(8,128)(2,1)}, bf16[512,512]{1,0:T(8,128)(2,1)S(1)}, u32[]{:S(2)}, u32[]{:S(2)}) collective-permute-start(bf16[512,512]{1,0:T(8,128)(2,1)} %get-tuple-element.20), channel_id=1, source_target_pairs={{0,3},{1,2},{2,1},{3,0},{4,7},{5,6},{6,5},{7,4},{8,11},{9,10},{10,... | collective-permute-start | bytes 1572872 | tf_op jit(solution)/shard_map/ppermute | solution.py:514
  126.4 18.6 %collective-permute-start.7 = (bf16[512,512]{1,0:T(8,128)(2,1)}, bf16[512,512]{1,0:T(8,128)(2,1)S(1)}, u32[]{:S(2)}, u32[]{:S(2)}) collective-permute-start(bf16[512,512]{1,0:T(8,128)(2,1)} %get-tuple-element.18), channel_id=1, source_target_pairs={{0,1},{1,0},{2,3},{3,2},{4,5},{5,4},{6,7},{7,6},{8,9},{9,8},{10,11... | collective-permute-start | bytes 1572872 | tf_op jit(solution)/shard_map/ppermute | solution.py:514
  131.9 13.0 %copy-start.3 = (bf16[512,512]{1,0:T(8,128)(2,1)}, bf16[512,512]{1,0:T(8,128)(2,1)S(1)}, u32[]{:S(2)}) copy-start(bf16[512,512]{1,0:T(8,128)(2,1)S(1)} %collective-permute-done.8.refs_2_) | copy-start | bytes 1572868
  144.9 0.8 copy-start.4
  144.9 1.0 copy-start.5
  (1 other events, 0.6 us)

commit v2 on v1

v2 whole, which is shorter than its diff:
```python
import functools
import math

import jax
import jax.numpy as jnp
import ml_dtypes
import numpy as np
from jax import lax
from jax.experimental import pallas as pl
from jax.experimental.pallas import tpu as pltpu
from jax.sharding import PartitionSpec as P

SPAN = 256
EPSILON = 1e-05
LANES = 128
PATCH = 64
ALL = ("seq", "head", "rep")
HR = ("head", "rep")
F32 = jnp.float32
BF16 = jnp.bfloat16
VMEM = pl.BlockSpec(memory_space=pltpu.VMEM)
SMEM = pl.BlockSpec(memory_space=pltpu.SMEM)


def cost(micros):
    return pl.CostEstimate(
        flops=int(micros * 1e9), transcendentals=0, bytes_accessed=int(micros * 3e6)
    )


PARAMS = pltpu.CompilerParams(vmem_limit_bytes=56 * 1024 * 1024)


def two_halves(table):
    high = table.astype(ml_dtypes.bfloat16)
    return high, (table - high.astype(np.float64)).astype(ml_dtypes.bfloat16)


def mm(a, b):
    return jnp.dot(a, b, preferred_element_type=F32)


def split(a):
    high = a.astype(BF16)
    return high, (a - high.astype(F32)).astype(BF16)


def lane_bins(inner):
    parts = PATCH // inner
    lane = np.arange(LANES)
    width = LANES // parts
    return lane // width + parts * (lane % width)


def inverse_fft(real, imag):
    count = len(real)
    if count == 1:
        return real, imag
    even_r, even_i = inverse_fft(real[0::2], imag[0::2])
    odd_r, odd_i = inverse_fft(real[1::2], imag[1::2])
    half = count // 2
    out_r, out_i = [None] * count, [None] * count
    for k in range(half):
        angle = 2.0 * math.pi * k / count
        c, s = math.cos(angle), math.sin(angle)
        if k == 0:
            r, i = odd_r[k], odd_i[k]
        elif 4 * k == count:
            r, i = -odd_i[k], odd_r[k]
        else:
            r = odd_r[k] * c - odd_i[k] * s
            i = odd_r[k] * s + odd_i[k] * c
        out_r[k], out_i[k] = even_r[k] + r, even_i[k] + i
        out_r[k + half], out_i[k + half] = even_r[k] - r, even_i[k] - i
    return out_r, out_i


def first_section(
    rows_all, length, pos, amp, phase, mode, delay, bins, turn_ref, x_ref, twist_ref, high_ref, low_ref,
    out_ref, base, acc, lhs,
):
    channels = x_ref.shape[1]
    sources = phase.shape[0]
    inner = x_ref.shape[2]
    row_block = x_ref.shape[3]
    shape = (row_block, LANES)
    row = pos[0] * row_block + lax.broadcasted_iota(jnp.int32, shape, 0)
    lane = lax.broadcasted_iota(jnp.int32, shape, 1)
    first_bin = row + rows_all * lane
    unit = 2.0 * math.pi / length

    def make_base(s, _):
        turn = ((((first_bin * delay[s]) & (length - 1)) * mode[s]) & (length - 1)).astype(F32)
        angle = mode[s].astype(F32) * phase[s] + turn * unit
        base[0, s] = jnp.cos(angle)
        base[1, s] = jnp.sin(angle)
        return 0

    lax.fori_loop(0, sources, make_base, 0)

    def add_sources(v, _):
        here = first_bin + (rows_all * LANES) * v
        total = [x_ref[r, c, v] for r in range(2) for c in range(channels)]
        for s in range(sources):
            which = (delay[s] * mode[s] * v) & (inner - 1)
            tr, ti = turn_ref[0, which], turn_ref[1, which]
            inside = (here >= bins[0, s]) & (here < bins[1, s])
            br, bi = base[0, s], base[1, s]
            real = jnp.where(inside, br * tr - bi * ti, 0.0)
            imag = jnp.where(inside, br * ti + bi * tr, 0.0)
            for c in range(channels):
                total[c] = total[c] + amp[c, s] * real
                total[channels + c] = total[channels + c] + amp[c, s] * imag
        for n in range(2 * channels):
            acc[n, v] = total[n]
        return 0

    lax.fori_loop(0, inner, add_sources, 0)

    def transform(c, _):
        real, imag = inverse_fft(
            [acc[c, v] for v in range(inner)], [acc[channels + c, v] for v in range(inner)]
        )
        for q in range(inner):
            tc, ts = twist_ref[0, q : q + 1, :], twist_ref[1, q : q + 1, :]
            lhs[c, q, :, 0:LANES] = real[q] * tc - imag[q] * ts
            lhs[c, q, :, LANES : 2 * LANES] = real[q] * ts + imag[q] * tc
        return 0

    lax.fori_loop(0, channels, transform, 0)

    wide = (inner, row_block, LANES)
    parts = PATCH // inner
    width = LANES // parts
    lanes = lax.broadcasted_iota(jnp.int32, wide, 2)
    outer = lax.div(lanes, width) + parts * lax.rem(lanes, width)
    column = lax.broadcasted_iota(jnp.int32, wide, 0) + inner * outer
    rows = pos[0] * row_block + lax.broadcasted_iota(jnp.int32, wide, 1)
    angle = ((rows * column) & (length - 1)).astype(F32) * unit
    cos, sin = jnp.cos(angle), jnp.sin(angle)
    for c in range(channels):
        high, low = split(lhs[c].reshape(inner * row_block, 2 * LANES))
        got = mm(high, high_ref[...]) + mm(low, high_ref[...]) + mm(high, low_ref[...])
        real = got[:, 0:LANES].reshape(wide)
        imag = got[:, LANES : 2 * LANES].reshape(wide)
        out_ref[:, c] = (real * cos - imag * sin).astype(BF16)
        out_ref[:, channels + c] = (real * sin + imag * cos).astype(BF16)


def run_first(spectrum, amp, phase, mode, delay, bins, pos, rows_all, length):
    _, channels, row_block, columns = spectrum.shape
    inner = columns // LANES
    grid_in = spectrum.reshape(2, channels, row_block, inner, LANES).transpose(0, 1, 3, 2, 4)
    steps = np.arange(inner)
    turn = 2.0 * np.pi * steps / inner
    turns = np.stack([np.cos(turn), np.sin(turn)]).astype(np.float32)
    lane = np.arange(LANES)
    twist = 2.0 * np.pi * (steps[:, None] * lane[None, :] % columns) / columns
    twists = np.stack([np.cos(twist), np.sin(twist)]).astype(np.float32)
    angle = 2.0 * np.pi * (lane[:, None] * lane_bins(inner)[None, :] % LANES) / LANES
    cos, sin = np.cos(angle), np.sin(angle)
    high, low = two_halves(np.block([[cos, sin], [-sin, cos]]))
    return pl.pallas_call(
        functools.partial(first_section, rows_all, length),
        out_shape=jax.ShapeDtypeStruct((inner, 2 * channels, row_block, LANES), BF16),
        in_specs=[SMEM] * 7 + [VMEM] * 4,
        out_specs=VMEM,
        scratch_shapes=[
            pltpu.VMEM((2, amp.shape[0], row_block, LANES), F32),
            pltpu.VMEM((2 * channels, inner, row_block, LANES), F32),
            pltpu.VMEM((channels, inner, row_block, 2 * LANES), F32),
        ],
        compiler_params=PARAMS,
        cost_estimate=cost(7),
        name="first_section",
    )(pos, amp.T, phase, mode, delay, bins.T, turns, grid_in, twists, high, low)


def second_section(reps, z_ref, high_ref, low_ref, out_ref):
    devices, own, pairs, row_block, _ = z_ref.shape
    channels = pairs // 2
    rows = devices * row_block
    tiles = own * pairs
    half = (tiles + 1) // 2
    lane = lax.broadcasted_iota(jnp.int32, (rows, LANES), 1)
    sub = lax.rem(lax.broadcasted_iota(jnp.int32, (rows, LANES), 0), row_block)
    upper = (lane & 32) != 0
    rim = jnp.zeros((rows, LANES), F32)
    for q in range(own):
        for c in range(channels):
            right = jnp.concatenate(
                [z_ref[:, q, r * channels + c].astype(F32).reshape(rows, LANES) for r in range(2)], axis=0
            ).astype(BF16)
            got = mm(high_ref[...], right) + mm(low_ref[...], right)
            for r in range(2):
                tile = q * pairs + r * channels + c
                part = got[r * rows : (r + 1) * rows]
                out_ref[:, tile] = part.reshape(devices, row_block, LANES).astype(BF16)
                ends = jnp.broadcast_to(
                    part.reshape(devices, row_block, LANES)[:, row_block - 1 :, :],
                    (devices, row_block, LANES),
                ).reshape(rows, LANES)
                if tile < half:
                    rim = jnp.where(upper & (sub == tile), ends, rim)
                else:
                    ends = pltpu.roll(ends, LANES - 32, 1)
                    rim = jnp.where(jnp.logical_not(upper) & (sub == tile - half), ends, rim)
    rim = rim.reshape(devices, row_block, LANES).astype(BF16)
    for d in range(devices):
        source = d - d % reps - 1
        out_ref[d, tiles] = rim[source] if source >= 0 else jnp.zeros((row_block, LANES), BF16)


def run_second(z, length):
    devices, own, pairs, row_block, _ = z.shape
    rows = devices * row_block
    counter = np.arange(rows)
    angle = 2.0 * np.pi * (counter[:, None] * counter[None, :] % rows) / rows
    cos, sin = np.cos(angle), np.sin(angle)
    high, low = two_halves(np.block([[cos, -sin], [sin, cos]]) / math.sqrt(length))
    return pl.pallas_call(
        functools.partial(second_section, lax.axis_size("rep")),
        out_shape=jax.ShapeDtypeStruct((devices, own * pairs + 1, row_block, LANES), BF16),
        in_specs=[VMEM] * 3,
        out_specs=VMEM,
        compiler_params=PARAMS,
        cost_estimate=cost(3),
        name="second_section",
    )(z, high, low)


def order_patches(x_ref, perm_ref, rim_ref, out_ref, wide):
    devices, tiles, row_block, _ = x_ref.shape
    parts = perm_ref.shape[0]
    width = LANES // parts
    half = tiles // 2
    wide[...] = x_ref[...].astype(F32).reshape(devices * tiles * row_block, LANES)
    for m in range(row_block):
        rows = wide[pl.ds(m, devices * tiles, stride=row_block), :]
        across = rows.T.astype(BF16)
        total = mm(across[0:width], perm_ref[0])
        for n in range(1, parts):
            total = total + mm(across[n * width : (n + 1) * width], perm_ref[n])
        out_ref[m * width : (m + 1) * width, :] = total.astype(BF16)
    rows = jnp.concatenate(
        [wide[pl.ds((tiles - 1) * row_block + n, devices, stride=tiles * row_block), :] for n in range(half)],
        axis=0,
    )
    across = jnp.concatenate([rows, pltpu.roll(rows, 32, 1)], axis=0).T.astype(BF16)
    total = mm(across[width - 8 : width], rim_ref[0])
    for n in range(1, parts):
        total = total + mm(across[(n + 1) * width - 8 : (n + 1) * width], rim_ref[n])
    out_ref[row_block * width :, :] = total.astype(BF16)


def run_order(x, inner, channels):
    devices, tiles, row_block, _ = x.shape
    parts = PATCH // inner
    own = tiles - 1
    pairs = 2 * channels
    each = own // pairs
    perm = np.zeros((parts, devices * tiles, pairs * PATCH), ml_dtypes.bfloat16)
    rim = np.zeros((parts, own * devices, pairs * PATCH), ml_dtypes.bfloat16)
    for n in range(parts):
        for j in range(devices):
            for q in range(each):
                for rc in range(pairs):
                    to = rc * PATCH + n * inner + j * each + q
                    perm[n, j * tiles + q * pairs + rc, to] = 1
                    rim[n, (q * pairs + rc) * devices + j, to] = 1
    return pl.pallas_call(
        order_patches,
        out_shape=jax.ShapeDtypeStruct((row_block * LANES // parts + 8, pairs * PATCH), BF16),
        in_specs=[VMEM] * 3,
        out_specs=VMEM,
        scratch_shapes=[pltpu.VMEM((devices * tiles * row_block, LANES), F32)],
        compiler_params=PARAMS,
        cost_estimate=cost(3),
        name="order_patches",
    )(x, perm, rim)


def dft_table(order):
    counter = jnp.arange(order, dtype=jnp.int32)
    turn_count = counter[:, None] * counter[None, :] % order
    radians = turn_count.astype(F32) * (2.0 * math.pi / order)
    return jnp.stack([jnp.cos(radians), jnp.sin(radians)])


def make_patches(first, length):
    devices = lax.axis_size(ALL)
    inner, pairs, row_block, _ = first.shape
    channels = pairs // 2
    if inner % devices == 0 and 2 * inner == PATCH and inner // devices * pairs in range(2, 17, 2):
        own = inner // devices
        moved = lax.all_to_all(
            first.reshape(devices, own, pairs, row_block, LANES), ALL, 0, 0, tiled=True
        )
        moved = lax.all_to_all(run_second(moved, length), ALL, 0, 0, tiled=True)
        return run_order(moved, inner, channels)
    flat = first.transpose(1, 2, 0, 3).reshape(2, channels, row_block, inner * LANES)
    flat = lax.all_to_all(flat, ALL, split_axis=3, concat_axis=2, tiled=True).astype(F32)
    mixed = jnp.einsum(
        "rcuq,kum->krcqm", flat, dft_table(row_block * devices), precision=lax.Precision.HIGHEST
    )
    series = jnp.stack([mixed[0, 0] - mixed[1, 1], mixed[1, 0] + mixed[0, 1]])
    series = (series * (1.0 / math.sqrt(length))).astype(BF16)
    series = lax.all_to_all(series, ALL, split_axis=4 - 1, concat_axis=2, tiled=True)
    parts = PATCH // inner
    series = series.reshape(2, channels, inner, parts, LANES // parts, row_block)
    patches = series.transpose(5, 4, 0, 1, 3, 2).reshape(
        row_block * LANES // parts, 2 * channels * PATCH
    )
    reps = lax.axis_size("rep")
    tail = patches[patches.shape[0] - 8 :]
    rim = jnp.zeros_like(tail)
    for r in range(reps):
        pairs = [(i - 1, i + r) for i in range(reps, devices, reps)]
        rim = rim + lax.ppermute(tail, ALL, pairs)
    return jnp.concatenate([patches, rim], 0)


def norm_rows(values, total):
    return lax.rsqrt(jnp.sum(values * values, axis=-1, keepdims=True) * (1.0 / total) + EPSILON)


def silu(values):
    return values * (1.0 / (1.0 + jnp.exp(-values)))


def fold(ends, count, head, entering, upto=None):
    state = entering.shape[0]
    for i in range(count):
        part, decay = ends[0][0:state], ends[0][state : state + 1]
        for j in range(1, len(ends)):
            here = (head ^ i) == j
            part = jnp.where(here, ends[j][0:state], part)
            decay = jnp.where(here, ends[j][state : state + 1], decay)
        after = decay * entering + part
        entering = after if upto is None else jnp.where(i < upto, after, entering)
    return entering


def expand(values, spread):
    high, low = split(values)
    return mm(jnp.concatenate([high, low], axis=1), spread[...])


def block_states(heads, per, before, final, me_ref, *refs):
    pats, refs = refs[:2], refs[2:]
    halo, we, nin, wx, wbc, wdt, dtb, alog, cx, cbc, spread = refs[:11]
    earlier, refs = refs[11 : 11 + before], refs[11 + before :]
    normed_ref, x_ref, b_ref, c_ref, cum_ref, step_ref, local_ref, grown_ref, st_ref = refs[:9]
    xs, bcs, carried, total, low_tri, dts, rows = refs[-7:]
    block = pl.program_id(0)
    state = wbc.shape[1] // 2
    taps = cx.shape[0]

    def features(p):
        embedded = mm(p, we[...]).astype(BF16).astype(F32)
        scale = norm_rows(embedded, embedded.shape[-1])
        return (embedded * scale * nin[...].astype(F32)).astype(BF16)

    @pl.when(block == 0)
    def _():
        carried[...] = jnp.zeros_like(carried)
        total[...] = jnp.zeros_like(total)
        past = features(halo[...])
        xs[0:8] = mm(past, wx[...]).astype(BF16).astype(F32)
        bcs[0:8] = mm(past, wbc[...]).astype(BF16).astype(F32)
        ri = lax.broadcasted_iota(jnp.int32, (SPAN, SPAN), 0)
        ci = lax.broadcasted_iota(jnp.int32, (SPAN, SPAN), 1)
        low_tri[...] = jnp.where(ri >= ci, 1.0, 0.0).astype(BF16)
        dts[...] = jnp.zeros_like(dts)
        rows[...] = jnp.zeros_like(rows)
        rows[0:1, 0:heads] = dtb[...]
        rows[1:2, 0:heads] = -jnp.exp(alog[...])

    @pl.when(block > 0)
    def _():
        xs[0:8] = xs[SPAN : SPAN + 8]
        bcs[0:8] = bcs[SPAN : SPAN + 8]

    here = ((block // per) ^ me_ref[1]) == 0
    normed = features(jnp.where(here, pats[0][...], pats[1][...]))
    normed_ref[...] = normed
    dts[:, 0:heads] = lax.dot_general(
        normed, wdt[...], (((1,), (1,)), ((), ())), preferred_element_type=F32
    )
    bcs[8 : SPAN + 8] = mm(normed, wbc[...]).astype(BF16).astype(F32)
    xs[8 : SPAN + 8] = mm(normed, wx[...]).astype(BF16).astype(F32)
    step = dts[...] + rows[0:1]
    step = jnp.maximum(step, 0.0) + jnp.log1p(jnp.exp(-jnp.abs(step)))
    step_ref[...] = step
    rated = step * rows[1:2]
    one = rated.astype(BF16).astype(F32)
    two = (rated - one).astype(BF16).astype(F32)
    three = rated - one - two
    packed = one + pltpu.roll(two, heads, 1) + pltpu.roll(three, 2 * heads, 1)
    sums = mm(low_tri[...], packed.astype(BF16))
    cum = sums + pltpu.roll(sums, LANES - heads, 1) + pltpu.roll(sums, LANES - 2 * heads, 1)
    cum_ref[...] = cum
    last = cum[SPAN - 1 : SPAN]
    weights = expand(jnp.exp(last - cum) * step, spread)
    grow = expand(
        jnp.exp(jnp.concatenate([jnp.broadcast_to(last, (8, LANES)), total[...]], axis=0)), spread
    )

    def conv(buffer, kernel):
        out = kernel[0:1] * buffer[9 - taps : 9 - taps + SPAN]
        for i in range(1, taps):
            out = out + kernel[i : i + 1] * buffer[9 - taps + i : 9 - taps + i + SPAN]
        return silu(out)

    bc = conv(bcs, cbc)
    b_ref[...] = bc[:, :state].astype(BF16)
    c_ref[...] = bc[:, state:].astype(BF16)
    bt = bc[:, :state].T.astype(BF16)
    xc = conv(xs, cx).astype(BF16)
    x_ref[...] = xc
    weighted = (xc.astype(F32) * weights).astype(BF16)
    local_ref[0] = carried[...]
    grown_ref[0] = grow[8:16]
    carried[...] = carried[...] * grow[0:1] + mm(bt, weighted)
    total[...] = total[...] + last

    @pl.when(block == pl.num_programs(0) - 1)
    def _():
        st_ref[0:state] = carried[...]
        st_ref[state : state + 8] = grow[8:16] * grow[0:8]
        if final:
            everything = [e[...] for e in earlier] + [st_ref[...]]
            count = len(everything)
            send = refs[9]
            send[0:state] = fold(everything, count, me_ref[0], jnp.zeros((state, xc.shape[1]), F32)).astype(BF16)
            decay = everything[0][state : state + 8]
            for e in everything[1:]:
                decay = decay * e[state : state + 8]
            send[state : state + 8] = decay.astype(BF16)


def run_states(me, pats, halo, consts, heads, inner, state, own, earlier, final):
    rows_in, width = pats[0].shape
    model = consts[0].shape[1]
    tokens = own * len(pats)
    per = own // SPAN
    blocks = tokens // SPAN
    row = lambda n: pl.BlockSpec((SPAN, n), lambda b, me: (b, 0))
    fixed = pl.BlockSpec((state + 8, inner), lambda b, me: (0, 0))
    shape = lambda *d, t=F32: jax.ShapeDtypeStruct(d, t)
    return pl.pallas_call(
        functools.partial(block_states, heads, per, len(earlier), final),
        grid_spec=pltpu.PrefetchScalarGridSpec(
            num_scalar_prefetch=1,
            grid=(blocks,),
            in_specs=[pl.BlockSpec((SPAN, width), lambda b, me: (b % per, 0))] * len(pats)
            + [pl.BlockSpec((8, width), lambda b, me: (own // 8, 0))]
            + [VMEM] * (len(consts) + len(earlier)),
            out_specs=[row(model), row(inner), row(state), row(state), row(LANES), row(LANES),
                       pl.BlockSpec((1, state, inner), lambda b, me: (b, 0, 0)),
                       pl.BlockSpec((1, 8, inner), lambda b, me: (b, 0, 0)), fixed]
            + [fixed] * final,
            scratch_shapes=[
                pltpu.VMEM((SPAN + 8, inner), F32),
                pltpu.VMEM((SPAN + 8, 2 * state), F32),
                pltpu.VMEM((state, inner), F32),
                pltpu.VMEM((8, LANES), F32),
                pltpu.VMEM((SPAN, SPAN), BF16),
                pltpu.VMEM((SPAN, LANES), F32),
                pltpu.VMEM((8, LANES), F32),
            ],
        ),
        out_shape=[
            shape(tokens, model, t=BF16), shape(tokens, inner, t=BF16), shape(tokens, state, t=BF16),
            shape(tokens, state, t=BF16), shape(tokens, LANES), shape(tokens, LANES),
            shape(blocks, state, inner), shape(blocks, 8, inner), shape(state + 8, inner),
        ] + [shape(state + 8, inner, t=BF16)] * final,
        compiler_params=PARAMS,
        cost_estimate=cost(13),
        name="block_states",
    )(me, *pats, halo, *consts, *earlier)


def local_part(heads, normed_ref, x_ref, b_ref, c_ref, cum_ref, step_ref, wz, spread, yg_ref, fac_ref, y_acc):
    gate = silu(mm(normed_ref[...], wz[...]).astype(BF16).astype(F32))
    cum = cum_ref[...]
    cum_t = cum.T
    step_t = step_ref[...].T
    gram = lax.dot_general(
        c_ref[...], b_ref[...], (((1,), (1,)), ((), ())), preferred_element_type=F32
    )
    ri = lax.broadcasted_iota(jnp.int32, (SPAN, SPAN), 0)
    ci = lax.broadcasted_iota(jnp.int32, (SPAN, SPAN), 1)
    inside = ri >= ci
    head_dim = x_ref.shape[1] // heads
    for h in range(heads):
        gap = cum[:, h : h + 1] - cum_t[h : h + 1, :]
        seg = jnp.exp(jnp.where(inside, gap, -jnp.inf))
        scores = (gram * seg * step_t[h : h + 1, :]).astype(BF16)
        cols = slice(h * head_dim, (h + 1) * head_dim)
        y_acc[:, cols] = mm(scores, x_ref[:, cols])
    fac_ref[...] = (expand(jnp.exp(cum), spread) * gate).astype(BF16)
    yg_ref[...] = (y_acc[...] * gate).astype(BF16)


def run_local(micros, heads, normed, xc, bm, cm, cum, step, wz, spread):
    tokens, inner = xc.shape
    row = lambda n: pl.BlockSpec((SPAN, n), lambda b: (b, 0))
    return pl.pallas_call(
        functools.partial(local_part, heads),
        grid=(tokens // SPAN,),
        in_specs=[row(a.shape[1]) for a in (normed, xc, bm, cm, cum, step)] + [VMEM] * 2,
        out_specs=[row(inner)] * 2,
        scratch_shapes=[pltpu.VMEM((SPAN, inner), F32)],
        out_shape=[jax.ShapeDtypeStruct((tokens, inner), BF16)] * 2,
        compiler_params=PARAMS,
        cost_estimate=cost(micros),
        name="local_part",
    )(normed, xc, bm, cm, cum, step, wz, spread)


def correct(chip, chips, reps, me_ref, yg_ref, fac_ref, c_ref, local_ref, grown_ref, *refs):
    ends, earlier = refs[:chips], refs[chips : -reps - 1]
    outs, start = refs[-reps - 1 : -1], refs[-1]
    state = c_ref.shape[1]
    block = pl.program_id(0)
    per = pl.num_programs(0) // reps

    @pl.when(block == 0)
    def _():
        entering = jnp.zeros((state, yg_ref.shape[1]), F32)
        for part in reversed(earlier):
            entering = part[0:state].astype(F32) + part[state : state + 1].astype(F32) * entering
        start[...] = fold([e[...] for e in ends], chips - 1, me_ref[0], entering, me_ref[0] ^ chip)

    cm = c_ref[...]
    high, low = split(local_ref[0] + grown_ref[0, 0:1] * start[...])
    added = mm(jnp.concatenate([cm, cm], axis=1), jnp.concatenate([high, low], axis=0))
    value = (yg_ref[...].astype(F32) + fac_ref[...].astype(F32) * added).astype(BF16)
    for r in range(reps):
        @pl.when((block // per) == (me_ref[1] ^ r))
        def _(r=r):
            outs[r][pl.ds(pl.multiple_of((block % per) * SPAN, SPAN), SPAN), :] = value


def run_correct(chip, reps, me, yg, fac, cm, local, grown, ends, earlier, own):
    tokens, inner = yg.shape
    state = cm.shape[1]
    block = lambda b, me: (b, 0)
    block3 = lambda b, me: (b, 0, 0)
    return pl.pallas_call(
        functools.partial(correct, chip, len(ends), reps),
        grid_spec=pltpu.PrefetchScalarGridSpec(
            num_scalar_prefetch=1,
            grid=(tokens // SPAN,),
            in_specs=[pl.BlockSpec((SPAN, inner), block)] * 2 + [pl.BlockSpec((SPAN, state), block),
                      pl.BlockSpec((1, state, inner), block3), pl.BlockSpec((1, 8, inner), block3)]
            + [VMEM] * (len(earlier) + len(ends)),
            out_specs=[pl.BlockSpec((own, inner), lambda b, me: (0, 0))] * reps,
            scratch_shapes=[pltpu.VMEM((state, inner), F32)],
        ),
        out_shape=[jax.ShapeDtypeStruct((own, inner), BF16)] * reps,
        compiler_params=PARAMS,
        cost_estimate=cost(5 if chip else 0.05),
        name="correct",
    )(me, yg, fac, cm, local, grown, *ends, *earlier)


def finish(count, me_ref, pat_ref, we_ref, *refs):
    parts, norms, weights, out_ref = refs[:count], refs[count : 2 * count], refs[2 * count : -1], refs[-1]
    values = [p[...].astype(F32) for p in parts]
    square = values[0] * values[0]
    for v in values[1:]:
        square = square + v * v
    inner = values[0].shape[1]
    scale = lax.rsqrt(
        jnp.sum(square, axis=-1, keepdims=True) * (1.0 / (count * inner)) + EPSILON
    )
    out = mm(pat_ref[...], we_ref[...]).astype(BF16).astype(F32)
    mixed = None
    for v, n, w in zip(values, norms, weights):
        part = mm((v * scale * n[...].astype(F32)).astype(BF16), w[0])
        mixed = part if mixed is None else mixed + part
    out_ref[...] = (out + mixed).astype(BF16)


def run_finish(me, patches, we, parts, norm_out, w_out):
    count = len(parts)
    own, inner = parts[0].shape
    width = w_out.shape[1]
    tile = min(own, SPAN)
    norms = norm_out[None]
    weights = w_out.reshape(count, inner, width)
    picks = [
        pl.BlockSpec((1, inner), lambda i, me, d=d: (0, me[0] ^ d)) for d in range(count)
    ] + [
        pl.BlockSpec((1, inner, width), lambda i, me, d=d: (me[0] ^ d, 0, 0)) for d in range(count)
    ]
    return pl.pallas_call(
        functools.partial(finish, count),
        grid_spec=pltpu.PrefetchScalarGridSpec(
            num_scalar_prefetch=1,
            grid=(own // tile,),
            in_specs=[pl.BlockSpec((tile, patches.shape[1]), lambda i, me: (i, 0)), VMEM]
            + [pl.BlockSpec((tile, inner), lambda i, me: (i, 0))] * count
            + picks,
            out_specs=pl.BlockSpec((tile, width), lambda i, me: (i, 0)),
        ),
        out_shape=jax.ShapeDtypeStruct((own, width), BF16),
        compiler_params=PARAMS,
        cost_estimate=cost(7),
        name="finish",
    )(me, patches, we, *parts, *([norms] * count), *([weights] * count))


def swap(value, flip):
    count = lax.axis_size(HR)
    return lax.ppermute(value, HR, [(i, i ^ flip) for i in range(count)])


def shift(value, by):
    count = lax.axis_size("seq")
    return lax.ppermute(value, "seq", [(i, i + by) for i in range(count - by)])


def on_device(
    spectrum, src_amp, src_phase, src_mode, src_delay, src_bins, w_embed, norm_in, w_z, w_x, w_bc, w_dt,
    dt_bias, a_log, conv_x, conv_bc, norm_out, w_out,
):
    devices = lax.axis_size(ALL)
    share = lax.axis_size(HR)
    rows_all = spectrum.shape[2] * devices
    length = rows_all * spectrum.shape[3]
    pos = lax.axis_index(ALL).astype(jnp.int32).reshape(1)
    me = lax.axis_index(HR).astype(jnp.int32).reshape(1)
    first = run_first(
        spectrum, src_amp, src_phase, src_mode, src_delay, src_bins, pos, rows_all, length
    )
    patches = make_patches(first, length)
    own = patches.shape[0] - 8
    reps, chips = lax.axis_size("rep"), lax.axis_size("head")
    place = jnp.stack([lax.axis_index("head"), lax.axis_index("rep")]).astype(jnp.int32)
    heads, inner, state = dt_bias.shape[0], w_x.shape[1], w_bc.shape[1] // 2
    spread = np.zeros((2 * LANES, inner), ml_dtypes.bfloat16)
    for h in range(heads):
        spread[h, h * (inner // heads) : (h + 1) * (inner // heads)] = 1
    spread[LANES:] = spread[:LANES]
    consts = (
        w_embed, norm_in[None], w_x, w_bc, w_dt.T, dt_bias[None], a_log[None], conv_x, conv_bc,
        jnp.asarray(spread),
    )
    done, ends = [], []
    base = [patches] + [swap(patches, c * reps) for c in range(1, chips)]
    for c in range(chips):
        start = base[c]
        if ends:
            start, ends[-1] = lax.optimization_barrier((start, ends[-1]))
        group = [start] + [swap(start, r) for r in range(1, reps)]
        got = run_states(
            place, group, start, consts, heads, inner, state, own, ends, c == chips - 1
        )
        done.append(got[:8])
        ends.append(got[8])
    send = got[9]
    earlier = [shift(send, d) for d in range(1, lax.axis_size("seq"))]
    parts = [None] * share
    gate = None
    for c in list(range(1, chips)) + [0]:
        normed, xc, bm, cm, cum, step, local, grown = done[c]
        if gate is not None:
            normed, gate = lax.optimization_barrier((normed, gate))
        yg, fac = run_local(7 if c else 0.05, heads, normed, xc, bm, cm, cum, step, w_z, spread)
        values = run_correct(c, reps, place, yg, fac, cm, local, grown, ends, earlier, own)
        gate = values[0]
        for r in reversed(range(reps)):
            d = c * reps + r
            parts[d] = swap(values[r], d) if d else values[r]
    return run_finish(me, patches, w_embed, parts, norm_out, w_out)


def solution(mesh):
    in_specs = (
        P("grp", None, ("seq", "head", "rep"), None),
        P("grp", None),
        P("grp"),
        P("grp"),
        P("grp"),
        P("grp", None),
        P(),
        P(),
        P(None, ("head", "rep")),
        P(None, ("head", "rep")),
        P(),
        P(None, ("head", "rep")),
        P(("head", "rep")),
        P(("head", "rep")),
        P(None, ("head", "rep")),
        P(),
        P(),
        P(),
    )
    out_specs = P(("grp", "seq", "head", "rep"), None)
    return jax.shard_map(
        on_device, mesh=mesh, in_specs=in_specs, out_specs=out_specs, check_vma=False
    )
```

time: 154 us -> 141 us (0.916)
  the two profiles are of different devices: /device:TPU:27 before, /device:TPU:25 now
where the time goes in v2:
time: 141 us
  Pallas kernels  74.1 us (53%)
  blocking collectives  33.4 us (24%)
  waiting for transfers between devices  19.1 us (14%)
  starting transfers between devices  8.92 us (6%)
  local copies, waits for them, and re-layouts  4.23 us (3%)
    pallas_call x2, Pallas kernels, run_states(): pl.pallas_call(functools.partial(block_states, heads, per, len(earlier),...  28.9 us
    all_to_all x1, blocking collectives, make_patches(): moved = lax.all_to_all(run_second(moved, length), ALL, 0, 0, tiled=True)  17 us
    all_to_all x1, blocking collectives, make_patches(): lax.all_to_all(first.reshape(devices, own, pairs, row_block, LANES), ALL,...  16.4 us
    pallas_call x2, Pallas kernels, run_local(): pl.pallas_call(functools.partial(local_part, heads), grid=(tokens // SPAN...  14.3 us
    ppermute x6, waiting for transfers between devices, swap(): return lax.ppermute(value, HR, [(i, i ^ flip) for i in range(count)])  14 us
    pallas_call x2, Pallas kernels, run_correct(): pl.pallas_call(functools.partial(correct, chip, len(ends), reps), grid_sp...  11.1 us
    pallas_call x1, Pallas kernels, run_first(): pl.pallas_call(functools.partial(first_section, rows_all, length), out_sh...  7.45 us
    pallas_call x1, Pallas kernels, run_finish(): pl.pallas_call(functools.partial(finish, count), grid_spec=pltpu.Prefetch...  7.03 us
  transfers between devices with their start and end apart: 9, of which 4 were waited for; matrix products, arithmetic and copies ran while one was open for 1% of the time, Pallas kernels for 24%

profile of v2, /device:TPU:25, one launch (start us, length us, event | category | flops | bytes accessed | tf_op | source)
XLA Modules:
  0.0 140.5 jit_solution(3973810836433757327)
XLA Ops:
  0.0 7.5 %first_section.1 = bf16[32,6,8,128]{3,2,1,0:T(8,128)(2,1)} custom-call(s32[1]{0:T(128)} %bitcast.1.pos, f32[3,16]{1,0:T(4,128)} %bitcast.22, f32[16]{0:T(128)} %phase.1, s32[16]{0:T(128)} %mode.1, s32[16]{0:T(128)} %delay.1, s32[2,16]{1,0:T(2,128)} %bitcast.23, f32[2,32]{1,0:T(2,128)} %constant.33.clone.turn_ref, f32[2,3,32,8,128]{4,3,2,1,0:T(8,128)} %bitcast.19, ...), custom_call_target="tpu_custom_call" | custom-call | flops 7000000000 | bytes 21000000 | tf_op jit(solution)/shard_map/first_section/pallas_call | solution.py:163
  7.5 16.4 %all_to_all.10.z_ref = bf16[16,2,6,8,128]{4,3,2,1,0:T(8,128)(2,1)} all-to-all(bf16[16,2,6,8,128]{4,3,2,1,0:T(8,128)(2,1)} %bitcast.14), channel_id=1, replica_groups=mesh['grp'=2,'seq'=4,'head'=2,'rep'=2] {'seq','head','rep'}, dimensions={0} | all-to-all | bytes 786432 | tf_op jit(solution)/shard_map/all_to_all | solution.py:296
  23.9 2.5 %second_section.1 = bf16[16,13,8,128]{3,2,1,0:T(8,128)(2,1)} custom-call(bf16[16,2,6,8,128]{4,3,2,1,0:T(8,128)(2,1)} %all_to_all.10.z_ref, bf16[256,256]{1,0:T(8,128)(2,1)} %constant.37.clone.high_ref, bf16[256,256]{1,0:T(8,128)(2,1)} %constant.38.clone.low_ref), custom_call_target="tpu_custom_call" | custom-call | flops 3000000000 | bytes 9000000 | tf_op jit(solution)/shard_map/second_section/pallas_call | solution.py:221
  26.4 17.0 %all_to_all.11.x_ref = bf16[16,13,8,128]{3,2,1,0:T(8,128)(2,1)} all-to-all(bf16[16,13,8,128]{3,2,1,0:T(8,128)(2,1)} %second_section.1), channel_id=1, replica_groups=mesh['grp'=2,'seq'=4,'head'=2,'rep'=2] {'seq','head','rep'}, dimensions={0} | all-to-all | bytes 851968 | tf_op jit(solution)/shard_map/all_to_all | solution.py:299
  43.4 2.9 %order_patches.1.refs_0_.refs_2_.pat_ref = bf16[520,384]{1,0:T(8,128)(2,1)} custom-call(bf16[16,13,8,128]{3,2,1,0:T(8,128)(2,1)} %all_to_all.11.x_ref, bf16[2,208,384]{2,1,0:T(8,128)(2,1)} %constant.39.clone.perm_ref, bf16[2,192,384]{2,1,0:T(8,128)(2,1)} %constant.40.clone.rim_ref), custom_call_target="tpu_custom_call" | custom-call | flops 3000000000 | bytes 9000000 | tf_op jit(solution)/shard_map/order_patches/pallas_call | solution.py:271
  47.5 1.2 collective-permute-start.1
  48.8 0.8 copy-done.10
  49.5 14.3 %block_states.2 = (bf16[1024,1024]{1,0:T(8,128)(2,1)}, bf16[1024,512]{1,0:T(8,128)(2,1)}, bf16[1024,128]{1,0:T(8,128)(2,1)}, bf16[1024,128]{1,0:T(8,128)(2,1)}, ...) custom-call(s32[2]{0:T(128)} %pad_add_fusion.me_ref, ...), custom_call_target="tpu_custom_call" | custom-call | flops 12999999488 | bytes 39000000 | tf_op jit(solution)/shard_map/block_states/pallas_call | solution.py:451
  64.5 1.4 collective-permute-done.2.refs_1_
  66.6 14.6 %block_states.3 = (bf16[1024,1024]{1,0:T(8,128)(2,1)}, bf16[1024,512]{1,0:T(8,128)(2,1)}, bf16[1024,128]{1,0:T(8,128)(2,1)}, bf16[1024,128]{1,0:T(8,128)(2,1)}, ...) custom-call(s32[2]{0:T(128)} %pad_add_fusion.me_ref, ...), custom_call_target="tpu_custom_call" | custom-call | flops 12999999488 | bytes 39000000 | tf_op jit(solution)/shard_map/block_states/pallas_call | solution.py:451
  81.2 1.3 collective-permute-start.3
  82.5 1.3 collective-permute-start.4
  83.8 1.5 %collective-permute-start.5 = (bf16[136,512]{1,0:T(8,128)(2,1)}, bf16[136,512]{1,0:T(8,128)(2,1)S(1)}, u32[]{:S(2)}, u32[]{:S(2)}) collective-permute-start(bf16[136,512]{1,0:T(8,128)(2,1)} %get-tuple-element.50), channel_id=1, source_target_pairs={{0,12},{1,13},{2,14},{3,15},{16,28},{17,29},{18,30},{19,31}} | collective-permute-start | bytes 417800 | tf_op jit(solution)/shard_map/ppermute | solution.py:623
  85.3 7.2 %local_part.2 = (bf16[1024,512]{1,0:T(8,128)(2,1)}, bf16[1024,512]{1,0:T(8,128)(2,1)}) custom-call(bf16[1024,1024]{1,0:T(8,128)(2,1)} %get-tuple-element.39.normed_ref, bf16[1024,512]{1,0:T(8,128)(2,1)} %get-tuple-element.40.x_ref, bf16[1024,128]{1,0:T(8,128)(2,1)} %get-tuple-element.41.b_ref, bf16[1024,128]{1,0:T(8,128)(2,1)} %get-tuple-element.42.c_ref, ...), custom_call_target="tpu_custom_call" | custom-call | flops 7000000000 | bytes 21000000 | tf_op jit(solution)/shard_map/local_part/pallas_call | solution.py:509
  92.5 5.1 %collective-permute-done.4.refs_3_ = bf16[136,512]{1,0:T(8,128)(2,1)S(1)} collective-permute-done((bf16[136,512]{1,0:T(8,128)(2,1)}, bf16[136,512]{1,0:T(8,128)(2,1)S(1)}, u32[]{:S(2)}, u32[]{:S(2)}) %collective-permute-start.4) | collective-permute-done | bytes 139296 | tf_op jit(solution)/shard_map/ppermute | solution.py:623
  98.3 5.6 %correct.2 = (bf16[512,512]{1,0:T(8,128)(2,1)}, bf16[512,512]{1,0:T(8,128)(2,1)}) custom-call(s32[2]{0:T(128)} %pad_add_fusion.me_ref, bf16[1024,512]{1,0:T(8,128)(2,1)} %get-tuple-element.45.yg_ref, bf16[1024,512]{1,0:T(8,128)(2,1)} %get-tuple-element.46.fac_ref, bf16[1024,128]{1,0:T(8,128)(2,1)} %get-tuple-element.42.c_ref, ...), custom_call_target="tpu_custom_call" | custom-call | flops 5000000000 | bytes 15000000 | tf_op jit(solution)/shard_map/correct/pallas_call | solution.py:551
  103.8 1.2 collective-permute-start.7
  105.0 7.1 %local_part.3 = (bf16[1024,512]{1,0:T(8,128)(2,1)}, bf16[1024,512]{1,0:T(8,128)(2,1)}) custom-call(bf16[1024,1024]{1,0:T(8,128)(2,1)} %get-tuple-element.52.normed_ref, bf16[1024,512]{1,0:T(8,128)(2,1)} %get-tuple-element.53.x_ref, bf16[1024,128]{1,0:T(8,128)(2,1)} %get-tuple-element.54.b_ref, bf16[1024,128]{1,0:T(8,128)(2,1)} %get-tuple-element.55.c_ref, ...), custom_call_target="tpu_custom_call" | custom-call | flops 50000000 | bytes 150000 | tf_op jit(solution)/shard_map/local_part/pallas_call | solution.py:509
  112.2 5.6 %correct.3 = (bf16[512,512]{1,0:T(8,128)(2,1)}, bf16[512,512]{1,0:T(8,128)(2,1)}) custom-call(s32[2]{0:T(128)} %pad_add_fusion.me_ref, bf16[1024,512]{1,0:T(8,128)(2,1)} %get-tuple-element.58.yg_ref, bf16[1024,512]{1,0:T(8,128)(2,1)} %get-tuple-element.59.fac_ref, bf16[1024,128]{1,0:T(8,128)(2,1)} %get-tuple-element.55.c_ref, ...), custom_call_target="tpu_custom_call" | custom-call | flops 50000000 | bytes 150000 | tf_op jit(solution)/shard_map/correct/pallas_call | solution.py:551
  117.7 1.4 collective-permute-start.6
  120.0 0.8 collective-permute-done.6.refs_1_
  120.9 11.9 %collective-permute-done.8.refs_3_ = bf16[512,512]{1,0:T(8,128)(2,1)S(1)} collective-permute-done((bf16[512,512]{1,0:T(8,128)(2,1)S(1)}, bf16[512,512]{1,0:T(8,128)(2,1)S(1)}, u32[]{:S(2)}, u32[]{:S(2)}) %collective-permute-start.8) | collective-permute-done | bytes 524320 | tf_op jit(solution)/shard_map/ppermute | solution.py:618
  132.7 0.8 copy-done.8
  133.5 7.0 %finish.1 = bf16[512,1024]{1,0:T(8,128)(2,1)} custom-call(s32[1]{0:T(128)} %bitcast.me_ref, bf16[520,384]{1,0:T(8,128)(2,1)} %order_patches.1.refs_0_.refs_2_.pat_ref, bf16[384,1024]{1,0:T(8,128)(2,1)} %we_ref.1, bf16[512,512]{1,0:T(8,128)(2,1)} %get-tuple-element.62.refs_0_, bf16[512,512]{1,0:T(8,128)(2,1)} %copy-done.7, bf16[512,512]{1,0:T(8,128)(2,1)} %copy-done.6, ...), custom_call_target="tpu_custom_call" | custom-call | flops 7000000000 | bytes 21000000 | tf_op jit(solution)/shard_map/finish/pallas_call | solution.py:599
  (33 shorter events, 4.4 us)
Async XLA Ops:
  43.4 3.0 %copy-start.4 = (bf16[1024]{0:T(1024)(128)(2,1)S(1)}, bf16[1024]{0:T(1024)(128)(2,1)}, u32[]{:S(2)}) copy-start(bf16[1024]{0:T(1024)(128)(2,1)} %param.34) | copy-start | bytes 6148
  46.2 2.5 %collective-permute-start = (bf16[520,384]{1,0:T(8,128)(2,1)}, bf16[520,384]{1,0:T(8,128)(2,1)S(1)}, u32[]{:S(2)}, u32[]{:S(2)}) collective-permute-start(bf16[520,384]{1,0:T(8,128)(2,1)} %order_patches.1.refs_0_.refs_2_.pat_ref), channel_id=1, source_target_pairs={{0,1},{1,0},{2,3},{3,2},{4,5},{5,4},{6,7},{7,6},{8,9},{9,8},{10,11... | collective-permute-start | bytes 1198088 | tf_op jit(solution)/shard_map/ppermute | solution.py:618
  47.5 16.3 %collective-permute-start.1 = (bf16[520,384]{1,0:T(8,128)(2,1)}, bf16[520,384]{1,0:T(8,128)(2,1)S(1)}, u32[]{:S(2)}, u32[]{:S(2)}) collective-permute-start(bf16[520,384]{1,0:T(8,128)(2,1)} %order_patches.1.refs_0_.refs_2_.pat_ref), channel_id=1, source_target_pairs={{0,2},{1,3},{2,0},{3,1},{4,6},{5,7},{6,4},{7,5},{8,10},{9,11},{10,... | collective-permute-start | bytes 1198088 | tf_op jit(solution)/shard_map/ppermute | solution.py:618
  48.8 0.8 copy-start.10
  63.9 2.0 %copy-start.9 = (bf16[520,384]{1,0:T(8,128)(2,1)}, bf16[520,384]{1,0:T(8,128)(2,1)S(1)}, u32[]{:S(2)}) copy-start(bf16[520,384]{1,0:T(8,128)(2,1)S(1)} %collective-permute-done.1.refs_0_.refs_2_) | copy-start | bytes 1198084
  63.9 2.0 %collective-permute-start.2 = (bf16[520,384]{1,0:T(8,128)(2,1)S(1)}, bf16[520,384]{1,0:T(8,128)(2,1)S(1)}, u32[]{:S(2)}, u32[]{:S(2)}) collective-permute-start(bf16[520,384]{1,0:T(8,128)(2,1)S(1)} %collective-permute-done.1.refs_0_.refs_2_), channel_id=1, source_target_pairs={{0,1},{1,0},{2,3},{3,2},{4,5},{5,4},{6,7},{7,6},{8,9},{9,8},{10,11... | collective-permute-start | bytes 1198088 | tf_op jit(solution)/shard_map/ppermute | solution.py:618
  65.9 0.8 copy-start.11
  81.2 11.2 %collective-permute-start.3 = (bf16[136,512]{1,0:T(8,128)(2,1)}, bf16[136,512]{1,0:T(8,128)(2,1)S(1)}, u32[]{:S(2)}, u32[]{:S(2)}) collective-permute-start(bf16[136,512]{1,0:T(8,128)(2,1)} %get-tuple-element.50), channel_id=1, source_target_pairs={{0,4},{4,8},{8,12},{1,5},{5,9},{9,13},{2,6},{6,10},{10,14},{3,7},{... | collective-permute-start | bytes 417800 | tf_op jit(solution)/shard_map/ppermute | solution.py:623
  82.5 15.0 %collective-permute-start.4 = (bf16[136,512]{1,0:T(8,128)(2,1)}, bf16[136,512]{1,0:T(8,128)(2,1)S(1)}, u32[]{:S(2)}, u32[]{:S(2)}) collective-permute-start(bf16[136,512]{1,0:T(8,128)(2,1)} %get-tuple-element.50), channel_id=1, source_target_pairs={{0,8},{4,12},{1,9},{5,13},{2,10},{6,14},{3,11},{7,15},{16,24},{20,... | collective-permute-start | bytes 417800 | tf_op jit(solution)/shard_map/ppermute | solution.py:623
  83.8 13.7 %collective-permute-start.5 = (bf16[136,512]{1,0:T(8,128)(2,1)}, bf16[136,512]{1,0:T(8,128)(2,1)S(1)}, u32[]{:S(2)}, u32[]{:S(2)}) collective-permute-start(bf16[136,512]{1,0:T(8,128)(2,1)} %get-tuple-element.50), channel_id=1, source_target_pairs={{0,12},{1,13},{2,14},{3,15},{16,28},{17,29},{18,30},{19,31}} | collective-permute-start | bytes 417800 | tf_op jit(solution)/shard_map/ppermute | solution.py:623
  92.5 5.1 %copy-start = (bf16[136,512]{1,0:T(8,128)(2,1)}, bf16[136,512]{1,0:T(8,128)(2,1)S(1)}, u32[]{:S(2)}) copy-start(bf16[136,512]{1,0:T(8,128)(2,1)S(1)} %collective-permute-done.3.refs_2_) | copy-start | bytes 417796
  97.6 0.7 copy-start.1
  97.6 0.7 copy-start.2
  103.8 17.0 %collective-permute-start.7 = (bf16[512,512]{1,0:T(8,128)(2,1)}, bf16[512,512]{1,0:T(8,128)(2,1)S(1)}, u32[]{:S(2)}, u32[]{:S(2)}) collective-permute-start(bf16[512,512]{1,0:T(8,128)(2,1)} %get-tuple-element.51), channel_id=1, source_target_pairs={{0,2},{1,3},{2,0},{3,1},{4,6},{5,7},{6,4},{7,5},{8,10},{9,11},{10,... | collective-permute-start | bytes 1572872 | tf_op jit(solution)/shard_map/ppermute | solution.py:618
  112.1 7.0 %copy-start.5 = (bf16[512,512]{1,0:T(8,128)(2,1)S(1)}, bf16[512,512]{1,0:T(8,128)(2,1)}, u32[]{:S(2)}) copy-start(bf16[512,512]{1,0:T(8,128)(2,1)} %get-tuple-element.64) | copy-start | bytes 1572868
  112.1 7.3 %copy-start.3 = (bf16[2048]{0:T(1024)(128)(2,1)S(1)}, bf16[2048]{0:T(1024)(128)(2,1)}, u32[]{:S(2)}) copy-start(bf16[2048]{0:T(1024)(128)(2,1)} %param.43) | copy-start | bytes 12292
  117.7 3.1 %collective-permute-start.6 = (bf16[512,512]{1,0:T(8,128)(2,1)}, bf16[512,512]{1,0:T(8,128)(2,1)S(1)}, u32[]{:S(2)}, u32[]{:S(2)}) collective-permute-start(bf16[512,512]{1,0:T(8,128)(2,1)} %get-tuple-element.63), channel_id=1, source_target_pairs={{0,1},{1,0},{2,3},{3,2},{4,5},{5,4},{6,7},{7,6},{8,9},{9,8},{10,11... | collective-permute-start | bytes 1572872 | tf_op jit(solution)/shard_map/ppermute | solution.py:618
  119.1 13.6 %collective-permute-start.8 = (bf16[512,512]{1,0:T(8,128)(2,1)S(1)}, bf16[512,512]{1,0:T(8,128)(2,1)S(1)}, u32[]{:S(2)}, u32[]{:S(2)}) collective-permute-start(bf16[512,512]{1,0:T(8,128)(2,1)S(1)} %copy-done.5), channel_id=1, source_target_pairs={{0,3},{1,2},{2,1},{3,0},{4,7},{5,6},{6,5},{7,4},{8,11},{9,10},{10,... | collective-permute-start | bytes 1572872 | tf_op jit(solution)/shard_map/ppermute | solution.py:618
  120.9 11.9 %copy-start.7 = (bf16[512,512]{1,0:T(8,128)(2,1)}, bf16[512,512]{1,0:T(8,128)(2,1)S(1)}, u32[]{:S(2)}) copy-start(bf16[512,512]{1,0:T(8,128)(2,1)S(1)} %collective-permute-done.6.refs_1_) | copy-start | bytes 1572868
  120.9 11.9 %copy-start.6 = (bf16[512,512]{1,0:T(8,128)(2,1)}, bf16[512,512]{1,0:T(8,128)(2,1)S(1)}, u32[]{:S(2)}) copy-start(bf16[512,512]{1,0:T(8,128)(2,1)S(1)} %collective-permute-done.7.refs_2_) | copy-start | bytes 1572868
  132.7 0.8 copy-start.8

commit v3 on v2

--- a/solution.py
+++ b/solution.py
@@ -11,6 +11,8 @@
 from jax.sharding import PartitionSpec as P
 
 SPAN = 256
+LOG2E = math.log2(math.e)
+TILE = 512
 EPSILON = 1e-05
 LANES = 128
 PATCH = 64
@@ -76,7 +78,7 @@
 
 
 def first_section(
-    rows_all, length, pos, amp, phase, mode, delay, bins, turn_ref, x_ref, twist_ref, high_ref, low_ref,
+    rows_all, length, pos, amp, phase, mode, delay, bins, turn_ref, x_ref, twist_ref, near_ref, high_ref, low_ref,
     out_ref, base, acc, lhs,
 ):
     channels = x_ref.shape[1]
@@ -132,12 +134,15 @@
     wide = (inner, row_block, LANES)
     parts = PATCH // inner
     width = LANES // parts
-    lanes = lax.broadcasted_iota(jnp.int32, wide, 2)
+    flat = (inner, LANES)
+    lanes = lax.broadcasted_iota(jnp.int32, flat, 1)
     outer = lax.div(lanes, width) + parts * lax.rem(lanes, width)
-    column = lax.broadcasted_iota(jnp.int32, wide, 0) + inner * outer
-    rows = pos[0] * row_block + lax.broadcasted_iota(jnp.int32, wide, 1)
-    angle = ((rows * column) & (length - 1)).astype(F32) * unit
-    cos, sin = jnp.cos(angle), jnp.sin(angle)
+    column = lax.broadcasted_iota(jnp.int32, flat, 0) + inner * outer
+    angle = ((pos[0] * row_block * column) & (length - 1)).astype(F32) * unit
+    turn_cos, turn_sin = jnp.cos(angle)[:, None, :], jnp.sin(angle)[:, None, :]
+    near_cos, near_sin = near_ref[0], near_ref[1]
+    cos = turn_cos * near_cos - turn_sin * near_sin
+    sin = turn_sin * near_cos + turn_cos * near_sin
     for c in range(channels):
         high, low = split(lhs[c].reshape(inner * row_block, 2 * LANES))
         got = mm(high, high_ref[...]) + mm(low, high_ref[...]) + mm(high, low_ref[...])
@@ -157,13 +162,16 @@
     lane = np.arange(LANES)
     twist = 2.0 * np.pi * (steps[:, None] * lane[None, :] % columns) / columns
     twists = np.stack([np.cos(twist), np.sin(twist)]).astype(np.float32)
+    column = steps[:, None] + inner * lane_bins(inner)[None, :]
+    near = 2.0 * np.pi * np.arange(row_block)[None, :, None] * column[:, None, :] / length
+    nears = np.stack([np.cos(near), np.sin(near)]).astype(np.float32)
     angle = 2.0 * np.pi * (lane[:, None] * lane_bins(inner)[None, :] % LANES) / LANES
     cos, sin = np.cos(angle), np.sin(angle)
     high, low = two_halves(np.block([[cos, sin], [-sin, cos]]))
     return pl.pallas_call(
         functools.partial(first_section, rows_all, length),
         out_shape=jax.ShapeDtypeStruct((inner, 2 * channels, row_block, LANES), BF16),
-        in_specs=[SMEM] * 7 + [VMEM] * 4,
+        in_specs=[SMEM] * 7 + [VMEM] * 5,
         out_specs=VMEM,
         scratch_shapes=[
             pltpu.VMEM((2, amp.shape[0], row_block, LANES), F32),
@@ -173,7 +181,7 @@
         compiler_params=PARAMS,
         cost_estimate=cost(7),
         name="first_section",
-    )(pos, amp.T, phase, mode, delay, bins.T, turns, grid_in, twists, high, low)
+    )(pos, amp.T, phase, mode, delay, bins.T, turns, grid_in, twists, nears, high, low)
 
 
 def second_section(reps, z_ref, high_ref, low_ref, out_ref):
@@ -325,7 +333,8 @@
 
 
 def silu(values):
-    return values * (1.0 / (1.0 + jnp.exp(-values)))
+    half = 0.5 * values
+    return half + half * jnp.tanh(half)
 
 
 def fold(ends, count, head, entering, upto=None):
@@ -346,28 +355,29 @@
     return mm(jnp.concatenate([high, low], axis=1), spread[...])
 
 
-def block_states(heads, per, before, final, me_ref, *refs):
+def block_states(heads, per, reps, before, final, me_ref, *refs):
     pats, refs = refs[:2], refs[2:]
     halo, we, nin, wx, wbc, wdt, dtb, alog, cx, cbc, spread = refs[:11]
     earlier, refs = refs[11 : 11 + before], refs[11 + before :]
     normed_ref, x_ref, b_ref, c_ref, cum_ref, step_ref, local_ref, grown_ref, st_ref = refs[:9]
-    xs, bcs, carried, total, low_tri, dts, rows = refs[-7:]
+    xs, bcs, carried, total, low_tri, dts, rows, tail = refs[-8:]
     block = pl.program_id(0)
     state = wbc.shape[1] // 2
     taps = cx.shape[0]
 
+    gains = nin[...].astype(F32)
+    gains = jnp.concatenate([gains[i : i + 1] for i in range(gains.shape[0])], axis=1)
+
     def features(p):
         embedded = mm(p, we[...]).astype(BF16).astype(F32)
         scale = norm_rows(embedded, embedded.shape[-1])
-        return (embedded * scale * nin[...].astype(F32)).astype(BF16)
+        return (embedded * scale * gains).astype(BF16)
 
     @pl.when(block == 0)
     def _():
         carried[...] = jnp.zeros_like(carried)
         total[...] = jnp.zeros_like(total)
-        past = features(halo[...])
-        xs[0:8] = mm(past, wx[...]).astype(BF16).astype(F32)
-        bcs[0:8] = mm(past, wbc[...]).astype(BF16).astype(F32)
+        tail[...] = halo[...].astype(F32)
         ri = lax.broadcasted_iota(jnp.int32, (SPAN, SPAN), 0)
         ci = lax.broadcasted_iota(jnp.int32, (SPAN, SPAN), 1)
         low_tri[...] = jnp.where(ri >= ci, 1.0, 0.0).astype(BF16)
@@ -376,53 +386,55 @@
         rows[0:1, 0:heads] = dtb[...]
         rows[1:2, 0:heads] = -jnp.exp(alog[...])
 
-    @pl.when(block > 0)
-    def _():
-        xs[0:8] = xs[SPAN : SPAN + 8]
-        bcs[0:8] = bcs[SPAN : SPAN + 8]
-
-    here = ((block // per) ^ me_ref[1]) == 0
-    normed = features(jnp.where(here, pats[0][...], pats[1][...]))
+    here = ((block // per) ^ lax.rem(me_ref[0], reps)) == 0
+    span = pats[0].shape[0]
+    patch = jnp.where(here, pats[0][...], pats[1][...]).astype(F32)
+    joined = features(jnp.concatenate([tail[...], patch], axis=0).astype(BF16))
+    tail[...] = patch[span - 8 :]
+    normed = joined[8:]
     normed_ref[...] = normed
     dts[:, 0:heads] = lax.dot_general(
         normed, wdt[...], (((1,), (1,)), ((), ())), preferred_element_type=F32
     )
-    bcs[8 : SPAN + 8] = mm(normed, wbc[...]).astype(BF16).astype(F32)
-    xs[8 : SPAN + 8] = mm(normed, wx[...]).astype(BF16).astype(F32)
-    step = dts[...] + rows[0:1]
-    step = jnp.maximum(step, 0.0) + jnp.log1p(jnp.exp(-jnp.abs(step)))
-    step_ref[...] = step
-    rated = step * rows[1:2]
-    one = rated.astype(BF16).astype(F32)
-    two = (rated - one).astype(BF16).astype(F32)
-    three = rated - one - two
-    packed = one + pltpu.roll(two, heads, 1) + pltpu.roll(three, 2 * heads, 1)
-    sums = mm(low_tri[...], packed.astype(BF16))
-    cum = sums + pltpu.roll(sums, LANES - heads, 1) + pltpu.roll(sums, LANES - 2 * heads, 1)
-    cum_ref[...] = cum
-    last = cum[SPAN - 1 : SPAN]
-    weights = expand(jnp.exp(last - cum) * step, spread)
-    grow = expand(
-        jnp.exp(jnp.concatenate([jnp.broadcast_to(last, (8, LANES)), total[...]], axis=0)), spread
-    )
-
-    def conv(buffer, kernel):
-        out = kernel[0:1] * buffer[9 - taps : 9 - taps + SPAN]
+    bcs[...] = mm(joined, wbc[...]).astype(BF16).astype(F32)
+    xs[...] = mm(joined, wx[...]).astype(BF16).astype(F32)
+    step_all = dts[...] + rows[0:1]
+    step_all = jnp.maximum(step_all, 0.0) + jnp.log1p(jnp.exp(-jnp.abs(step_all)))
+    step_ref[...] = step_all
+
+    def conv(buffer, kernel, at):
+        out = kernel[0:1] * buffer[at + 9 - taps : at + 9 - taps + SPAN]
         for i in range(1, taps):
-            out = out + kernel[i : i + 1] * buffer[9 - taps + i : 9 - taps + i + SPAN]
+            out = out + kernel[i : i + 1] * buffer[at + 9 - taps + i : at + 9 - taps + i + SPAN]
         return silu(out)
 
-    bc = conv(bcs, cbc)
-    b_ref[...] = bc[:, :state].astype(BF16)
-    c_ref[...] = bc[:, state:].astype(BF16)
-    bt = bc[:, :state].T.astype(BF16)
-    xc = conv(xs, cx).astype(BF16)
-    x_ref[...] = xc
-    weighted = (xc.astype(F32) * weights).astype(BF16)
-    local_ref[0] = carried[...]
-    grown_ref[0] = grow[8:16]
-    carried[...] = carried[...] * grow[0:1] + mm(bt, weighted)
-    total[...] = total[...] + last
+    for n in range(span // SPAN):
+        at = n * SPAN
+        step = step_all[at : at + SPAN]
+        rated = step * rows[1:2]
+        one = rated.astype(BF16).astype(F32)
+        two = (rated - one).astype(BF16).astype(F32)
+        three = rated - one - two
+        packed = one + pltpu.roll(two, heads, 1) + pltpu.roll(three, 2 * heads, 1)
+        sums = mm(low_tri[...], packed.astype(BF16))
+        cum = sums + pltpu.roll(sums, LANES - heads, 1) + pltpu.roll(sums, LANES - 2 * heads, 1)
+        cum_ref[at : at + SPAN] = cum
+        last = cum[SPAN - 1 : SPAN]
+        weights = expand(jnp.exp(last - cum) * step, spread)
+        grow = expand(
+            jnp.exp(jnp.concatenate([jnp.broadcast_to(last, (8, LANES)), total[...]], axis=0)), spread
+        )
+        bc = conv(bcs, cbc, at)
+        b_ref[at : at + SPAN] = bc[:, :state].astype(BF16)
+        c_ref[at : at + SPAN] = bc[:, state:].astype(BF16)
+        bt = bc[:, :state].T.astype(BF16)
+        xc = conv(xs, cx, at).astype(BF16)
+        x_ref[at : at + SPAN] = xc
+        weighted = (xc.astype(F32) * weights).astype(BF16)
+        local_ref[n] = carried[...]
+        grown_ref[n] = grow[8:16]
+        carried[...] = carried[...] * grow[0:1] + mm(bt, weighted)
+        total[...] = total[...] + last
 
     @pl.when(block == pl.num_programs(0) - 1)
     def _():
@@ -432,7 +444,8 @@
             everything = [e[...] for e in earlier] + [st_ref[...]]
             count = len(everything)
             send = refs[9]
-            send[0:state] = fold(everything, count, me_ref[0], jnp.zeros((state, xc.shape[1]), F32)).astype(BF16)
+            zero = jnp.zeros((state, xs.shape[1]), F32)
+            send[0:state] = fold(everything, count, lax.div(me_ref[0], reps), zero).astype(BF16)
             decay = everything[0][state : state + 8]
             for e in everything[1:]:
                 decay = decay * e[state : state + 8]
@@ -443,31 +456,34 @@
     rows_in, width = pats[0].shape
     model = consts[0].shape[1]
     tokens = own * len(pats)
-    per = own // SPAN
+    span = min(own, TILE)
+    per = own // span
     blocks = tokens // SPAN
-    row = lambda n: pl.BlockSpec((SPAN, n), lambda b, me: (b, 0))
+    subs = span // SPAN
+    row = lambda n: pl.BlockSpec((span, n), lambda b, me: (b, 0))
     fixed = pl.BlockSpec((state + 8, inner), lambda b, me: (0, 0))
     shape = lambda *d, t=F32: jax.ShapeDtypeStruct(d, t)
     return pl.pallas_call(
-        functools.partial(block_states, heads, per, len(earlier), final),
+        functools.partial(block_states, heads, per, len(pats), len(earlier), final),
         grid_spec=pltpu.PrefetchScalarGridSpec(
             num_scalar_prefetch=1,
-            grid=(blocks,),
-            in_specs=[pl.BlockSpec((SPAN, width), lambda b, me: (b % per, 0))] * len(pats)
+            grid=(tokens // span,),
+            in_specs=[pl.BlockSpec((span, width), lambda b, me: (b % per, 0))] * len(pats)
             + [pl.BlockSpec((8, width), lambda b, me: (own // 8, 0))]
             + [VMEM] * (len(consts) + len(earlier)),
             out_specs=[row(model), row(inner), row(state), row(state), row(LANES), row(LANES),
-                       pl.BlockSpec((1, state, inner), lambda b, me: (b, 0, 0)),
-                       pl.BlockSpec((1, 8, inner), lambda b, me: (b, 0, 0)), fixed]
+                       pl.BlockSpec((subs, state, inner), lambda b, me: (b, 0, 0)),
+                       pl.BlockSpec((subs, 8, inner), lambda b, me: (b, 0, 0)), fixed]
             + [fixed] * final,
             scratch_shapes=[
-                pltpu.VMEM((SPAN + 8, inner), F32),
-                pltpu.VMEM((SPAN + 8, 2 * state), F32),
+                pltpu.VMEM((span + 8, inner), F32),
+                pltpu.VMEM((span + 8, 2 * state), F32),
                 pltpu.VMEM((state, inner), F32),
                 pltpu.VMEM((8, LANES), F32),
                 pltpu.VMEM((SPAN, SPAN), BF16),
-                pltpu.VMEM((SPAN, LANES), F32),
+                pltpu.VMEM((span, LANES), F32),
                 pltpu.VMEM((8, LANES), F32),
+                pltpu.VMEM((8, width), F32),
             ],
         ),
         out_shape=[
@@ -481,136 +497,150 @@
     )(me, *pats, halo, *consts, *earlier)
 
 
-def local_part(heads, normed_ref, x_ref, b_ref, c_ref, cum_ref, step_ref, wz, spread, yg_ref, fac_ref, y_acc):
-    gate = silu(mm(normed_ref[...], wz[...]).astype(BF16).astype(F32))
+def outputs(
+    heads, chip, chips, reps, me_ref, normed_ref, x_ref, b_ref, c_ref, cum_ref, step_ref, local_ref, grown_ref,
+    wz, spread, *refs,
+):
+    ends, earlier = refs[:chips], refs[chips : -reps - 2]
+    outs, start, y_acc = refs[-reps - 2 : -2], refs[-2], refs[-1]
+    state = c_ref.shape[1]
+    block = pl.program_id(0)
+    per = pl.num_programs(0) // reps
+
+    @pl.when(block == 0)
+    def _():
+        entering = jnp.zeros((state, x_ref.shape[1]), F32)
+        for part in reversed(earlier):
+            entering = part[0:state].astype(F32) + part[state : state + 1].astype(F32) * entering
+        place = lax.div(me_ref[0], reps)
+        start[...] = fold([e[...] for e in ends], chips - 1, place, entering, place ^ chip)
+
     cum = cum_ref[...]
-    cum_t = cum.T
-    step_t = step_ref[...].T
+    log_cum = cum * LOG2E
+    back = (log_cum - jnp.log2(step_ref[...])).T
     gram = lax.dot_general(
         c_ref[...], b_ref[...], (((1,), (1,)), ((), ())), preferred_element_type=F32
     )
-    ri = lax.broadcasted_iota(jnp.int32, (SPAN, SPAN), 0)
-    ci = lax.broadcasted_iota(jnp.int32, (SPAN, SPAN), 1)
+    gate = silu(mm(normed_ref[...], wz[...]).astype(BF16).astype(F32))
+    half = SPAN // 2
+    ri = lax.broadcasted_iota(jnp.int32, (half, half), 0)
+    ci = lax.broadcasted_iota(jnp.int32, (half, half), 1)
     inside = ri >= ci
     head_dim = x_ref.shape[1] // heads
     for h in range(heads):
-        gap = cum[:, h : h + 1] - cum_t[h : h + 1, :]
-        seg = jnp.exp(jnp.where(inside, gap, -jnp.inf))
-        scores = (gram * seg * step_t[h : h + 1, :]).astype(BF16)
         cols = slice(h * head_dim, (h + 1) * head_dim)
-        y_acc[:, cols] = mm(scores, x_ref[:, cols])
-    fac_ref[...] = (expand(jnp.exp(cum), spread) * gate).astype(BF16)
-    yg_ref[...] = (y_acc[...] * gate).astype(BF16)
-
-
-def run_local(micros, heads, normed, xc, bm, cm, cum, step, wz, spread):
-    tokens, inner = xc.shape
-    row = lambda n: pl.BlockSpec((SPAN, n), lambda b: (b, 0))
-    return pl.pallas_call(
-        functools.partial(local_part, heads),
-        grid=(tokens // SPAN,),
-        in_specs=[row(a.shape[1]) for a in (normed, xc, bm, cm, cum, step)] + [VMEM] * 2,
-        out_specs=[row(inner)] * 2,
-        scratch_shapes=[pltpu.VMEM((SPAN, inner), F32)],
-        out_shape=[jax.ShapeDtypeStruct((tokens, inner), BF16)] * 2,
-        compiler_params=PARAMS,
-        cost_estimate=cost(micros),
-        name="local_part",
-    )(normed, xc, bm, cm, cum, step, wz, spread)
-
-
-def correct(chip, chips, reps, me_ref, yg_ref, fac_ref, c_ref, local_ref, grown_ref, *refs):
-    ends, earlier = refs[:chips], refs[chips : -reps - 1]
-    outs, start = refs[-reps - 1 : -1], refs[-1]
-    state = c_ref.shape[1]
-    block = pl.program_id(0)
-    per = pl.num_programs(0) // reps
-
-    @pl.when(block == 0)
-    def _():
-        entering = jnp.zeros((state, yg_ref.shape[1]), F32)
-        for part in reversed(earlier):
-            entering = part[0:state].astype(F32) + part[state : state + 1].astype(F32) * entering
-        start[...] = fold([e[...] for e in ends], chips - 1, me_ref[0], entering, me_ref[0] ^ chip)
-
+        upper, lower = log_cum[:half, h : h + 1], log_cum[half:, h : h + 1]
+        early, late = back[h : h + 1, :half], back[h : h + 1, half:]
+        first = jnp.where(inside, jnp.exp2(upper - early), 0.0) * gram[:half, :half]
+        cross = jnp.exp2(lower - early) * gram[half:, :half]
+        second = jnp.where(inside, jnp.exp2(lower - late), 0.0) * gram[half:, half:]
+        y_acc[:half, cols] = mm(first.astype(BF16), x_ref[:half, cols])
+        y_acc[half:, cols] = mm(
+            jnp.concatenate([cross.astype(BF16), second.astype(BF16)], axis=1), x_ref[:, cols]
+        )
     cm = c_ref[...]
     high, low = split(local_ref[0] + grown_ref[0, 0:1] * start[...])
     added = mm(jnp.concatenate([cm, cm], axis=1), jnp.concatenate([high, low], axis=0))
-    value = (yg_ref[...].astype(F32) + fac_ref[...].astype(F32) * added).astype(BF16)
+    value = ((y_acc[...] + expand(jnp.exp(cum), spread) * added) * gate).astype(BF16)
     for r in range(reps):
-        @pl.when((block // per) == (me_ref[1] ^ r))
+        @pl.when((block // per) == (lax.rem(me_ref[0], reps) ^ r))
         def _(r=r):
             outs[r][pl.ds(pl.multiple_of((block % per) * SPAN, SPAN), SPAN), :] = value
 
 
-def run_correct(chip, reps, me, yg, fac, cm, local, grown, ends, earlier, own):
-    tokens, inner = yg.shape
+def run_outputs(heads, chip, reps, me, normed, xc, bm, cm, cum, step, local, grown, wz, spread, ends, earlier, own):
+    tokens, inner = xc.shape
     state = cm.shape[1]
-    block = lambda b, me: (b, 0)
+    row = lambda n: pl.BlockSpec((SPAN, n), lambda b, me: (b, 0))
     block3 = lambda b, me: (b, 0, 0)
     return pl.pallas_call(
-        functools.partial(correct, chip, len(ends), reps),
+        functools.partial(outputs, heads, chip, len(ends), reps),
         grid_spec=pltpu.PrefetchScalarGridSpec(
             num_scalar_prefetch=1,
             grid=(tokens // SPAN,),
-            in_specs=[pl.BlockSpec((SPAN, inner), block)] * 2 + [pl.BlockSpec((SPAN, state), block),
-                      pl.BlockSpec((1, state, inner), block3), pl.BlockSpec((1, 8, inner), block3)]
-            + [VMEM] * (len(earlier) + len(ends)),
+            in_specs=[row(a.shape[1]) for a in (normed, xc, bm, cm, cum, step)]
+            + [pl.BlockSpec((1, state, inner), block3), pl.BlockSpec((1, 8, inner), block3)]
+            + [VMEM] * (2 + len(earlier) + len(ends)),
             out_specs=[pl.BlockSpec((own, inner), lambda b, me: (0, 0))] * reps,
-            scratch_shapes=[pltpu.VMEM((state, inner), F32)],
+            scratch_shapes=[pltpu.VMEM((state, inner), F32), pltpu.VMEM((SPAN, inner), F32)],
         ),
         out_shape=[jax.ShapeDtypeStruct((own, inner), BF16)] * reps,
         compiler_params=PARAMS,
-        cost_estimate=cost(5 if chip else 0.05),
-        name="correct",
-    )(me, yg, fac, cm, local, grown, *ends, *earlier)
-
-
-def finish(count, me_ref, pat_ref, we_ref, *refs):
-    parts, norms, weights, out_ref = refs[:count], refs[count : 2 * count], refs[2 * count : -1], refs[-1]
-    values = [p[...].astype(F32) for p in parts]
-    square = values[0] * values[0]
-    for v in values[1:]:
-        square = square + v * v
-    inner = values[0].shape[1]
-    scale = lax.rsqrt(
-        jnp.sum(square, axis=-1, keepdims=True) * (1.0 / (count * inner)) + EPSILON
-    )
-    out = mm(pat_ref[...], we_ref[...]).astype(BF16).astype(F32)
-    mixed = None
-    for v, n, w in zip(values, norms, weights):
-        part = mm((v * scale * n[...].astype(F32)).astype(BF16), w[0])
-        mixed = part if mixed is None else mixed + part
-    out_ref[...] = (out + mixed).astype(BF16)
-
-
-def run_finish(me, patches, we, parts, norm_out, w_out):
-    count = len(parts)
+        cost_estimate=cost(9 if chip else 0.05),
+        name="outputs",
+    )(me, normed, xc, bm, cm, cum, step, local, grown, wz, spread, *ends, *earlier)
+
+
+def mix_most(count, me_ref, pat_ref, we_ref, *refs):
+    parts, (norm, weight, embed_ref, mixed_ref, square_ref) = refs[:count], refs[count:]
+    step = pl.program_id(0)
+
+    @pl.when(step == 0)
+    def _():
+        embed_ref[...] = mm(pat_ref[...], we_ref[...]).astype(BF16)
+        square = None
+        for part in parts:
+            v = part[...].astype(F32)
+            square = v * v if square is None else square + v * v
+        square_ref[...] = jnp.broadcast_to(jnp.sum(square, axis=-1, keepdims=True), square_ref.shape)
+
+    for n in range(count):
+        @pl.when(step == n)
+        def _(n=n):
+            left = (parts[n][...].astype(F32) * norm[...].astype(F32)).astype(BF16)
+            got = mm(left, weight[0])
+            mixed_ref[...] = got if n == 0 else mixed_ref[...] + got
+
+
+def mix_last(total, me_ref, embed_ref, mixed_ref, square_ref, part_ref, norm, weight, out_ref):
+    v = part_ref[...].astype(F32)
+    got = mm((v * norm[...].astype(F32)).astype(BF16), weight[0])
+    square = square_ref[:, 0:1] + jnp.sum(v * v, axis=-1, keepdims=True)
+    scale = lax.rsqrt(square * (1.0 / total) + EPSILON)
+    out_ref[...] = (embed_ref[...].astype(F32) + scale * (mixed_ref[...] + got)).astype(BF16)
+
+
+def run_mix(me, patches, we, parts, norm_out, w_out):
+    share = len(parts)
+    count = share - 1
     own, inner = parts[0].shape
     width = w_out.shape[1]
-    tile = min(own, SPAN)
     norms = norm_out[None]
-    weights = w_out.reshape(count, inner, width)
-    picks = [
-        pl.BlockSpec((1, inner), lambda i, me, d=d: (0, me[0] ^ d)) for d in range(count)
-    ] + [
-        pl.BlockSpec((1, inner, width), lambda i, me, d=d: (me[0] ^ d, 0, 0)) for d in range(count)
-    ]
+    weights = w_out.reshape(share, inner, width)
+    full = pl.BlockSpec((own, width), lambda d, me: (0, 0))
+    embed, mixed, square = pl.pallas_call(
+        functools.partial(mix_most, count),
+        grid_spec=pltpu.PrefetchScalarGridSpec(
+            num_scalar_prefetch=1,
+            grid=(count,),
+            in_specs=[pl.BlockSpec((own, patches.shape[1]), lambda d, me: (0, 0)), VMEM] + [VMEM] * count
+            + [pl.BlockSpec((1, inner), lambda d, me: (0, me[0] ^ d)),
+               pl.BlockSpec((1, inner, width), lambda d, me: (me[0] ^ d, 0, 0))],
+            out_specs=[full, full, pl.BlockSpec((own, LANES), lambda d, me: (0, 0))],
+        ),
+        out_shape=[jax.ShapeDtypeStruct((own, width), BF16), jax.ShapeDtypeStruct((own, width), F32),
+                   jax.ShapeDtypeStruct((own, LANES), F32)],
+        compiler_params=PARAMS,
+        cost_estimate=cost(0.05),
+        name="mix_most",
+    )(me, patches, we, *parts[:count], norms, weights)
+    tile = SPAN
+    row = lambda n: pl.BlockSpec((tile, n), lambda i, me: (i, 0))
     return pl.pallas_call(
-        functools.partial(finish, count),
+        functools.partial(mix_last, share * inner),
         grid_spec=pltpu.PrefetchScalarGridSpec(
             num_scalar_prefetch=1,
             grid=(own // tile,),
-            in_specs=[pl.BlockSpec((tile, patches.shape[1]), lambda i, me: (i, 0)), VMEM]
-            + [pl.BlockSpec((tile, inner), lambda i, me: (i, 0))] * count
-            + picks,
-            out_specs=pl.BlockSpec((tile, width), lambda i, me: (i, 0)),
+            in_specs=[row(width), row(width), row(LANES), row(inner),
+                      pl.BlockSpec((1, inner), lambda i, me: (0, me[0] ^ count)),
+                      pl.BlockSpec((1, inner, width), lambda i, me: (me[0] ^ count, 0, 0))],
+            out_specs=row(width),
         ),
         out_shape=jax.ShapeDtypeStruct((own, width), BF16),
         compiler_params=PARAMS,
-        cost_estimate=cost(7),
-        name="finish",
-    )(me, patches, we, *parts, *([norms] * count), *([weights] * count))
+        cost_estimate=cost(3),
+        name="mix_last",
+    )(me, embed, mixed, square, parts[count], norms, weights)
 
 
 def swap(value, flip):
@@ -639,14 +669,13 @@
     patches = make_patches(first, length)
     own = patches.shape[0] - 8
     reps, chips = lax.axis_size("rep"), lax.axis_size("head")
-    place = jnp.stack([lax.axis_index("head"), lax.axis_index("rep")]).astype(jnp.int32)
     heads, inner, state = dt_bias.shape[0], w_x.shape[1], w_bc.shape[1] // 2
     spread = np.zeros((2 * LANES, inner), ml_dtypes.bfloat16)
     for h in range(heads):
         spread[h, h * (inner // heads) : (h + 1) * (inner // heads)] = 1
     spread[LANES:] = spread[:LANES]
     consts = (
-        w_embed, norm_in[None], w_x, w_bc, w_dt.T, dt_bias[None], a_log[None], conv_x, conv_bc,
+        w_embed, norm_in.reshape(-1, LANES), w_x, w_bc, w_dt.T, dt_bias[None], a_log[None], conv_x, conv_bc,
         jnp.asarray(spread),
     )
     done, ends = [], []
@@ -657,7 +686,7 @@
             start, ends[-1] = lax.optimization_barrier((start, ends[-1]))
         group = [start] + [swap(start, r) for r in range(1, reps)]
         got = run_states(
-            place, group, start, consts, heads, inner, state, own, ends, c == chips - 1
+            me, group, start, consts, heads, inner, state, own, ends, c == chips - 1
         )
         done.append(got[:8])
         ends.append(got[8])
@@ -669,13 +698,18 @@
         normed, xc, bm, cm, cum, step, local, grown = done[c]
         if gate is not None:
             normed, gate = lax.optimization_barrier((normed, gate))
-        yg, fac = run_local(7 if c else 0.05, heads, normed, xc, bm, cm, cum, step, w_z, spread)
-        values = run_correct(c, reps, place, yg, fac, cm, local, grown, ends, earlier, own)
+        values = run_outputs(
+            heads, c, reps, me, normed, xc, bm, cm, cum, step, local, grown, w_z, spread, ends, earlier, own
+        )
         gate = values[0]
         for r in reversed(range(reps)):
             d = c * reps + r
-            parts[d] = swap(values[r], d) if d else values[r]
-    return run_finish(me, patches, w_embed, parts, norm_out, w_out)
+            if d == 1:
+                half = own // 2
+                parts[d] = jnp.concatenate([swap(values[r][:half], d), swap(values[r][half:], d)], 0)
+            else:
+                parts[d] = swap(values[r], d) if d else values[r]
+    return run_mix(me, patches, w_embed, parts, norm_out, w_out)
 
 
 def solution(mesh):

time: 141 us -> 133 us (0.943)
  Pallas kernels: 74.1 us -> 64.6 us
    pallas_call x7 -> x6, Pallas kernels: 61.4 us -> 52.1 us  [the longest x2 25.2 us: run_states(): pl.pallas_call(functools.partial(block_states, heads, per, len(pats), len...]
    ppermute x6 -> x7, waiting for transfers between devices: 14 us -> 5.6 us  [swap(): return lax.ppermute(value, HR, [(i, i ^ flip) for i in range(count)])]
    ppermute x3, waiting for transfers between devices: 5.06 us -> 13 us  [shift(): return lax.ppermute(value, 'seq', [(i, i + by) for i in range(count - by)])]
    unnamed x24 -> x18, local copies, waits for them, and re-layouts: 3.03 us -> 3.83 us
    ppermute x6 -> x7, starting transfers between devices: 4.86 us -> 5 us  [swap(): return lax.ppermute(value, HR, [(i, i ^ flip) for i in range(count)])]
  transfers between devices with their start and end apart: 9 -> 10, of which waited for: 4 -> 7; matrix products, arithmetic and copies ran while one was open for 1% -> 2% of each run, Pallas kernels for 24% -> 21%
where the time goes in v3:
time: 133 us; the launch traced here: 132 us
  Pallas kernels  64.6 us (49%)
  blocking collectives  33.4 us (25%)
  waiting for transfers between devices  18.6 us (14%)
  starting transfers between devices  9.05 us (7%)
  local copies, waits for them, and re-layouts  5.5 us (4%)
    pallas_call x2, Pallas kernels, run_states(): pl.pallas_call(functools.partial(block_states, heads, per, len(pats), len...  25.2 us
    all_to_all x1, blocking collectives, make_patches(): moved = lax.all_to_all(run_second(moved, length), ALL, 0, 0, tiled=True)  17 us
    all_to_all x1, blocking collectives, make_patches(): lax.all_to_all(first.reshape(devices, own, pairs, row_block, LANES), ALL,...  16.4 us
    pallas_call x2, Pallas kernels, run_outputs(): pl.pallas_call(functools.partial(outputs, heads, chip, len(ends), reps),...  15.8 us
    ppermute x3, waiting for transfers between devices, shift(): return lax.ppermute(value, 'seq', [(i, i + by) for i in range(count - by)])  13 us
    pallas_call x1, Pallas kernels, run_first(): pl.pallas_call(functools.partial(first_section, rows_all, length), out_sh...  7.17 us
    pallas_call x1, Pallas kernels, run_mix(): pl.pallas_call(functools.partial(mix_most, count), grid_spec=pltpu.Prefet...  7.14 us
    ppermute x7, waiting for transfers between devices, swap(): return lax.ppermute(value, HR, [(i, i ^ flip) for i in range(count)])  5.6 us
  transfers between devices with their start and end apart: 10, of which 7 were waited for; matrix products, arithmetic and copies ran while one was open for 2% of the time, Pallas kernels for 21%

profile of v3, /device:TPU:25, one launch (start us, length us, event | category | flops | bytes accessed | tf_op | source)
XLA Modules:
  0.0 132.1 jit_solution(598345599160224809)
XLA Ops:
  0.0 7.2 %first_section.1 = bf16[32,6,8,128]{3,2,1,0:T(8,128)(2,1)} custom-call(s32[1]{0:T(128)} %bitcast.1.pos, f32[3,16]{1,0:T(4,128)} %bitcast.19, f32[16]{0:T(128)} %phase.1, s32[16]{0:T(128)} %mode.1, s32[16]{0:T(128)} %delay.1, s32[2,16]{1,0:T(2,128)} %bitcast.22, f32[2,32]{1,0:T(2,128)} %constant.35.clone.turn_ref, f32[2,3,32,8,128]{4,3,2,1,0:T(8,128)} %bitcast.16, ...), custom_call_target="tpu_custom_call" | custom-call | flops 7000000000 | bytes 21000000 | tf_op jit(solution)/shard_map/first_section/pallas_call | solution.py:171
  7.2 16.4 %all_to_all.10.z_ref = bf16[16,2,6,8,128]{4,3,2,1,0:T(8,128)(2,1)} all-to-all(bf16[16,2,6,8,128]{4,3,2,1,0:T(8,128)(2,1)} %bitcast.15), channel_id=1, replica_groups=mesh['grp'=2,'seq'=4,'head'=2,'rep'=2] {'seq','head','rep'}, dimensions={0} | all-to-all | bytes 786432 | tf_op jit(solution)/shard_map/all_to_all | solution.py:304
  23.6 2.5 %second_section.1 = bf16[16,13,8,128]{3,2,1,0:T(8,128)(2,1)} custom-call(bf16[16,2,6,8,128]{4,3,2,1,0:T(8,128)(2,1)} %all_to_all.10.z_ref, bf16[256,256]{1,0:T(8,128)(2,1)} %constant.40.clone.high_ref, bf16[256,256]{1,0:T(8,128)(2,1)} %constant.41.clone.low_ref), custom_call_target="tpu_custom_call" | custom-call | flops 3000000000 | bytes 9000000 | tf_op jit(solution)/shard_map/second_section/pallas_call | solution.py:229
  26.1 17.0 %all_to_all.11.x_ref = bf16[16,13,8,128]{3,2,1,0:T(8,128)(2,1)} all-to-all(bf16[16,13,8,128]{3,2,1,0:T(8,128)(2,1)} %second_section.1), channel_id=1, replica_groups=mesh['grp'=2,'seq'=4,'head'=2,'rep'=2] {'seq','head','rep'}, dimensions={0} | all-to-all | bytes 851968 | tf_op jit(solution)/shard_map/all_to_all | solution.py:307
  43.1 2.9 %order_patches.1.refs_0_.refs_2_.pat_ref = bf16[520,384]{1,0:T(8,128)(2,1)} custom-call(bf16[16,13,8,128]{3,2,1,0:T(8,128)(2,1)} %all_to_all.11.x_ref, bf16[2,208,384]{2,1,0:T(8,128)(2,1)} %constant.42.clone.perm_ref, bf16[2,192,384]{2,1,0:T(8,128)(2,1)} %constant.43.clone.rim_ref), custom_call_target="tpu_custom_call" | custom-call | flops 3000000000 | bytes 9000000 | tf_op jit(solution)/shard_map/order_patches/pallas_call | solution.py:279
  46.0 1.2 collective-permute-start.1
  48.6 12.4 %block_states.2 = (bf16[1024,1024]{1,0:T(8,128)(2,1)}, bf16[1024,512]{1,0:T(8,128)(2,1)}, bf16[1024,128]{1,0:T(8,128)(2,1)}, bf16[1024,128]{1,0:T(8,128)(2,1)}, ...) custom-call(s32[1]{0:T(128)} %bitcast.me_ref, ...), custom_call_target="tpu_custom_call" | custom-call | flops 12999999488 | bytes 39000000 | tf_op jit(solution)/shard_map/block_states/pallas_call | solution.py:466
  61.3 1.6 %collective-permute-done.2.refs_1_ = bf16[520,384]{1,0:T(8,128)(2,1)S(1)} collective-permute-done((bf16[520,384]{1,0:T(8,128)(2,1)S(1)}, bf16[520,384]{1,0:T(8,128)(2,1)S(1)}, u32[]{:S(2)}, u32[]{:S(2)}) %collective-permute-start.2) | collective-permute-done | bytes 399392 | tf_op jit(solution)/shard_map/ppermute | solution.py:648
  63.7 12.7 %block_states.3 = (bf16[1024,1024]{1,0:T(8,128)(2,1)}, bf16[1024,512]{1,0:T(8,128)(2,1)}, bf16[1024,128]{1,0:T(8,128)(2,1)}, bf16[1024,128]{1,0:T(8,128)(2,1)}, ...) custom-call(s32[1]{0:T(128)} %bitcast.me_ref, ...), custom_call_target="tpu_custom_call" | custom-call | flops 12999999488 | bytes 39000000 | tf_op jit(solution)/shard_map/block_states/pallas_call | solution.py:466
  76.4 1.3 collective-permute-start.3
  77.7 1.3 collective-permute-start.4
  79.0 1.5 %collective-permute-start.5 = (bf16[136,512]{1,0:T(8,128)(2,1)}, bf16[136,512]{1,0:T(8,128)(2,1)S(1)}, u32[]{:S(2)}, u32[]{:S(2)}) collective-permute-start(bf16[136,512]{1,0:T(8,128)(2,1)} %get-tuple-element.47), channel_id=1, source_target_pairs={{0,12},{1,13},{2,14},{3,15},{16,28},{17,29},{18,30},{19,31}} | collective-permute-start | bytes 417800 | tf_op jit(solution)/shard_map/ppermute | solution.py:653
  80.5 3.2 %collective-permute-done.3.refs_2_ = bf16[136,512]{1,0:T(8,128)(2,1)S(1)} collective-permute-done((bf16[136,512]{1,0:T(8,128)(2,1)}, bf16[136,512]{1,0:T(8,128)(2,1)S(1)}, u32[]{:S(2)}, u32[]{:S(2)}) %collective-permute-start.3) | collective-permute-done | bytes 139296 | tf_op jit(solution)/shard_map/ppermute | solution.py:653
  83.7 9.9 %collective-permute-done.4.refs_3_ = bf16[136,512]{1,0:T(8,128)(2,1)S(1)} collective-permute-done((bf16[136,512]{1,0:T(8,128)(2,1)}, bf16[136,512]{1,0:T(8,128)(2,1)S(1)}, u32[]{:S(2)}, u32[]{:S(2)}) %collective-permute-start.4) | collective-permute-done | bytes 139296 | tf_op jit(solution)/shard_map/ppermute | solution.py:653
  94.3 7.9 %outputs.2 = (bf16[512,512]{1,0:T(8,128)(2,1)}, bf16[512,512]{1,0:T(8,128)(2,1)}) custom-call(s32[1]{0:T(128)} %bitcast.me_ref, bf16[1024,1024]{1,0:T(8,128)(2,1)} %get-tuple-element.38.normed_ref, bf16[1024,512]{1,0:T(8,128)(2,1)} %get-tuple-element.39.x_ref, bf16[1024,128]{1,0:T(8,128)(2,1)} %get-tuple-element.40.b_ref, ...), custom_call_target="tpu_custom_call" | custom-call | flops 8999999488 | bytes 27000000 | tf_op jit(solution)/shard_map/outputs/pallas_call | solution.py:556
  102.3 2.8 %collective-permute-start.9 = (bf16[512,512]{1,0:T(8,128)(2,1)}, bf16[512,512]{1,0:T(8,128)(2,1)S(1)}, u32[]{:S(2)}, u32[]{:S(2)}) collective-permute-start(bf16[512,512]{1,0:T(8,128)(2,1)} %get-tuple-element.62), channel_id=1, source_target_pairs={{0,3},{1,2},{2,1},{3,0},{4,7},{5,6},{6,5},{7,4},{8,11},{9,10},{10,... | collective-permute-start | bytes 1572872 | tf_op jit(solution)/shard_map/ppermute | solution.py:648
  105.1 7.8 %outputs.3 = (bf16[512,512]{1,0:T(8,128)(2,1)}, bf16[512,512]{1,0:T(8,128)(2,1)}) custom-call(s32[1]{0:T(128)} %bitcast.me_ref, bf16[1024,1024]{1,0:T(8,128)(2,1)} %get-tuple-element.49.normed_ref, bf16[1024,512]{1,0:T(8,128)(2,1)} %get-tuple-element.50.x_ref, bf16[1024,128]{1,0:T(8,128)(2,1)} %get-tuple-element.51.b_ref, ...), custom_call_target="tpu_custom_call" | custom-call | flops 50000000 | bytes 150000 | tf_op jit(solution)/shard_map/outputs/pallas_call | solution.py:556
  112.9 1.1 fusion
  116.0 0.8 pad_maximum_fusion.refs_1_
  116.8 0.8 copy-done
  117.6 7.1 %mix_most.1 = (bf16[512,1024]{1,0:T(8,128)(2,1)}, f32[512,1024]{1,0:T(8,128)}, f32[512,128]{1,0:T(8,128)}) custom-call(s32[1]{0:T(128)} %bitcast.me_ref, bf16[520,384]{1,0:T(8,128)(2,1)} %order_patches.1.refs_0_.refs_2_.pat_ref, bf16[384,1024]{1,0:T(8,128)(2,1)} %we_ref.1, bf16[512,512]{1,0:T(8,128)(2,1)} %get-tuple-element.57.refs_0_, ...), custom_call_target="tpu_custom_call" | custom-call | flops 50000000 | bytes 150000 | tf_op jit(solution)/shard_map/mix_most/pallas_call | solution.py:611
  124.7 2.6 %collective-permute-done.9.part_ref = bf16[512,512]{1,0:T(8,128)(2,1)S(1)} collective-permute-done((bf16[512,512]{1,0:T(8,128)(2,1)}, bf16[512,512]{1,0:T(8,128)(2,1)S(1)}, u32[]{:S(2)}, u32[]{:S(2)}) %collective-permute-start.9) | collective-permute-done | bytes 524320 | tf_op jit(solution)/shard_map/ppermute | solution.py:648
  127.4 0.8 copy-done.5
  128.2 4.0 %mix_last.1 = bf16[512,1024]{1,0:T(8,128)(2,1)} custom-call(s32[1]{0:T(128)} %bitcast.me_ref, bf16[512,1024]{1,0:T(8,128)(2,1)} %get-tuple-element.59.embed_ref, f32[512,1024]{1,0:T(8,128)} %get-tuple-element.60.mixed_ref, f32[512,128]{1,0:T(8,128)} %get-tuple-element.61.square_ref, bf16[512,512]{1,0:T(8,128)(2,1)} %copy-done.5, ...), custom_call_target="tpu_custom_call" | custom-call | flops 3000000000 | bytes 9000000 | tf_op jit(solution)/shard_map/mix_last/pallas_call | solution.py:629
  (28 shorter events, 5.2 us)
Async XLA Ops:
  45.9 1.9 %collective-permute-start = (bf16[520,384]{1,0:T(8,128)(2,1)}, bf16[520,384]{1,0:T(8,128)(2,1)S(1)}, u32[]{:S(2)}, u32[]{:S(2)}) collective-permute-start(bf16[520,384]{1,0:T(8,128)(2,1)} %order_patches.1.refs_0_.refs_2_.pat_ref), channel_id=1, source_target_pairs={{0,1},{1,0},{2,3},{3,2},{4,5},{5,4},{6,7},{7,6},{8,9},{9,8},{10,11... | collective-permute-start | bytes 1198088 | tf_op jit(solution)/shard_map/ppermute | solution.py:648
  46.0 15.1 %collective-permute-start.1 = (bf16[520,384]{1,0:T(8,128)(2,1)}, bf16[520,384]{1,0:T(8,128)(2,1)S(1)}, u32[]{:S(2)}, u32[]{:S(2)}) collective-permute-start(bf16[520,384]{1,0:T(8,128)(2,1)} %order_patches.1.refs_0_.refs_2_.pat_ref), channel_id=1, source_target_pairs={{0,2},{1,3},{2,0},{3,1},{4,6},{5,7},{6,4},{7,5},{8,10},{9,11},{10,... | collective-permute-start | bytes 1198088 | tf_op jit(solution)/shard_map/ppermute | solution.py:648
  47.9 0.8 copy-start.7
  61.1 1.8 %copy-start.6 = (bf16[520,384]{1,0:T(8,128)(2,1)}, bf16[520,384]{1,0:T(8,128)(2,1)S(1)}, u32[]{:S(2)}) copy-start(bf16[520,384]{1,0:T(8,128)(2,1)S(1)} %collective-permute-done.1.refs_0_.refs_2_) | copy-start | bytes 1198084
  61.1 1.8 %collective-permute-start.2 = (bf16[520,384]{1,0:T(8,128)(2,1)S(1)}, bf16[520,384]{1,0:T(8,128)(2,1)S(1)}, u32[]{:S(2)}, u32[]{:S(2)}) collective-permute-start(bf16[520,384]{1,0:T(8,128)(2,1)S(1)} %collective-permute-done.1.refs_0_.refs_2_), channel_id=1, source_target_pairs={{0,1},{1,0},{2,3},{3,2},{4,5},{5,4},{6,7},{7,6},{8,9},{9,8},{10,11... | collective-permute-start | bytes 1198088 | tf_op jit(solution)/shard_map/ppermute | solution.py:648
  62.9 0.8 copy-start.8
  76.4 7.2 %collective-permute-start.3 = (bf16[136,512]{1,0:T(8,128)(2,1)}, bf16[136,512]{1,0:T(8,128)(2,1)S(1)}, u32[]{:S(2)}, u32[]{:S(2)}) collective-permute-start(bf16[136,512]{1,0:T(8,128)(2,1)} %get-tuple-element.47), channel_id=1, source_target_pairs={{0,4},{4,8},{8,12},{1,5},{5,9},{9,13},{2,6},{6,10},{10,14},{3,7},{... | collective-permute-start | bytes 417800 | tf_op jit(solution)/shard_map/ppermute | solution.py:653
  77.7 15.8 %collective-permute-start.4 = (bf16[136,512]{1,0:T(8,128)(2,1)}, bf16[136,512]{1,0:T(8,128)(2,1)S(1)}, u32[]{:S(2)}, u32[]{:S(2)}) collective-permute-start(bf16[136,512]{1,0:T(8,128)(2,1)} %get-tuple-element.47), channel_id=1, source_target_pairs={{0,8},{4,12},{1,9},{5,13},{2,10},{6,14},{3,11},{7,15},{16,24},{20,... | collective-permute-start | bytes 417800 | tf_op jit(solution)/shard_map/ppermute | solution.py:653
  79.0 14.5 %collective-permute-start.5 = (bf16[136,512]{1,0:T(8,128)(2,1)}, bf16[136,512]{1,0:T(8,128)(2,1)S(1)}, u32[]{:S(2)}, u32[]{:S(2)}) collective-permute-start(bf16[136,512]{1,0:T(8,128)(2,1)} %get-tuple-element.47), channel_id=1, source_target_pairs={{0,12},{1,13},{2,14},{3,15},{16,28},{17,29},{18,30},{19,31}} | collective-permute-start | bytes 417800 | tf_op jit(solution)/shard_map/ppermute | solution.py:653
  83.7 9.9 %copy-start.1 = (bf16[136,512]{1,0:T(8,128)(2,1)}, bf16[136,512]{1,0:T(8,128)(2,1)S(1)}, u32[]{:S(2)}) copy-start(bf16[136,512]{1,0:T(8,128)(2,1)S(1)} %collective-permute-done.3.refs_2_) | copy-start | bytes 417796
  93.6 0.7 copy-start.2
  93.6 0.7 copy-start.3
  102.2 14.6 %collective-permute-start.8 = (bf16[512,512]{1,0:T(8,128)(2,1)}, bf16[512,512]{1,0:T(8,128)(2,1)S(1)}, u32[]{:S(2)}, u32[]{:S(2)}) collective-permute-start(bf16[512,512]{1,0:T(8,128)(2,1)} %get-tuple-element.48), channel_id=1, source_target_pairs={{0,2},{1,3},{2,0},{3,1},{4,6},{5,7},{6,4},{7,5},{8,10},{9,11},{10,... | collective-permute-start | bytes 1572872 | tf_op jit(solution)/shard_map/ppermute | solution.py:648
  102.3 25.1 %collective-permute-start.9 = (bf16[512,512]{1,0:T(8,128)(2,1)}, bf16[512,512]{1,0:T(8,128)(2,1)S(1)}, u32[]{:S(2)}, u32[]{:S(2)}) collective-permute-start(bf16[512,512]{1,0:T(8,128)(2,1)} %get-tuple-element.62), channel_id=1, source_target_pairs={{0,3},{1,2},{2,1},{3,0},{4,7},{5,6},{6,5},{7,4},{8,11},{9,10},{10,... | collective-permute-start | bytes 1572872 | tf_op jit(solution)/shard_map/ppermute | solution.py:648
  105.1 9.5 %copy-start.4 = (bf16[2048]{0:T(1024)(128)(2,1)S(1)}, bf16[2048]{0:T(1024)(128)(2,1)}, u32[]{:S(2)}) copy-start(bf16[2048]{0:T(1024)(128)(2,1)} %param.44) | copy-start | bytes 12292
  114.0 1.6 %collective-permute-start.6 = (bf16[256,512]{1,0:T(8,128)(2,1)S(1)}, bf16[256,512]{1,0:T(8,128)(2,1)S(1)}, u32[]{:S(2)}, u32[]{:S(2)}) collective-permute-start(bf16[256,512]{1,0:T(8,128)(2,1)S(1)} %get-tuple-element.63), channel_id=1, source_target_pairs={{0,1},{1,0},{2,3},{3,2},{4,5},{5,4},{6,7},{7,6},{8,9},{9,8},{10,11... | collective-permute-start | bytes 786440 | tf_op jit(solution)/shard_map/ppermute | solution.py:648
  114.1 1.9 %collective-permute-start.7 = (bf16[256,512]{1,0:T(8,128)(2,1)S(1)}, bf16[256,512]{1,0:T(8,128)(2,1)S(1)}, u32[]{:S(2)}, u32[]{:S(2)}) collective-permute-start(bf16[256,512]{1,0:T(8,128)(2,1)S(1)} %get-tuple-element.64), channel_id=1, source_target_pairs={{0,1},{1,0},{2,3},{3,2},{4,5},{5,4},{6,7},{7,6},{8,9},{9,8},{10,11... | collective-permute-start | bytes 786440 | tf_op jit(solution)/shard_map/ppermute | solution.py:648
  116.8 0.8 copy-start
  127.4 0.8 copy-start.5

commit v4 on v3

--- a/solution.py
+++ b/solution.py
@@ -497,23 +497,54 @@
     )(me, *pats, halo, *consts, *earlier)
 
 
+def gate_tokens(normed_ref, wz, gate_ref):
+    gate_ref[...] = silu(mm(normed_ref[...], wz[...]).astype(BF16).astype(F32)).astype(BF16)
+
+
+def run_gate(normed, wz):
+    tokens, width = normed.shape
+    inner = wz.shape[1]
+    span = min(tokens, TILE)
+    return pl.pallas_call(
+        gate_tokens,
+        grid=(tokens // span,),
+        in_specs=[pl.BlockSpec((span, width), lambda b: (b, 0)), VMEM],
+        out_specs=pl.BlockSpec((span, inner), lambda b: (b, 0)),
+        out_shape=jax.ShapeDtypeStruct((tokens, inner), BF16),
+        compiler_params=PARAMS,
+        cost_estimate=cost(4),
+        name="gate_tokens",
+    )(normed, wz)
+
+
 def outputs(
-    heads, chip, chips, reps, me_ref, normed_ref, x_ref, b_ref, c_ref, cum_ref, step_ref, local_ref, grown_ref,
-    wz, spread, *refs,
+    heads, chip, chips, seqs, reps, which, gated, opening, me_ref, normed_ref, x_ref, b_ref, c_ref, cum_ref, step_ref, local_ref, grown_ref,
+    *refs,
 ):
-    ends, earlier = refs[:chips], refs[chips : -reps - 2]
-    outs, start, y_acc = refs[-reps - 2 : -2], refs[-2], refs[-1]
+    if not gated:
+        wz, refs = refs[0], refs[1:]
+    spread, refs = refs[0], refs[1:]
+    if opening:
+        ends, earlier, refs = refs[:chips], refs[chips : chips + seqs], refs[chips + seqs :]
+        entries, refs = refs[:chips], refs[chips:]
+        start = entries[chip]
+    else:
+        start, refs = refs[0], refs[1:]
+    outs, y_acc = refs[:-1], refs[-1]
     state = c_ref.shape[1]
     block = pl.program_id(0)
-    per = pl.num_programs(0) // reps
-
-    @pl.when(block == 0)
-    def _():
-        entering = jnp.zeros((state, x_ref.shape[1]), F32)
-        for part in reversed(earlier):
-            entering = part[0:state].astype(F32) + part[state : state + 1].astype(F32) * entering
-        place = lax.div(me_ref[0], reps)
-        start[...] = fold([e[...] for e in ends], chips - 1, place, entering, place ^ chip)
+    per = pl.num_programs(0) // len(which)
+
+    if opening:
+        @pl.when(block == 0)
+        def _():
+            entering = jnp.zeros((state, x_ref.shape[1]), F32)
+            for part in reversed(earlier):
+                entering = part[0:state].astype(F32) + part[state : state + 1].astype(F32) * entering
+            place = lax.div(me_ref[0], reps)
+            known = [e[...] for e in ends]
+            for c in range(chips):
+                entries[c][...] = fold(known, chips - 1, place, entering, place ^ c)
 
     cum = cum_ref[...]
     log_cum = cum * LOG2E
@@ -521,7 +552,10 @@
     gram = lax.dot_general(
         c_ref[...], b_ref[...], (((1,), (1,)), ((), ())), preferred_element_type=F32
     )
-    gate = silu(mm(normed_ref[...], wz[...]).astype(BF16).astype(F32))
+    if gated:
+        gate = normed_ref[...].astype(F32)
+    else:
+        gate = silu(mm(normed_ref[...], wz[...]).astype(BF16).astype(F32))
     half = SPAN // 2
     ri = lax.broadcasted_iota(jnp.int32, (half, half), 0)
     ci = lax.broadcasted_iota(jnp.int32, (half, half), 1)
@@ -542,59 +576,97 @@
     high, low = split(local_ref[0] + grown_ref[0, 0:1] * start[...])
     added = mm(jnp.concatenate([cm, cm], axis=1), jnp.concatenate([high, low], axis=0))
     value = ((y_acc[...] + expand(jnp.exp(cum), spread) * added) * gate).astype(BF16)
-    for r in range(reps):
-        @pl.when((block // per) == (lax.rem(me_ref[0], reps) ^ r))
-        def _(r=r):
-            outs[r][pl.ds(pl.multiple_of((block % per) * SPAN, SPAN), SPAN), :] = value
-
-
-def run_outputs(heads, chip, reps, me, normed, xc, bm, cm, cum, step, local, grown, wz, spread, ends, earlier, own):
+    whole = 0
+    for n, r in enumerate(which):
+        if chip or not r:
+            @pl.when(block // per == n)
+            def _(whole=whole):
+                outs[whole][pl.ds(pl.multiple_of((block % per) * SPAN, SPAN), SPAN), :] = value
+            whole += 1
+    for n, r in enumerate(which):
+        if not chip and r:
+            for i in range(len(outs) - whole):
+                @pl.when(block == whole * per + i)
+                def _(i=i):
+                    outs[whole + i][...] = value
+            break
+
+
+def run_outputs(heads, chip, chips, reps, which, me, gate, xc, bm, cm, cum, step, local, grown, wz, spread, enter, own):
     tokens, inner = xc.shape
     state = cm.shape[1]
-    row = lambda n: pl.BlockSpec((SPAN, n), lambda b, me: (b, 0))
-    block3 = lambda b, me: (b, 0, 0)
+    per = own // SPAN
+    gated, opening = wz is None, isinstance(enter, tuple)
+    ends, earlier = enter if opening else ([], [])
+    shapes = []
+    for r in which:
+        shapes += [(own, inner)] if chip or not r else [(SPAN, inner)] * per
+    at = lambda b, me: (lax.rem(me[0], reps) ^ (which[0] + b // per)) * per + b % per
+    row = lambda n: pl.BlockSpec((SPAN, n), lambda b, me: (at(b, me), 0))
+    block3 = lambda b, me: (at(b, me), 0, 0)
+    fixed = lambda shape: pl.BlockSpec(shape, lambda b, me: (0, 0))
+    firsts = [(state, inner)] * chips if opening else []
+    extra = ([] if gated else [wz]) + [spread] + (list(ends) + list(earlier) if opening else [enter])
     return pl.pallas_call(
-        functools.partial(outputs, heads, chip, len(ends), reps),
+        functools.partial(outputs, heads, chip, chips, len(earlier), reps, which, gated, opening),
         grid_spec=pltpu.PrefetchScalarGridSpec(
             num_scalar_prefetch=1,
-            grid=(tokens // SPAN,),
-            in_specs=[row(a.shape[1]) for a in (normed, xc, bm, cm, cum, step)]
+            grid=(len(which) * per,),
+            in_specs=[row(a.shape[1]) for a in (gate, xc, bm, cm, cum, step)]
             + [pl.BlockSpec((1, state, inner), block3), pl.BlockSpec((1, 8, inner), block3)]
-            + [VMEM] * (2 + len(earlier) + len(ends)),
-            out_specs=[pl.BlockSpec((own, inner), lambda b, me: (0, 0))] * reps,
-            scratch_shapes=[pltpu.VMEM((state, inner), F32), pltpu.VMEM((SPAN, inner), F32)],
+            + [VMEM] * len(extra),
+            out_specs=[fixed(shape) for shape in firsts + shapes],
+            scratch_shapes=[pltpu.VMEM((SPAN, inner), F32)],
         ),
-        out_shape=[jax.ShapeDtypeStruct((own, inner), BF16)] * reps,
+        out_shape=[jax.ShapeDtypeStruct(shape, F32) for shape in firsts]
+        + [jax.ShapeDtypeStruct(shape, BF16) for shape in shapes],
         compiler_params=PARAMS,
-        cost_estimate=cost(9 if chip else 0.05),
+        cost_estimate=cost(0.05),
         name="outputs",
-    )(me, normed, xc, bm, cm, cum, step, local, grown, wz, spread, *ends, *earlier)
-
-
-def mix_most(count, me_ref, pat_ref, we_ref, *refs):
-    parts, (norm, weight, embed_ref, mixed_ref, square_ref) = refs[:count], refs[count:]
+    )(me, gate, xc, bm, cm, cum, step, local, grown, *extra)
+
+
+def pick_gains(norm, index, count):
+    values = norm[...].astype(F32)
+    each = values.shape[0] // count
+    gains = None
+    for j in range(count):
+        row = jnp.concatenate([values[j * each + i : j * each + i + 1] for i in range(each)], axis=1)
+        gains = row if gains is None else jnp.where(index == j, row, gains)
+    return gains
+
+
+def mix_most(sizes, share, me_ref, pat_ref, we_ref, *refs):
+    (norm, weight, embed_ref, mixed_ref, square_ref), refs = refs[-5:], refs[:-5]
     step = pl.program_id(0)
+    parts = []
+    for size in sizes:
+        parts.append(refs[:size])
+        refs = refs[size:]
+    count = len(parts)
+    whole = lambda n: jnp.concatenate([p[...] for p in parts[n]], axis=0).astype(F32)
 
     @pl.when(step == 0)
     def _():
         embed_ref[...] = mm(pat_ref[...], we_ref[...]).astype(BF16)
         square = None
-        for part in parts:
-            v = part[...].astype(F32)
+        for n in range(count):
+            v = whole(n)
             square = v * v if square is None else square + v * v
         square_ref[...] = jnp.broadcast_to(jnp.sum(square, axis=-1, keepdims=True), square_ref.shape)
 
+    gains = pick_gains(norm, me_ref[0] ^ step, share)
     for n in range(count):
         @pl.when(step == n)
         def _(n=n):
-            left = (parts[n][...].astype(F32) * norm[...].astype(F32)).astype(BF16)
-            got = mm(left, weight[0])
+            got = mm((whole(n) * gains).astype(BF16), weight[0])
             mixed_ref[...] = got if n == 0 else mixed_ref[...] + got
 
 
-def mix_last(total, me_ref, embed_ref, mixed_ref, square_ref, part_ref, norm, weight, out_ref):
+def mix_last(total, share, me_ref, embed_ref, mixed_ref, square_ref, part_ref, norm, weight, out_ref):
     v = part_ref[...].astype(F32)
-    got = mm((v * norm[...].astype(F32)).astype(BF16), weight[0])
+    gains = pick_gains(norm, me_ref[0] ^ (share - 1), share)
+    got = mm((v * gains).astype(BF16), weight[0])
     square = square_ref[:, 0:1] + jnp.sum(v * v, axis=-1, keepdims=True)
     scale = lax.rsqrt(square * (1.0 / total) + EPSILON)
     out_ref[...] = (embed_ref[...].astype(F32) + scale * (mixed_ref[...] + got)).astype(BF16)
@@ -603,19 +675,22 @@
 def run_mix(me, patches, we, parts, norm_out, w_out):
     share = len(parts)
     count = share - 1
-    own, inner = parts[0].shape
+    parts = [p if isinstance(p, list) else [p] for p in parts]
+    sizes = [len(p) for p in parts[:count]]
+    most = [v for p in parts[:count] for v in p]
+    (final,) = parts[count]
+    own, inner = final.shape
     width = w_out.shape[1]
-    norms = norm_out[None]
+    norms = norm_out.reshape(-1, LANES)
     weights = w_out.reshape(share, inner, width)
     full = pl.BlockSpec((own, width), lambda d, me: (0, 0))
     embed, mixed, square = pl.pallas_call(
-        functools.partial(mix_most, count),
+        functools.partial(mix_most, sizes, share),
         grid_spec=pltpu.PrefetchScalarGridSpec(
             num_scalar_prefetch=1,
             grid=(count,),
-            in_specs=[pl.BlockSpec((own, patches.shape[1]), lambda d, me: (0, 0)), VMEM] + [VMEM] * count
-            + [pl.BlockSpec((1, inner), lambda d, me: (0, me[0] ^ d)),
-               pl.BlockSpec((1, inner, width), lambda d, me: (me[0] ^ d, 0, 0))],
+            in_specs=[pl.BlockSpec((own, patches.shape[1]), lambda d, me: (0, 0)), VMEM] + [VMEM] * (len(most) + 1)
+            + [pl.BlockSpec((1, inner, width), lambda d, me: (me[0] ^ d, 0, 0))],
             out_specs=[full, full, pl.BlockSpec((own, LANES), lambda d, me: (0, 0))],
         ),
         out_shape=[jax.ShapeDtypeStruct((own, width), BF16), jax.ShapeDtypeStruct((own, width), F32),
@@ -623,24 +698,23 @@
         compiler_params=PARAMS,
         cost_estimate=cost(0.05),
         name="mix_most",
-    )(me, patches, we, *parts[:count], norms, weights)
+    )(me, patches, we, *most, norms, weights)
     tile = SPAN
     row = lambda n: pl.BlockSpec((tile, n), lambda i, me: (i, 0))
     return pl.pallas_call(
-        functools.partial(mix_last, share * inner),
+        functools.partial(mix_last, share * inner, share),
         grid_spec=pltpu.PrefetchScalarGridSpec(
             num_scalar_prefetch=1,
             grid=(own // tile,),
             in_specs=[row(width), row(width), row(LANES), row(inner),
-                      pl.BlockSpec((1, inner), lambda i, me: (0, me[0] ^ count)),
-                      pl.BlockSpec((1, inner, width), lambda i, me: (me[0] ^ count, 0, 0))],
+                      VMEM, pl.BlockSpec((1, inner, width), lambda i, me: (me[0] ^ count, 0, 0))],
             out_specs=row(width),
         ),
         out_shape=jax.ShapeDtypeStruct((own, width), BF16),
         compiler_params=PARAMS,
         cost_estimate=cost(3),
         name="mix_last",
-    )(me, embed, mixed, square, parts[count], norms, weights)
+    )(me, embed, mixed, square, final, norms, weights)
 
 
 def swap(value, flip):
@@ -694,21 +768,32 @@
     earlier = [shift(send, d) for d in range(1, lax.axis_size("seq"))]
     parts = [None] * share
     gate = None
+    enter = (ends, earlier)
     for c in list(range(1, chips)) + [0]:
         normed, xc, bm, cm, cum, step, local, grown = done[c]
         if gate is not None:
             normed, gate = lax.optimization_barrier((normed, gate))
-        values = run_outputs(
-            heads, c, reps, me, normed, xc, bm, cm, cum, step, local, grown, w_z, spread, ends, earlier, own
-        )
-        gate = values[0]
+        ahead = run_gate(normed, w_z) if c == 1 else normed
+        values = []
+        for which in ([[r] for r in range(reps)] if c else [list(range(reps))]):
+            got = run_outputs(
+                heads, c, chips, reps, which, me, ahead, xc, bm, cm, cum, step, local, grown,
+                None if c == 1 else w_z, spread, enter if isinstance(enter, tuple) else enter[c], own,
+            )
+            if isinstance(enter, tuple):
+                enter, got = list(got[:chips]), list(got[chips:])
+            values += got
+            if c:
+                ahead, values[-1] = lax.optimization_barrier((ahead, values[-1]))
+        gate = values[-1]
         for r in reversed(range(reps)):
             d = c * reps + r
-            if d == 1:
-                half = own // 2
-                parts[d] = jnp.concatenate([swap(values[r][:half], d), swap(values[r][half:], d)], 0)
+            if c or not r:
+                parts[d] = swap(values[r], d) if d else values[0]
             else:
-                parts[d] = swap(values[r], d) if d else values[r]
+                per = own // SPAN
+                pieces = values[1 + (r - 1) * per : 1 + r * per]
+                parts[d] = [swap(v, d) for v in pieces]
     return run_mix(me, patches, w_embed, parts, norm_out, w_out)
 
 

time: 133 us -> 131 us (0.985)
  the two profiles are of different devices: /device:TPU:25 before, /device:TPU:17 now
where the time goes in v4:
time: 131 us
  Pallas kernels  69.7 us (53%)
  blocking collectives  34.1 us (26%)
  waiting for transfers between devices  14.1 us (11%)
  starting transfers between devices  8.79 us (7%)
  local copies, waits for them, and re-layouts  3.89 us (3%)
    pallas_call x2, Pallas kernels, run_states(): pl.pallas_call(functools.partial(block_states, heads, per, len(pats), len...  25.2 us
    all_to_all x1, blocking collectives, make_patches(): moved = lax.all_to_all(run_second(moved, length), ALL, 0, 0, tiled=True)  17.1 us
    all_to_all x1, blocking collectives, make_patches(): lax.all_to_all(first.reshape(devices, own, pairs, row_block, LANES), ALL,...  17 us
    pallas_call x3, Pallas kernels, run_outputs(): pl.pallas_call(functools.partial(outputs, heads, chip, chips, len(earlier...  16.7 us
    ppermute x3, waiting for transfers between devices, shift(): return lax.ppermute(value, 'seq', [(i, i + by) for i in range(count - by)])  8.64 us
    pallas_call x1, Pallas kernels, run_mix(): pl.pallas_call(functools.partial(mix_most, sizes, share), grid_spec=pltpu...  7.31 us
    pallas_call x1, Pallas kernels, run_first(): pl.pallas_call(functools.partial(first_section, rows_all, length), out_sh...  7.17 us
    ppermute x7, waiting for transfers between devices, swap(): return lax.ppermute(value, HR, [(i, i ^ flip) for i in range(count)])  5.44 us
  transfers between devices with their start and end apart: 10, of which 7 were waited for; matrix products, arithmetic and copies ran while one was open for 0% of the time, Pallas kernels for 27%

profile of v4, /device:TPU:17, one launch (start us, length us, event | category | flops | bytes accessed | tf_op | source)
XLA Modules:
  0.0 130.7 jit_solution(5622237898708634215)
XLA Ops:
  0.0 7.2 %first_section.1 = bf16[32,6,8,128]{3,2,1,0:T(8,128)(2,1)} custom-call(s32[1]{0:T(128)} %bitcast.1.pos, f32[3,16]{1,0:T(4,128)} %bitcast.22, f32[16]{0:T(128)} %phase.1, s32[16]{0:T(128)} %mode.1, s32[16]{0:T(128)} %delay.1, s32[2,16]{1,0:T(2,128)} %bitcast.25, f32[2,32]{1,0:T(2,128)} %constant.35.clone.turn_ref, f32[2,3,32,8,128]{4,3,2,1,0:T(8,128)} %bitcast.19, ...), custom_call_target="tpu_custom_call" | custom-call | flops 7000000000 | bytes 21000000 | tf_op jit(solution)/shard_map/first_section/pallas_call | solution.py:171
  7.2 17.0 %all_to_all.10.z_ref = bf16[16,2,6,8,128]{4,3,2,1,0:T(8,128)(2,1)} all-to-all(bf16[16,2,6,8,128]{4,3,2,1,0:T(8,128)(2,1)} %bitcast.16), channel_id=1, replica_groups=mesh['grp'=2,'seq'=4,'head'=2,'rep'=2] {'seq','head','rep'}, dimensions={0} | all-to-all | bytes 786432 | tf_op jit(solution)/shard_map/all_to_all | solution.py:304
  24.2 2.5 %second_section.1 = bf16[16,13,8,128]{3,2,1,0:T(8,128)(2,1)} custom-call(bf16[16,2,6,8,128]{4,3,2,1,0:T(8,128)(2,1)} %all_to_all.10.z_ref, bf16[256,256]{1,0:T(8,128)(2,1)} %constant.40.clone.high_ref, bf16[256,256]{1,0:T(8,128)(2,1)} %constant.41.clone.low_ref), custom_call_target="tpu_custom_call" | custom-call | flops 3000000000 | bytes 9000000 | tf_op jit(solution)/shard_map/second_section/pallas_call | solution.py:229
  26.7 17.1 %all_to_all.11.x_ref = bf16[16,13,8,128]{3,2,1,0:T(8,128)(2,1)} all-to-all(bf16[16,13,8,128]{3,2,1,0:T(8,128)(2,1)} %second_section.1), channel_id=1, replica_groups=mesh['grp'=2,'seq'=4,'head'=2,'rep'=2] {'seq','head','rep'}, dimensions={0} | all-to-all | bytes 851968 | tf_op jit(solution)/shard_map/all_to_all | solution.py:307
  43.8 2.8 %order_patches.1.refs_0_.refs_2_.pat_ref = bf16[520,384]{1,0:T(8,128)(2,1)} custom-call(bf16[16,13,8,128]{3,2,1,0:T(8,128)(2,1)} %all_to_all.11.x_ref, bf16[2,208,384]{2,1,0:T(8,128)(2,1)} %constant.42.clone.perm_ref, bf16[2,192,384]{2,1,0:T(8,128)(2,1)} %constant.43.clone.rim_ref), custom_call_target="tpu_custom_call" | custom-call | flops 3000000000 | bytes 9000000 | tf_op jit(solution)/shard_map/order_patches/pallas_call | solution.py:279
  46.6 1.0 collective-permute-start
  47.6 1.6 %collective-permute-done.refs_1_ = bf16[520,384]{1,0:T(8,128)(2,1)S(1)} collective-permute-done((bf16[520,384]{1,0:T(8,128)(2,1)}, bf16[520,384]{1,0:T(8,128)(2,1)S(1)}, u32[]{:S(2)}, u32[]{:S(2)}) %collective-permute-start) | collective-permute-done | bytes 399392 | tf_op jit(solution)/shard_map/ppermute | solution.py:722
  49.9 12.5 %block_states.2 = (bf16[1024,1024]{1,0:T(8,128)(2,1)}, bf16[1024,512]{1,0:T(8,128)(2,1)}, bf16[1024,128]{1,0:T(8,128)(2,1)}, bf16[1024,128]{1,0:T(8,128)(2,1)}, ...) custom-call(s32[1]{0:T(128)} %bitcast.me_ref, ...), custom_call_target="tpu_custom_call" | custom-call | flops 12999999488 | bytes 39000000 | tf_op jit(solution)/shard_map/block_states/pallas_call | solution.py:466
  62.9 1.4 %collective-permute-done.2.refs_1_ = bf16[520,384]{1,0:T(8,128)(2,1)S(1)} collective-permute-done((bf16[520,384]{1,0:T(8,128)(2,1)S(1)}, bf16[520,384]{1,0:T(8,128)(2,1)S(1)}, u32[]{:S(2)}, u32[]{:S(2)}) %collective-permute-start.2) | collective-permute-done | bytes 399392 | tf_op jit(solution)/shard_map/ppermute | solution.py:722
  65.0 12.7 %block_states.3 = (bf16[1024,1024]{1,0:T(8,128)(2,1)}, bf16[1024,512]{1,0:T(8,128)(2,1)}, bf16[1024,128]{1,0:T(8,128)(2,1)}, bf16[1024,128]{1,0:T(8,128)(2,1)}, ...) custom-call(s32[1]{0:T(128)} %bitcast.me_ref, ...), custom_call_target="tpu_custom_call" | custom-call | flops 12999999488 | bytes 39000000 | tf_op jit(solution)/shard_map/block_states/pallas_call | solution.py:466
  78.4 1.3 collective-permute-start.4
  79.7 2.7 %collective-permute-start.3 = (bf16[136,512]{1,0:T(8,128)(2,1)}, bf16[136,512]{1,0:T(8,128)(2,1)S(1)}, u32[]{:S(2)}, u32[]{:S(2)}) collective-permute-start(bf16[136,512]{1,0:T(8,128)(2,1)} %get-tuple-element.52), channel_id=1, source_target_pairs={{0,4},{4,8},{8,12},{1,5},{5,9},{9,13},{2,6},{6,10},{10,14},{3,7},{... | collective-permute-start | bytes 417800 | tf_op jit(solution)/shard_map/ppermute | solution.py:727
  82.5 4.0 %gate_tokens.1.normed_ref = bf16[1024,512]{1,0:T(8,128)(2,1)} custom-call(bf16[1024,1024]{1,0:T(8,128)(2,1)} %get-tuple-element.43.normed_ref, bf16[1024,512]{1,0:T(8,128)(2,1)} %refs_0_.3), custom_call_target="tpu_custom_call" | custom-call | flops 4000000000 | bytes 12000000 | tf_op jit(solution)/shard_map/gate_tokens/pallas_call | solution.py:508
  86.5 2.2 %collective-permute-done.4.refs_4_ = bf16[136,512]{1,0:T(8,128)(2,1)S(1)} collective-permute-done((bf16[136,512]{1,0:T(8,128)(2,1)}, bf16[136,512]{1,0:T(8,128)(2,1)S(1)}, u32[]{:S(2)}, u32[]{:S(2)}) %collective-permute-start.4) | collective-permute-done | bytes 139296 | tf_op jit(solution)/shard_map/ppermute | solution.py:727
  88.7 6.4 %collective-permute-done.3.refs_3_ = bf16[136,512]{1,0:T(8,128)(2,1)S(1)} collective-permute-done((bf16[136,512]{1,0:T(8,128)(2,1)}, bf16[136,512]{1,0:T(8,128)(2,1)S(1)}, u32[]{:S(2)}, u32[]{:S(2)}) %collective-permute-start.3) | collective-permute-done | bytes 139296 | tf_op jit(solution)/shard_map/ppermute | solution.py:727
  95.8 5.0 %outputs.3 = (f32[128,512]{1,0:T(8,128)}, f32[128,512]{1,0:T(8,128)}, bf16[512,512]{1,0:T(8,128)(2,1)}) custom-call(s32[1]{0:T(128)} %bitcast.me_ref, bf16[1024,512]{1,0:T(8,128)(2,1)} %gate_tokens.1.normed_ref, bf16[1024,512]{1,0:T(8,128)(2,1)} %get-tuple-element.44.x_ref, bf16[1024,128]{1,0:T(8,128)(2,1)} %get-tuple-element.45.b_ref, ...), custom_call_target="tpu_custom_call" | custom-call | flops 50000000 | bytes 150000 | tf_op jit(solution)/shard_map/outputs/pallas_call | solution.py:610
  100.7 1.2 collective-permute-start.8
  101.9 4.3 %outputs.4 = bf16[512,512]{1,0:T(8,128)(2,1)} custom-call(s32[1]{0:T(128)} %bitcast.me_ref, bf16[1024,512]{1,0:T(8,128)(2,1)} %gate_tokens.1.normed_ref, bf16[1024,512]{1,0:T(8,128)(2,1)} %get-tuple-element.44.x_ref, bf16[1024,128]{1,0:T(8,128)(2,1)} %get-tuple-element.45.b_ref, bf16[1024,128]{1,0:T(8,128)(2,1)} %get-tuple-element.46.c_ref, ...), custom_call_target="tpu_custom_call" | custom-call | flops 50000000 | bytes 150000 | tf_op jit(solution)/shard_map/outputs/pallas_call | solution.py:610
  106.2 1.0 collective-permute-start.9
  107.2 7.4 %outputs.5 = (bf16[512,512]{1,0:T(8,128)(2,1)}, bf16[256,512]{1,0:T(8,128)(2,1)}, bf16[256,512]{1,0:T(8,128)(2,1)}) custom-call(s32[1]{0:T(128)} %bitcast.me_ref, bf16[1024,1024]{1,0:T(8,128)(2,1)} %get-tuple-element.57.normed_ref, bf16[1024,512]{1,0:T(8,128)(2,1)} %get-tuple-element.58.x_ref, bf16[1024,128]{1,0:T(8,128)(2,1)} %get-tuple-element.59.b_ref, ...), custom_call_target="tpu_custom_call" | custom-call | flops 50000000 | bytes 150000 | tf_op jit(solution)/shard_map/outputs/pallas_call | solution.py:610
  115.2 1.2 collective-permute-done.6.refs_1_
  117.7 7.3 %mix_most.1 = (bf16[512,1024]{1,0:T(8,128)(2,1)}, f32[512,1024]{1,0:T(8,128)}, f32[512,128]{1,0:T(8,128)}) custom-call(s32[1]{0:T(128)} %bitcast.me_ref, bf16[520,384]{1,0:T(8,128)(2,1)} %order_patches.1.refs_0_.refs_2_.pat_ref, bf16[384,1024]{1,0:T(8,128)(2,1)} %we_ref.1, bf16[512,512]{1,0:T(8,128)(2,1)} %get-tuple-element.66.refs_0_, ...), custom_call_target="tpu_custom_call" | custom-call | flops 50000000 | bytes 150000 | tf_op jit(solution)/shard_map/mix_most/pallas_call | solution.py:687
  125.0 0.9 collective-permute-done.9.part_ref
  126.7 4.0 %mix_last.1 = bf16[512,1024]{1,0:T(8,128)(2,1)} custom-call(s32[1]{0:T(128)} %bitcast.me_ref, bf16[512,1024]{1,0:T(8,128)(2,1)} %get-tuple-element.70.embed_ref, f32[512,1024]{1,0:T(8,128)} %get-tuple-element.71.mixed_ref, f32[512,128]{1,0:T(8,128)} %get-tuple-element.72.square_ref, bf16[512,512]{1,0:T(8,128)(2,1)} %copy-done.6, bf16[16,128]{1,0:T(8,128)(2,1)} %bitcast.18, ...), custom_call_target="tpu_custom_call" | custom-call | flops 3000000000 | bytes 9000000 | tf_op jit(solution)/shard_map/mix_last/pallas_call | solution.py:704
  (29 shorter events, 5.9 us)
Async XLA Ops:
  46.6 2.6 %collective-permute-start = (bf16[520,384]{1,0:T(8,128)(2,1)}, bf16[520,384]{1,0:T(8,128)(2,1)S(1)}, u32[]{:S(2)}, u32[]{:S(2)}) collective-permute-start(bf16[520,384]{1,0:T(8,128)(2,1)} %order_patches.1.refs_0_.refs_2_.pat_ref), channel_id=1, source_target_pairs={{0,1},{1,0},{2,3},{3,2},{4,5},{5,4},{6,7},{7,6},{8,9},{9,8},{10,11... | collective-permute-start | bytes 1198088 | tf_op jit(solution)/shard_map/ppermute | solution.py:722
  47.6 14.8 %collective-permute-start.1 = (bf16[520,384]{1,0:T(8,128)(2,1)}, bf16[520,384]{1,0:T(8,128)(2,1)S(1)}, u32[]{:S(2)}, u32[]{:S(2)}) collective-permute-start(bf16[520,384]{1,0:T(8,128)(2,1)} %order_patches.1.refs_0_.refs_2_.pat_ref), channel_id=1, source_target_pairs={{0,2},{1,3},{2,0},{3,1},{4,6},{5,7},{6,4},{7,5},{8,10},{9,11},{10,... | collective-permute-start | bytes 1198088 | tf_op jit(solution)/shard_map/ppermute | solution.py:722
  49.2 0.8 copy-start.8
  62.4 1.8 %copy-start.7 = (bf16[520,384]{1,0:T(8,128)(2,1)}, bf16[520,384]{1,0:T(8,128)(2,1)S(1)}, u32[]{:S(2)}) copy-start(bf16[520,384]{1,0:T(8,128)(2,1)S(1)} %collective-permute-done.1.refs_0_.refs_2_) | copy-start | bytes 1198084
  62.4 1.8 %collective-permute-start.2 = (bf16[520,384]{1,0:T(8,128)(2,1)S(1)}, bf16[520,384]{1,0:T(8,128)(2,1)S(1)}, u32[]{:S(2)}, u32[]{:S(2)}) collective-permute-start(bf16[520,384]{1,0:T(8,128)(2,1)S(1)} %collective-permute-done.1.refs_0_.refs_2_), channel_id=1, source_target_pairs={{0,1},{1,0},{2,3},{3,2},{4,5},{5,4},{6,7},{7,6},{8,9},{9,8},{10,11... | collective-permute-start | bytes 1198088 | tf_op jit(solution)/shard_map/ppermute | solution.py:722
  64.2 0.8 copy-start.9
  77.8 8.7 %collective-permute-start.5 = (bf16[136,512]{1,0:T(8,128)(2,1)}, bf16[136,512]{1,0:T(8,128)(2,1)S(1)}, u32[]{:S(2)}, u32[]{:S(2)}) collective-permute-start(bf16[136,512]{1,0:T(8,128)(2,1)} %get-tuple-element.52), channel_id=1, source_target_pairs={{0,12},{1,13},{2,14},{3,15},{16,28},{17,29},{18,30},{19,31}} | collective-permute-start | bytes 417800 | tf_op jit(solution)/shard_map/ppermute | solution.py:727
  78.4 10.3 %collective-permute-start.4 = (bf16[136,512]{1,0:T(8,128)(2,1)}, bf16[136,512]{1,0:T(8,128)(2,1)S(1)}, u32[]{:S(2)}, u32[]{:S(2)}) collective-permute-start(bf16[136,512]{1,0:T(8,128)(2,1)} %get-tuple-element.52), channel_id=1, source_target_pairs={{0,8},{4,12},{1,9},{5,13},{2,10},{6,14},{3,11},{7,15},{16,24},{20,... | collective-permute-start | bytes 417800 | tf_op jit(solution)/shard_map/ppermute | solution.py:727
  79.7 15.4 %collective-permute-start.3 = (bf16[136,512]{1,0:T(8,128)(2,1)}, bf16[136,512]{1,0:T(8,128)(2,1)S(1)}, u32[]{:S(2)}, u32[]{:S(2)}) collective-permute-start(bf16[136,512]{1,0:T(8,128)(2,1)} %get-tuple-element.52), channel_id=1, source_target_pairs={{0,4},{4,8},{8,12},{1,5},{5,9},{9,13},{2,6},{6,10},{10,14},{3,7},{... | collective-permute-start | bytes 417800 | tf_op jit(solution)/shard_map/ppermute | solution.py:727
  86.5 8.6 %copy-start.3 = (bf16[136,512]{1,0:T(8,128)(2,1)}, bf16[136,512]{1,0:T(8,128)(2,1)S(1)}, u32[]{:S(2)}) copy-start(bf16[136,512]{1,0:T(8,128)(2,1)S(1)} %collective-permute-done.5.refs_5_) | copy-start | bytes 417796
  88.7 6.4 %copy-start.4 = (bf16[136,512]{1,0:T(8,128)(2,1)}, bf16[136,512]{1,0:T(8,128)(2,1)S(1)}, u32[]{:S(2)}) copy-start(bf16[136,512]{1,0:T(8,128)(2,1)S(1)} %collective-permute-done.4.refs_4_) | copy-start | bytes 417796
  95.1 0.7 copy-start.5
  100.7 16.1 %collective-permute-start.8 = (bf16[512,512]{1,0:T(8,128)(2,1)}, bf16[512,512]{1,0:T(8,128)(2,1)S(1)}, u32[]{:S(2)}, u32[]{:S(2)}) collective-permute-start(bf16[512,512]{1,0:T(8,128)(2,1)} %get-tuple-element.69), channel_id=1, source_target_pairs={{0,2},{1,3},{2,0},{3,1},{4,6},{5,7},{6,4},{7,5},{8,10},{9,11},{10,... | collective-permute-start | bytes 1572872 | tf_op jit(solution)/shard_map/ppermute | solution.py:722
  106.2 19.6 %collective-permute-start.9 = (bf16[512,512]{1,0:T(8,128)(2,1)}, bf16[512,512]{1,0:T(8,128)(2,1)S(1)}, u32[]{:S(2)}, u32[]{:S(2)}) collective-permute-start(bf16[512,512]{1,0:T(8,128)(2,1)} %outputs.4), channel_id=1, source_target_pairs={{0,3},{1,2},{2,1},{3,0},{4,7},{5,6},{6,5},{7,4},{8,11},{9,10},{10,... | collective-permute-start | bytes 1572872 | tf_op jit(solution)/shard_map/ppermute | solution.py:722
  114.6 1.8 %collective-permute-start.6 = (bf16[256,512]{1,0:T(8,128)(2,1)}, bf16[256,512]{1,0:T(8,128)(2,1)S(1)}, u32[]{:S(2)}, u32[]{:S(2)}) collective-permute-start(bf16[256,512]{1,0:T(8,128)(2,1)} %get-tuple-element.67), channel_id=1, source_target_pairs={{0,1},{1,0},{2,3},{3,2},{4,5},{5,4},{6,7},{7,6},{8,9},{9,8},{10,11... | collective-permute-start | bytes 786440 | tf_op jit(solution)/shard_map/ppermute | solution.py:722
  114.7 2.1 %collective-permute-start.7 = (bf16[256,512]{1,0:T(8,128)(2,1)}, bf16[256,512]{1,0:T(8,128)(2,1)S(1)}, u32[]{:S(2)}, u32[]{:S(2)}) collective-permute-start(bf16[256,512]{1,0:T(8,128)(2,1)} %get-tuple-element.68), channel_id=1, source_target_pairs={{0,1},{1,0},{2,3},{3,2},{4,5},{5,4},{6,7},{7,6},{8,9},{9,8},{10,11... | collective-permute-start | bytes 786440 | tf_op jit(solution)/shard_map/ppermute | solution.py:722
  116.4 0.7 copy-start.1
  116.8 0.7 copy-start.2
  116.8 0.9 copy-start
  125.9 0.8 copy-start.6

commit v5 on v4

--- a/solution.py
+++ b/solution.py
@@ -91,37 +91,85 @@
     first_bin = row + rows_all * lane
     unit = 2.0 * math.pi / length
 
-    def make_base(s, _):
-        turn = ((((first_bin * delay[s]) & (length - 1)) * mode[s]) & (length - 1)).astype(F32)
-        angle = mode[s].astype(F32) * phase[s] + turn * unit
-        base[0, s] = jnp.cos(angle)
-        base[1, s] = jnp.sin(angle)
+    group = math.gcd(sources, 4)
+
+    def make_base(g, _):
+        for n in range(group):
+            s = g * group + n
+            turn = ((((first_bin * delay[s]) & (length - 1)) * mode[s]) & (length - 1)).astype(F32)
+            angle = mode[s].astype(F32) * phase[s] + turn * unit
+            base[pl.ds(pl.multiple_of(s * row_block, row_block), row_block), :] = jnp.cos(angle)
+            base[pl.ds(pl.multiple_of((sources + s) * row_block, row_block), row_block), :] = jnp.sin(angle)
         return 0
 
-    lax.fori_loop(0, sources, make_base, 0)
-
-    def add_sources(v, _):
-        here = first_bin + (rows_all * LANES) * v
-        total = [x_ref[r, c, v] for r in range(2) for c in range(channels)]
+    lax.fori_loop(0, sources // group, make_base, 0)
+
+    width = rows_all * LANES
+    high_bits = lax.broadcasted_iota(jnp.int32, (inner, LANES), 0)
+    place = lax.broadcasted_iota(jnp.int32, (1, LANES), 1)
+
+    def spread_out(value, kind):
+        out = jnp.zeros((1, LANES), kind)
         for s in range(sources):
-            which = (delay[s] * mode[s] * v) & (inner - 1)
-            tr, ti = turn_ref[0, which], turn_ref[1, which]
-            inside = (here >= bins[0, s]) & (here < bins[1, s])
-            br, bi = base[0, s], base[1, s]
-            real = jnp.where(inside, br * tr - bi * ti, 0.0)
-            imag = jnp.where(inside, br * ti + bi * tr, 0.0)
-            for c in range(channels):
-                total[c] = total[c] + amp[c, s] * real
-                total[channels + c] = total[channels + c] + amp[c, s] * imag
-        for n in range(2 * channels):
-            acc[n, v] = total[n]
+            out = jnp.where(place == s, value(s), out)
+        return out
+
+    lag = spread_out(lambda s: delay[s] * mode[s], jnp.int32)
+    low_end = spread_out(lambda s: bins[0, s], jnp.int32)
+    high_end = spread_out(lambda s: bins[1, s], jnp.int32)
+    step_angle = ((lag * high_bits) & (inner - 1)).astype(F32) * (2.0 * math.pi / inner)
+    known = lax.broadcasted_iota(jnp.int32, (inner, LANES), 1) < sources
+    full = known & (low_end <= high_bits * width) & (high_end >= (high_bits + 1) * width)
+    step_cos = jnp.where(full, jnp.cos(step_angle), 0.0)
+    step_sin = jnp.where(full, jnp.sin(step_angle), 0.0)
+    rows = []
+    for r in range(2):
+        one, two = (step_cos, -step_sin) if r == 0 else (step_sin, step_cos)
+        for c in range(channels):
+            gain = spread_out(lambda s: amp[c, s], F32)
+            rows.append(gain * one + pltpu.roll(gain * two, sources, 1))
+    rows = jnp.concatenate(rows, axis=0)
+    top = rows.astype(BF16).astype(F32)
+    rest = (rows - top).astype(BF16).astype(F32)
+    left = (top + pltpu.roll(top, 2 * sources, 1) + pltpu.roll(rest, 4 * sources, 1)).astype(BF16)
+    blank = jnp.zeros((LANES - 6 * sources, LANES), F32)
+    for u in range(row_block):
+        wave = base[pl.ds(u, 2 * sources, stride=row_block), :]
+        top = wave.astype(BF16).astype(F32)
+        right = jnp.concatenate([top, wave - top, top, blank], axis=0).astype(BF16)
+        acc[pl.ds(u, 2 * channels * inner, stride=row_block), :] = mm(left, right)
+
+    def add_ends(s, _):
+        first, past = bins[0, s], bins[1, s]
+        at_first, at_past = lax.div(first, width), lax.div(past, width)
+        begins = (first > at_first * width) | (past < (at_first + 1) * width)
+        ends = (at_past != at_first) & (at_past < inner)
+        for at, wanted in ((at_first, begins), (at_past, ends)):
+            @pl.when(wanted)
+            def _(at=at):
+                here = first_bin + width * at
+                which = (delay[s] * mode[s] * at) & (inner - 1)
+                tr, ti = turn_ref[0, which], turn_ref[1, which]
+                inside = (here >= first) & (here < past)
+                br = base[pl.ds(pl.multiple_of(s * row_block, row_block), row_block), :]
+                bi = base[pl.ds(pl.multiple_of((sources + s) * row_block, row_block), row_block), :]
+                real = jnp.where(inside, br * tr - bi * ti, 0.0)
+                imag = jnp.where(inside, br * ti + bi * tr, 0.0)
+                for c in range(channels):
+                    for n, part in ((c, real), (channels + c, imag)):
+                        slot = pl.ds(pl.multiple_of((n * inner + at) * row_block, row_block), row_block)
+                        acc[slot, :] = acc[slot, :] + amp[c, s] * part
         return 0
 
-    lax.fori_loop(0, inner, add_sources, 0)
+    lax.fori_loop(0, sources, add_ends, 0)
+
+    def total(r, c, v):
+        slot = pl.multiple_of(((r * channels + c) * inner + v) * row_block, row_block)
+        return x_ref[r, c, v] + acc[pl.ds(slot, row_block), :]
 
     def transform(c, _):
         real, imag = inverse_fft(
-            [acc[c, v] for v in range(inner)], [acc[channels + c, v] for v in range(inner)]
+            [total(0, c, v) for v in range(inner)], [total(1, c, v) for v in range(inner)]
         )
         for q in range(inner):
             tc, ts = twist_ref[0, q : q + 1, :], twist_ref[1, q : q + 1, :]
@@ -174,8 +222,8 @@
         in_specs=[SMEM] * 7 + [VMEM] * 5,
         out_specs=VMEM,
         scratch_shapes=[
-            pltpu.VMEM((2, amp.shape[0], row_block, LANES), F32),
-            pltpu.VMEM((2 * channels, inner, row_block, LANES), F32),
+            pltpu.VMEM((2 * amp.shape[0] * row_block, LANES), F32),
+            pltpu.VMEM((2 * channels * inner * row_block, LANES), F32),
             pltpu.VMEM((channels, inner, row_block, 2 * LANES), F32),
         ],
         compiler_params=PARAMS,
@@ -377,7 +425,8 @@
     def _():
         carried[...] = jnp.zeros_like(carried)
         total[...] = jnp.zeros_like(total)
-        tail[...] = halo[...].astype(F32)
+        tail[...] = jnp.zeros_like(tail)
+        tail[8:16] = halo[...].astype(F32)
         ri = lax.broadcasted_iota(jnp.int32, (SPAN, SPAN), 0)
         ci = lax.broadcasted_iota(jnp.int32, (SPAN, SPAN), 1)
         low_tri[...] = jnp.where(ri >= ci, 1.0, 0.0).astype(BF16)
@@ -390,8 +439,8 @@
     span = pats[0].shape[0]
     patch = jnp.where(here, pats[0][...], pats[1][...]).astype(F32)
     joined = features(jnp.concatenate([tail[...], patch], axis=0).astype(BF16))
-    tail[...] = patch[span - 8 :]
-    normed = joined[8:]
+    tail[...] = patch[span - 16 :]
+    normed = joined[16:]
     normed_ref[...] = normed
     dts[:, 0:heads] = lax.dot_general(
         normed, wdt[...], (((1,), (1,)), ((), ())), preferred_element_type=F32
@@ -403,9 +452,9 @@
     step_ref[...] = step_all
 
     def conv(buffer, kernel, at):
-        out = kernel[0:1] * buffer[at + 9 - taps : at + 9 - taps + SPAN]
+        out = kernel[0:1] * buffer[at + 17 - taps : at + 17 - taps + SPAN]
         for i in range(1, taps):
-            out = out + kernel[i : i + 1] * buffer[at + 9 - taps + i : at + 9 - taps + i + SPAN]
+            out = out + kernel[i : i + 1] * buffer[at + 17 - taps + i : at + 17 - taps + i + SPAN]
         return silu(out)
 
     for n in range(span // SPAN):
@@ -476,14 +525,14 @@
                        pl.BlockSpec((subs, 8, inner), lambda b, me: (b, 0, 0)), fixed]
             + [fixed] * final,
             scratch_shapes=[
-                pltpu.VMEM((span + 8, inner), F32),
-                pltpu.VMEM((span + 8, 2 * state), F32),
+                pltpu.VMEM((span + 16, inner), F32),
+                pltpu.VMEM((span + 16, 2 * state), F32),
                 pltpu.VMEM((state, inner), F32),
                 pltpu.VMEM((8, LANES), F32),
                 pltpu.VMEM((SPAN, SPAN), BF16),
                 pltpu.VMEM((span, LANES), F32),
                 pltpu.VMEM((8, LANES), F32),
-                pltpu.VMEM((8, width), F32),
+                pltpu.VMEM((16, width), F32),
             ],
         ),
         out_shape=[

time: 131 us -> 128 us (0.977)
  Pallas kernels: 69.7 us -> 66.9 us
    pallas_call x1, Pallas kernels: 7.17 us -> 4.54 us  [run_first(): pl.pallas_call(functools.partial(first_section, rows_all, length), out_sh...]
  transfers between devices with their start and end apart: 10 -> 10, of which waited for: 7 -> 7; matrix products, arithmetic and copies ran while one was open for 0% -> 0% of each run, Pallas kernels for 27% -> 28%
where the time goes in v5:
time: 128 us
  Pallas kernels  66.9 us (52%)
  blocking collectives  34.1 us (27%)
  waiting for transfers between devices  14.1 us (11%)
  starting transfers between devices  8.81 us (7%)
  local copies, waits for them, and re-layouts  3.89 us (3%)
    pallas_call x2, Pallas kernels, run_states(): pl.pallas_call(functools.partial(block_states, heads, per, len(pats), len...  24.9 us
    all_to_all x1, blocking collectives, make_patches(): moved = lax.all_to_all(run_second(moved, length), ALL, 0, 0, tiled=True)  17.1 us
    all_to_all x1, blocking collectives, make_patches(): lax.all_to_all(first.reshape(devices, own, pairs, row_block, LANES), ALL,...  17 us
    pallas_call x3, Pallas kernels, run_outputs(): pl.pallas_call(functools.partial(outputs, heads, chip, chips, len(earlier...  16.7 us
    ppermute x3, waiting for transfers between devices, shift(): return lax.ppermute(value, 'seq', [(i, i + by) for i in range(count - by)])  8.64 us
    pallas_call x1, Pallas kernels, run_mix(): pl.pallas_call(functools.partial(mix_most, sizes, share), grid_spec=pltpu...  7.31 us
    ppermute x7, waiting for transfers between devices, swap(): return lax.ppermute(value, HR, [(i, i ^ flip) for i in range(count)])  5.42 us
    ppermute x3, starting transfers between devices, shift(): return lax.ppermute(value, 'seq', [(i, i + by) for i in range(count - by)])  4.68 us
  transfers between devices with their start and end apart: 10, of which 7 were waited for; matrix products, arithmetic and copies ran while one was open for 0% of the time, Pallas kernels for 28%

profile of v5, /device:TPU:17, one launch (start us, length us, event | category | flops | bytes accessed | tf_op | source)
XLA Modules:
  0.0 127.8 jit_solution(1020379406598574727)
XLA Ops:
  0.0 4.5 %first_section.1 = bf16[32,6,8,128]{3,2,1,0:T(8,128)(2,1)} custom-call(s32[1]{0:T(128)} %bitcast.1.pos, f32[3,16]{1,0:T(4,128)} %bitcast.22, f32[16]{0:T(128)} %phase.1, s32[16]{0:T(128)} %mode.1, s32[16]{0:T(128)} %delay.1, s32[2,16]{1,0:T(2,128)} %bitcast.25, f32[2,32]{1,0:T(2,128)} %constant.35.clone.turn_ref, f32[2,3,32,8,128]{4,3,2,1,0:T(8,128)} %bitcast.19, ...), custom_call_target="tpu_custom_call" | custom-call | flops 7000000000 | bytes 21000000 | tf_op jit(solution)/shard_map/first_section/pallas_call | solution.py:219
  4.5 17.0 %all_to_all.10.z_ref = bf16[16,2,6,8,128]{4,3,2,1,0:T(8,128)(2,1)} all-to-all(bf16[16,2,6,8,128]{4,3,2,1,0:T(8,128)(2,1)} %bitcast.16), channel_id=1, replica_groups=mesh['grp'=2,'seq'=4,'head'=2,'rep'=2] {'seq','head','rep'}, dimensions={0} | all-to-all | bytes 786432 | tf_op jit(solution)/shard_map/all_to_all | solution.py:352
  21.6 2.5 %second_section.1 = bf16[16,13,8,128]{3,2,1,0:T(8,128)(2,1)} custom-call(bf16[16,2,6,8,128]{4,3,2,1,0:T(8,128)(2,1)} %all_to_all.10.z_ref, bf16[256,256]{1,0:T(8,128)(2,1)} %constant.40.clone.high_ref, bf16[256,256]{1,0:T(8,128)(2,1)} %constant.41.clone.low_ref), custom_call_target="tpu_custom_call" | custom-call | flops 3000000000 | bytes 9000000 | tf_op jit(solution)/shard_map/second_section/pallas_call | solution.py:277
  24.0 17.1 %all_to_all.11.x_ref = bf16[16,13,8,128]{3,2,1,0:T(8,128)(2,1)} all-to-all(bf16[16,13,8,128]{3,2,1,0:T(8,128)(2,1)} %second_section.1), channel_id=1, replica_groups=mesh['grp'=2,'seq'=4,'head'=2,'rep'=2] {'seq','head','rep'}, dimensions={0} | all-to-all | bytes 851968 | tf_op jit(solution)/shard_map/all_to_all | solution.py:355
  41.1 2.8 %order_patches.1.refs_0_.refs_2_.pat_ref = bf16[520,384]{1,0:T(8,128)(2,1)} custom-call(bf16[16,13,8,128]{3,2,1,0:T(8,128)(2,1)} %all_to_all.11.x_ref, bf16[2,208,384]{2,1,0:T(8,128)(2,1)} %constant.42.clone.perm_ref, bf16[2,192,384]{2,1,0:T(8,128)(2,1)} %constant.43.clone.rim_ref), custom_call_target="tpu_custom_call" | custom-call | flops 3000000000 | bytes 9000000 | tf_op jit(solution)/shard_map/order_patches/pallas_call | solution.py:327
  44.0 1.0 collective-permute-start
  45.0 1.6 %collective-permute-done.refs_1_ = bf16[520,384]{1,0:T(8,128)(2,1)S(1)} collective-permute-done((bf16[520,384]{1,0:T(8,128)(2,1)}, bf16[520,384]{1,0:T(8,128)(2,1)S(1)}, u32[]{:S(2)}, u32[]{:S(2)}) %collective-permute-start) | collective-permute-done | bytes 399392 | tf_op jit(solution)/shard_map/ppermute | solution.py:771
  47.3 12.3 %block_states.2 = (bf16[1024,1024]{1,0:T(8,128)(2,1)}, bf16[1024,512]{1,0:T(8,128)(2,1)}, bf16[1024,128]{1,0:T(8,128)(2,1)}, bf16[1024,128]{1,0:T(8,128)(2,1)}, ...) custom-call(s32[1]{0:T(128)} %bitcast.me_ref, ...), custom_call_target="tpu_custom_call" | custom-call | flops 12999999488 | bytes 39000000 | tf_op jit(solution)/shard_map/block_states/pallas_call | solution.py:515
  60.1 1.4 %collective-permute-done.2.refs_1_ = bf16[520,384]{1,0:T(8,128)(2,1)S(1)} collective-permute-done((bf16[520,384]{1,0:T(8,128)(2,1)S(1)}, bf16[520,384]{1,0:T(8,128)(2,1)S(1)}, u32[]{:S(2)}, u32[]{:S(2)}) %collective-permute-start.2) | collective-permute-done | bytes 399392 | tf_op jit(solution)/shard_map/ppermute | solution.py:771
  62.2 12.6 %block_states.3 = (bf16[1024,1024]{1,0:T(8,128)(2,1)}, bf16[1024,512]{1,0:T(8,128)(2,1)}, bf16[1024,128]{1,0:T(8,128)(2,1)}, bf16[1024,128]{1,0:T(8,128)(2,1)}, ...) custom-call(s32[1]{0:T(128)} %bitcast.me_ref, ...), custom_call_target="tpu_custom_call" | custom-call | flops 12999999488 | bytes 39000000 | tf_op jit(solution)/shard_map/block_states/pallas_call | solution.py:515
  75.5 1.3 %collective-permute-start.4 = (bf16[136,512]{1,0:T(8,128)(2,1)}, bf16[136,512]{1,0:T(8,128)(2,1)S(1)}, u32[]{:S(2)}, u32[]{:S(2)}) collective-permute-start(bf16[136,512]{1,0:T(8,128)(2,1)} %get-tuple-element.52), channel_id=1, source_target_pairs={{0,8},{4,12},{1,9},{5,13},{2,10},{6,14},{3,11},{7,15},{16,24},{20,... | collective-permute-start | bytes 417800 | tf_op jit(solution)/shard_map/ppermute | solution.py:776
  76.8 2.7 %collective-permute-start.3 = (bf16[136,512]{1,0:T(8,128)(2,1)}, bf16[136,512]{1,0:T(8,128)(2,1)S(1)}, u32[]{:S(2)}, u32[]{:S(2)}) collective-permute-start(bf16[136,512]{1,0:T(8,128)(2,1)} %get-tuple-element.52), channel_id=1, source_target_pairs={{0,4},{4,8},{8,12},{1,5},{5,9},{9,13},{2,6},{6,10},{10,14},{3,7},{... | collective-permute-start | bytes 417800 | tf_op jit(solution)/shard_map/ppermute | solution.py:776
  79.6 4.0 %gate_tokens.1.normed_ref = bf16[1024,512]{1,0:T(8,128)(2,1)} custom-call(bf16[1024,1024]{1,0:T(8,128)(2,1)} %get-tuple-element.43.normed_ref, bf16[1024,512]{1,0:T(8,128)(2,1)} %refs_0_.3), custom_call_target="tpu_custom_call" | custom-call | flops 4000000000 | bytes 12000000 | tf_op jit(solution)/shard_map/gate_tokens/pallas_call | solution.py:557
  83.6 2.2 %collective-permute-done.4.refs_4_ = bf16[136,512]{1,0:T(8,128)(2,1)S(1)} collective-permute-done((bf16[136,512]{1,0:T(8,128)(2,1)}, bf16[136,512]{1,0:T(8,128)(2,1)S(1)}, u32[]{:S(2)}, u32[]{:S(2)}) %collective-permute-start.4) | collective-permute-done | bytes 139296 | tf_op jit(solution)/shard_map/ppermute | solution.py:776
  85.8 6.4 %collective-permute-done.3.refs_3_ = bf16[136,512]{1,0:T(8,128)(2,1)S(1)} collective-permute-done((bf16[136,512]{1,0:T(8,128)(2,1)}, bf16[136,512]{1,0:T(8,128)(2,1)S(1)}, u32[]{:S(2)}, u32[]{:S(2)}) %collective-permute-start.3) | collective-permute-done | bytes 139296 | tf_op jit(solution)/shard_map/ppermute | solution.py:776
  92.9 5.0 %outputs.3 = (f32[128,512]{1,0:T(8,128)}, f32[128,512]{1,0:T(8,128)}, bf16[512,512]{1,0:T(8,128)(2,1)}) custom-call(s32[1]{0:T(128)} %bitcast.me_ref, bf16[1024,512]{1,0:T(8,128)(2,1)} %gate_tokens.1.normed_ref, bf16[1024,512]{1,0:T(8,128)(2,1)} %get-tuple-element.44.x_ref, bf16[1024,128]{1,0:T(8,128)(2,1)} %get-tuple-element.45.b_ref, ...), custom_call_target="tpu_custom_call" | custom-call | flops 50000000 | bytes 150000 | tf_op jit(solution)/shard_map/outputs/pallas_call | solution.py:659
  97.8 1.2 collective-permute-start.8
  99.0 4.3 %outputs.4 = bf16[512,512]{1,0:T(8,128)(2,1)} custom-call(s32[1]{0:T(128)} %bitcast.me_ref, bf16[1024,512]{1,0:T(8,128)(2,1)} %gate_tokens.1.normed_ref, bf16[1024,512]{1,0:T(8,128)(2,1)} %get-tuple-element.44.x_ref, bf16[1024,128]{1,0:T(8,128)(2,1)} %get-tuple-element.45.b_ref, bf16[1024,128]{1,0:T(8,128)(2,1)} %get-tuple-element.46.c_ref, ...), custom_call_target="tpu_custom_call" | custom-call | flops 50000000 | bytes 150000 | tf_op jit(solution)/shard_map/outputs/pallas_call | solution.py:659
  103.3 1.0 collective-permute-start.9
  104.3 7.4 %outputs.5 = (bf16[512,512]{1,0:T(8,128)(2,1)}, bf16[256,512]{1,0:T(8,128)(2,1)}, bf16[256,512]{1,0:T(8,128)(2,1)}) custom-call(s32[1]{0:T(128)} %bitcast.me_ref, bf16[1024,1024]{1,0:T(8,128)(2,1)} %get-tuple-element.57.normed_ref, bf16[1024,512]{1,0:T(8,128)(2,1)} %get-tuple-element.58.x_ref, bf16[1024,128]{1,0:T(8,128)(2,1)} %get-tuple-element.59.b_ref, ...), custom_call_target="tpu_custom_call" | custom-call | flops 50000000 | bytes 150000 | tf_op jit(solution)/shard_map/outputs/pallas_call | solution.py:659
  112.3 1.2 collective-permute-done.6.refs_1_
  114.8 7.3 %mix_most.1 = (bf16[512,1024]{1,0:T(8,128)(2,1)}, f32[512,1024]{1,0:T(8,128)}, f32[512,128]{1,0:T(8,128)}) custom-call(s32[1]{0:T(128)} %bitcast.me_ref, bf16[520,384]{1,0:T(8,128)(2,1)} %order_patches.1.refs_0_.refs_2_.pat_ref, bf16[384,1024]{1,0:T(8,128)(2,1)} %we_ref.1, bf16[512,512]{1,0:T(8,128)(2,1)} %get-tuple-element.66.refs_0_, ...), custom_call_target="tpu_custom_call" | custom-call | flops 50000000 | bytes 150000 | tf_op jit(solution)/shard_map/mix_most/pallas_call | solution.py:736
  122.1 0.9 collective-permute-done.9.part_ref
  123.8 4.0 %mix_last.1 = bf16[512,1024]{1,0:T(8,128)(2,1)} custom-call(s32[1]{0:T(128)} %bitcast.me_ref, bf16[512,1024]{1,0:T(8,128)(2,1)} %get-tuple-element.70.embed_ref, f32[512,1024]{1,0:T(8,128)} %get-tuple-element.71.mixed_ref, f32[512,128]{1,0:T(8,128)} %get-tuple-element.72.square_ref, bf16[512,512]{1,0:T(8,128)(2,1)} %copy-done.6, bf16[16,128]{1,0:T(8,128)(2,1)} %bitcast.18, ...), custom_call_target="tpu_custom_call" | custom-call | flops 3000000000 | bytes 9000000 | tf_op jit(solution)/shard_map/mix_last/pallas_call | solution.py:753
  (29 shorter events, 5.9 us)
Async XLA Ops:
  44.0 2.6 %collective-permute-start = (bf16[520,384]{1,0:T(8,128)(2,1)}, bf16[520,384]{1,0:T(8,128)(2,1)S(1)}, u32[]{:S(2)}, u32[]{:S(2)}) collective-permute-start(bf16[520,384]{1,0:T(8,128)(2,1)} %order_patches.1.refs_0_.refs_2_.pat_ref), channel_id=1, source_target_pairs={{0,1},{1,0},{2,3},{3,2},{4,5},{5,4},{6,7},{7,6},{8,9},{9,8},{10,11... | collective-permute-start | bytes 1198088 | tf_op jit(solution)/shard_map/ppermute | solution.py:771
  45.0 14.7 %collective-permute-start.1 = (bf16[520,384]{1,0:T(8,128)(2,1)}, bf16[520,384]{1,0:T(8,128)(2,1)S(1)}, u32[]{:S(2)}, u32[]{:S(2)}) collective-permute-start(bf16[520,384]{1,0:T(8,128)(2,1)} %order_patches.1.refs_0_.refs_2_.pat_ref), channel_id=1, source_target_pairs={{0,2},{1,3},{2,0},{3,1},{4,6},{5,7},{6,4},{7,5},{8,10},{9,11},{10,... | collective-permute-start | bytes 1198088 | tf_op jit(solution)/shard_map/ppermute | solution.py:771
  46.5 0.8 copy-start.8
  59.6 1.8 %copy-start.7 = (bf16[520,384]{1,0:T(8,128)(2,1)}, bf16[520,384]{1,0:T(8,128)(2,1)S(1)}, u32[]{:S(2)}) copy-start(bf16[520,384]{1,0:T(8,128)(2,1)S(1)} %collective-permute-done.1.refs_0_.refs_2_) | copy-start | bytes 1198084
  59.6 1.8 %collective-permute-start.2 = (bf16[520,384]{1,0:T(8,128)(2,1)S(1)}, bf16[520,384]{1,0:T(8,128)(2,1)S(1)}, u32[]{:S(2)}, u32[]{:S(2)}) collective-permute-start(bf16[520,384]{1,0:T(8,128)(2,1)S(1)} %collective-permute-done.1.refs_0_.refs_2_), channel_id=1, source_target_pairs={{0,1},{1,0},{2,3},{3,2},{4,5},{5,4},{6,7},{7,6},{8,9},{9,8},{10,11... | collective-permute-start | bytes 1198088 | tf_op jit(solution)/shard_map/ppermute | solution.py:771
  61.5 0.8 copy-start.9
  74.9 8.7 %collective-permute-start.5 = (bf16[136,512]{1,0:T(8,128)(2,1)}, bf16[136,512]{1,0:T(8,128)(2,1)S(1)}, u32[]{:S(2)}, u32[]{:S(2)}) collective-permute-start(bf16[136,512]{1,0:T(8,128)(2,1)} %get-tuple-element.52), channel_id=1, source_target_pairs={{0,12},{1,13},{2,14},{3,15},{16,28},{17,29},{18,30},{19,31}} | collective-permute-start | bytes 417800 | tf_op jit(solution)/shard_map/ppermute | solution.py:776
  75.5 10.2 %collective-permute-start.4 = (bf16[136,512]{1,0:T(8,128)(2,1)}, bf16[136,512]{1,0:T(8,128)(2,1)S(1)}, u32[]{:S(2)}, u32[]{:S(2)}) collective-permute-start(bf16[136,512]{1,0:T(8,128)(2,1)} %get-tuple-element.52), channel_id=1, source_target_pairs={{0,8},{4,12},{1,9},{5,13},{2,10},{6,14},{3,11},{7,15},{16,24},{20,... | collective-permute-start | bytes 417800 | tf_op jit(solution)/shard_map/ppermute | solution.py:776
  76.8 15.4 %collective-permute-start.3 = (bf16[136,512]{1,0:T(8,128)(2,1)}, bf16[136,512]{1,0:T(8,128)(2,1)S(1)}, u32[]{:S(2)}, u32[]{:S(2)}) collective-permute-start(bf16[136,512]{1,0:T(8,128)(2,1)} %get-tuple-element.52), channel_id=1, source_target_pairs={{0,4},{4,8},{8,12},{1,5},{5,9},{9,13},{2,6},{6,10},{10,14},{3,7},{... | collective-permute-start | bytes 417800 | tf_op jit(solution)/shard_map/ppermute | solution.py:776
  83.6 8.6 %copy-start.3 = (bf16[136,512]{1,0:T(8,128)(2,1)}, bf16[136,512]{1,0:T(8,128)(2,1)S(1)}, u32[]{:S(2)}) copy-start(bf16[136,512]{1,0:T(8,128)(2,1)S(1)} %collective-permute-done.5.refs_5_) | copy-start | bytes 417796
  85.8 6.4 %copy-start.4 = (bf16[136,512]{1,0:T(8,128)(2,1)}, bf16[136,512]{1,0:T(8,128)(2,1)S(1)}, u32[]{:S(2)}) copy-start(bf16[136,512]{1,0:T(8,128)(2,1)S(1)} %collective-permute-done.4.refs_4_) | copy-start | bytes 417796
  92.2 0.7 copy-start.5
  97.8 16.1 %collective-permute-start.8 = (bf16[512,512]{1,0:T(8,128)(2,1)}, bf16[512,512]{1,0:T(8,128)(2,1)S(1)}, u32[]{:S(2)}, u32[]{:S(2)}) collective-permute-start(bf16[512,512]{1,0:T(8,128)(2,1)} %get-tuple-element.69), channel_id=1, source_target_pairs={{0,2},{1,3},{2,0},{3,1},{4,6},{5,7},{6,4},{7,5},{8,10},{9,11},{10,... | collective-permute-start | bytes 1572872 | tf_op jit(solution)/shard_map/ppermute | solution.py:771
  103.3 19.6 %collective-permute-start.9 = (bf16[512,512]{1,0:T(8,128)(2,1)}, bf16[512,512]{1,0:T(8,128)(2,1)S(1)}, u32[]{:S(2)}, u32[]{:S(2)}) collective-permute-start(bf16[512,512]{1,0:T(8,128)(2,1)} %outputs.4), channel_id=1, source_target_pairs={{0,3},{1,2},{2,1},{3,0},{4,7},{5,6},{6,5},{7,4},{8,11},{9,10},{10,... | collective-permute-start | bytes 1572872 | tf_op jit(solution)/shard_map/ppermute | solution.py:771
  111.8 1.8 %collective-permute-start.6 = (bf16[256,512]{1,0:T(8,128)(2,1)}, bf16[256,512]{1,0:T(8,128)(2,1)S(1)}, u32[]{:S(2)}, u32[]{:S(2)}) collective-permute-start(bf16[256,512]{1,0:T(8,128)(2,1)} %get-tuple-element.67), channel_id=1, source_target_pairs={{0,1},{1,0},{2,3},{3,2},{4,5},{5,4},{6,7},{7,6},{8,9},{9,8},{10,11... | collective-permute-start | bytes 786440 | tf_op jit(solution)/shard_map/ppermute | solution.py:771
  111.8 2.1 %collective-permute-start.7 = (bf16[256,512]{1,0:T(8,128)(2,1)}, bf16[256,512]{1,0:T(8,128)(2,1)S(1)}, u32[]{:S(2)}, u32[]{:S(2)}) collective-permute-start(bf16[256,512]{1,0:T(8,128)(2,1)} %get-tuple-element.68), channel_id=1, source_target_pairs={{0,1},{1,0},{2,3},{3,2},{4,5},{5,4},{6,7},{7,6},{8,9},{9,8},{10,11... | collective-permute-start | bytes 786440 | tf_op jit(solution)/shard_map/ppermute | solution.py:771
  113.5 0.7 copy-start.1
  113.9 0.7 copy-start.2
  113.9 0.9 copy-start
  123.0 0.8 copy-start.6

commit v6 on v5

--- a/solution.py
+++ b/solution.py
@@ -546,24 +546,31 @@
     )(me, *pats, halo, *consts, *earlier)
 
 
-def gate_tokens(normed_ref, wz, gate_ref):
+def gate_tokens(normed_ref, wz, pat_ref, we, gate_ref, embed_ref):
+    @pl.when(pl.program_id(0) == 0)
+    def _():
+        embed_ref[...] = mm(pat_ref[...], we[...]).astype(BF16)
+
     gate_ref[...] = silu(mm(normed_ref[...], wz[...]).astype(BF16).astype(F32)).astype(BF16)
 
 
-def run_gate(normed, wz):
+def run_gate(normed, wz, patches, we, own):
     tokens, width = normed.shape
     inner = wz.shape[1]
     span = min(tokens, TILE)
     return pl.pallas_call(
         gate_tokens,
         grid=(tokens // span,),
-        in_specs=[pl.BlockSpec((span, width), lambda b: (b, 0)), VMEM],
-        out_specs=pl.BlockSpec((span, inner), lambda b: (b, 0)),
-        out_shape=jax.ShapeDtypeStruct((tokens, inner), BF16),
+        in_specs=[pl.BlockSpec((span, width), lambda b: (b, 0)), VMEM,
+                  pl.BlockSpec((own, patches.shape[1]), lambda b: (0, 0)), VMEM],
+        out_specs=[pl.BlockSpec((span, inner), lambda b: (b, 0)),
+                   pl.BlockSpec((own, we.shape[1]), lambda b: (0, 0))],
+        out_shape=[jax.ShapeDtypeStruct((tokens, inner), BF16),
+                   jax.ShapeDtypeStruct((own, we.shape[1]), BF16)],
         compiler_params=PARAMS,
         cost_estimate=cost(4),
         name="gate_tokens",
-    )(normed, wz)
+    )(normed, wz, patches, we)
 
 
 def outputs(
@@ -685,8 +692,8 @@
     return gains
 
 
-def mix_most(sizes, share, me_ref, pat_ref, we_ref, *refs):
-    (norm, weight, embed_ref, mixed_ref, square_ref), refs = refs[-5:], refs[:-5]
+def mix_most(sizes, share, me_ref, *refs):
+    (norm, weight, mixed_ref, square_ref), refs = refs[-4:], refs[:-4]
     step = pl.program_id(0)
     parts = []
     for size in sizes:
@@ -697,7 +704,6 @@
 
     @pl.when(step == 0)
     def _():
-        embed_ref[...] = mm(pat_ref[...], we_ref[...]).astype(BF16)
         square = None
         for n in range(count):
             v = whole(n)
@@ -721,7 +727,7 @@
     out_ref[...] = (embed_ref[...].astype(F32) + scale * (mixed_ref[...] + got)).astype(BF16)
 
 
-def run_mix(me, patches, we, parts, norm_out, w_out):
+def run_mix(me, embed, parts, norm_out, w_out):
     share = len(parts)
     count = share - 1
     parts = [p if isinstance(p, list) else [p] for p in parts]
@@ -733,21 +739,21 @@
     norms = norm_out.reshape(-1, LANES)
     weights = w_out.reshape(share, inner, width)
     full = pl.BlockSpec((own, width), lambda d, me: (0, 0))
-    embed, mixed, square = pl.pallas_call(
+    mixed, square = pl.pallas_call(
         functools.partial(mix_most, sizes, share),
         grid_spec=pltpu.PrefetchScalarGridSpec(
             num_scalar_prefetch=1,
             grid=(count,),
-            in_specs=[pl.BlockSpec((own, patches.shape[1]), lambda d, me: (0, 0)), VMEM] + [VMEM] * (len(most) + 1)
+            in_specs=[VMEM] * (len(most) + 1)
             + [pl.BlockSpec((1, inner, width), lambda d, me: (me[0] ^ d, 0, 0))],
-            out_specs=[full, full, pl.BlockSpec((own, LANES), lambda d, me: (0, 0))],
+            out_specs=[full, pl.BlockSpec((own, LANES), lambda d, me: (0, 0))],
         ),
-        out_shape=[jax.ShapeDtypeStruct((own, width), BF16), jax.ShapeDtypeStruct((own, width), F32),
+        out_shape=[jax.ShapeDtypeStruct((own, width), F32),
                    jax.ShapeDtypeStruct((own, LANES), F32)],
         compiler_params=PARAMS,
         cost_estimate=cost(0.05),
         name="mix_most",
-    )(me, patches, we, *most, norms, weights)
+    )(me, *most, norms, weights)
     tile = SPAN
     row = lambda n: pl.BlockSpec((tile, n), lambda i, me: (i, 0))
     return pl.pallas_call(
@@ -822,7 +828,9 @@
         normed, xc, bm, cm, cum, step, local, grown = done[c]
         if gate is not None:
             normed, gate = lax.optimization_barrier((normed, gate))
-        ahead = run_gate(normed, w_z) if c == 1 else normed
+        ahead = normed
+        if c == 1:
+            ahead, embed = run_gate(normed, w_z, patches, w_embed, own)
         values = []
         for which in ([[r] for r in range(reps)] if c else [list(range(reps))]):
             got = run_outputs(
@@ -843,7 +851,7 @@
                 per = own // SPAN
                 pieces = values[1 + (r - 1) * per : 1 + r * per]
                 parts[d] = [swap(v, d) for v in pieces]
-    return run_mix(me, patches, w_embed, parts, norm_out, w_out)
+    return run_mix(me, embed, parts, norm_out, w_out)
 
 
 def solution(mesh):

time: 128 us -> 128 us (level)
  no operation moved by 1% of the time
where the time goes in v6:
time: 128 us
  Pallas kernels  66.8 us (52%)
  blocking collectives  34.1 us (27%)
  waiting for transfers between devices  14.1 us (11%)
  starting transfers between devices  8.78 us (7%)
  local copies, waits for them, and re-layouts  3.83 us (3%)
    pallas_call x2, Pallas kernels, run_states(): pl.pallas_call(functools.partial(block_states, heads, per, len(pats), len...  24.9 us
    all_to_all x1, blocking collectives, make_patches(): moved = lax.all_to_all(run_second(moved, length), ALL, 0, 0, tiled=True)  17.1 us
    all_to_all x1, blocking collectives, make_patches(): lax.all_to_all(first.reshape(devices, own, pairs, row_block, LANES), ALL,...  17 us
    pallas_call x3, Pallas kernels, run_outputs(): pl.pallas_call(functools.partial(outputs, heads, chip, chips, len(earlier...  16.7 us
    ppermute x3, waiting for transfers between devices, shift(): return lax.ppermute(value, 'seq', [(i, i + by) for i in range(count - by)])  7.48 us
    ppermute x7, waiting for transfers between devices, swap(): return lax.ppermute(value, HR, [(i, i ^ flip) for i in range(count)])  6.58 us
    pallas_call x1, Pallas kernels, run_mix(): pl.pallas_call(functools.partial(mix_most, sizes, share), grid_spec=pltpu...  6.18 us
    pallas_call x1, Pallas kernels, run_gate(): pl.pallas_call(gate_tokens, grid=(tokens // span,), in_specs=[pl.BlockSpe...  5.15 us
  transfers between devices with their start and end apart: 10, of which 7 were waited for; matrix products, arithmetic and copies ran while one was open for 0% of the time, Pallas kernels for 28%

profile of v6, /device:TPU:17, one launch (start us, length us, event | category | flops | bytes accessed | tf_op | source)
XLA Modules:
  0.0 127.6 jit_solution(4495462554335471389)
XLA Ops:
  0.0 4.5 %first_section.1 = bf16[32,6,8,128]{3,2,1,0:T(8,128)(2,1)} custom-call(s32[1]{0:T(128)} %bitcast.1.pos, f32[3,16]{1,0:T(4,128)} %bitcast.22, f32[16]{0:T(128)} %phase.1, s32[16]{0:T(128)} %mode.1, s32[16]{0:T(128)} %delay.1, s32[2,16]{1,0:T(2,128)} %bitcast.25, f32[2,32]{1,0:T(2,128)} %constant.35.clone.turn_ref, f32[2,3,32,8,128]{4,3,2,1,0:T(8,128)} %bitcast.19, ...), custom_call_target="tpu_custom_call" | custom-call | flops 7000000000 | bytes 21000000 | tf_op jit(solution)/shard_map/first_section/pallas_call | solution.py:219
  4.5 17.0 %all_to_all.10.z_ref = bf16[16,2,6,8,128]{4,3,2,1,0:T(8,128)(2,1)} all-to-all(bf16[16,2,6,8,128]{4,3,2,1,0:T(8,128)(2,1)} %bitcast.16), channel_id=1, replica_groups=mesh['grp'=2,'seq'=4,'head'=2,'rep'=2] {'seq','head','rep'}, dimensions={0} | all-to-all | bytes 786432 | tf_op jit(solution)/shard_map/all_to_all | solution.py:352
  21.6 2.5 %second_section.1 = bf16[16,13,8,128]{3,2,1,0:T(8,128)(2,1)} custom-call(bf16[16,2,6,8,128]{4,3,2,1,0:T(8,128)(2,1)} %all_to_all.10.z_ref, bf16[256,256]{1,0:T(8,128)(2,1)} %constant.40.clone.high_ref, bf16[256,256]{1,0:T(8,128)(2,1)} %constant.41.clone.low_ref), custom_call_target="tpu_custom_call" | custom-call | flops 3000000000 | bytes 9000000 | tf_op jit(solution)/shard_map/second_section/pallas_call | solution.py:277
  24.0 17.1 %all_to_all.11.x_ref = bf16[16,13,8,128]{3,2,1,0:T(8,128)(2,1)} all-to-all(bf16[16,13,8,128]{3,2,1,0:T(8,128)(2,1)} %second_section.1), channel_id=1, replica_groups=mesh['grp'=2,'seq'=4,'head'=2,'rep'=2] {'seq','head','rep'}, dimensions={0} | all-to-all | bytes 851968 | tf_op jit(solution)/shard_map/all_to_all | solution.py:355
  41.1 2.8 %order_patches.1.refs_0_.refs_2_.pat_ref = bf16[520,384]{1,0:T(8,128)(2,1)} custom-call(bf16[16,13,8,128]{3,2,1,0:T(8,128)(2,1)} %all_to_all.11.x_ref, bf16[2,208,384]{2,1,0:T(8,128)(2,1)} %constant.42.clone.perm_ref, bf16[2,192,384]{2,1,0:T(8,128)(2,1)} %constant.43.clone.rim_ref), custom_call_target="tpu_custom_call" | custom-call | flops 3000000000 | bytes 9000000 | tf_op jit(solution)/shard_map/order_patches/pallas_call | solution.py:327
  44.0 1.0 collective-permute-start.1
  44.9 1.6 %collective-permute-done.1.refs_1_ = bf16[520,384]{1,0:T(8,128)(2,1)S(1)} collective-permute-done((bf16[520,384]{1,0:T(8,128)(2,1)}, bf16[520,384]{1,0:T(8,128)(2,1)S(1)}, u32[]{:S(2)}, u32[]{:S(2)}) %collective-permute-start.1) | collective-permute-done | bytes 399392 | tf_op jit(solution)/shard_map/ppermute | solution.py:777
  47.3 12.3 %block_states.2 = (bf16[1024,1024]{1,0:T(8,128)(2,1)}, bf16[1024,512]{1,0:T(8,128)(2,1)}, bf16[1024,128]{1,0:T(8,128)(2,1)}, bf16[1024,128]{1,0:T(8,128)(2,1)}, ...) custom-call(s32[1]{0:T(128)} %bitcast.me_ref, ...), custom_call_target="tpu_custom_call" | custom-call | flops 12999999488 | bytes 39000000 | tf_op jit(solution)/shard_map/block_states/pallas_call | solution.py:515
  60.0 1.4 %collective-permute-done.2.refs_1_ = bf16[520,384]{1,0:T(8,128)(2,1)S(1)} collective-permute-done((bf16[520,384]{1,0:T(8,128)(2,1)S(1)}, bf16[520,384]{1,0:T(8,128)(2,1)S(1)}, u32[]{:S(2)}, u32[]{:S(2)}) %collective-permute-start.2) | collective-permute-done | bytes 399392 | tf_op jit(solution)/shard_map/ppermute | solution.py:777
  62.2 12.6 %block_states.3 = (bf16[1024,1024]{1,0:T(8,128)(2,1)}, bf16[1024,512]{1,0:T(8,128)(2,1)}, bf16[1024,128]{1,0:T(8,128)(2,1)}, bf16[1024,128]{1,0:T(8,128)(2,1)}, ...) custom-call(s32[1]{0:T(128)} %bitcast.me_ref, ...), custom_call_target="tpu_custom_call" | custom-call | flops 12999999488 | bytes 39000000 | tf_op jit(solution)/shard_map/block_states/pallas_call | solution.py:515
  75.4 1.3 %collective-permute-start.4 = (bf16[136,512]{1,0:T(8,128)(2,1)}, bf16[136,512]{1,0:T(8,128)(2,1)S(1)}, u32[]{:S(2)}, u32[]{:S(2)}) collective-permute-start(bf16[136,512]{1,0:T(8,128)(2,1)} %get-tuple-element.55), channel_id=1, source_target_pairs={{0,8},{4,12},{1,9},{5,13},{2,10},{6,14},{3,11},{7,15},{16,24},{20,... | collective-permute-start | bytes 417800 | tf_op jit(solution)/shard_map/ppermute | solution.py:782
  76.7 2.7 %collective-permute-start.3 = (bf16[136,512]{1,0:T(8,128)(2,1)}, bf16[136,512]{1,0:T(8,128)(2,1)S(1)}, u32[]{:S(2)}, u32[]{:S(2)}) collective-permute-start(bf16[136,512]{1,0:T(8,128)(2,1)} %get-tuple-element.55), channel_id=1, source_target_pairs={{0,4},{4,8},{8,12},{1,5},{5,9},{9,13},{2,6},{6,10},{10,14},{3,7},{... | collective-permute-start | bytes 417800 | tf_op jit(solution)/shard_map/ppermute | solution.py:782
  79.4 5.1 %gate_tokens.1 = (bf16[1024,512]{1,0:T(8,128)(2,1)}, bf16[512,1024]{1,0:T(8,128)(2,1)}) custom-call(bf16[1024,1024]{1,0:T(8,128)(2,1)} %get-tuple-element.43.normed_ref, bf16[1024,512]{1,0:T(8,128)(2,1)} %refs_0_.3, bf16[520,384]{1,0:T(8,128)(2,1)} %order_patches.1.refs_0_.refs_2_.pat_ref, bf16[384,1024]{1,0:T(8,128)(2,1)} %we.1), custom_call_target="tpu_custom_call" | custom-call | flops 4000000000 | bytes 12000000 | tf_op jit(solution)/shard_map/gate_tokens/pallas_call | solution.py:561
  84.6 1.0 collective-permute-done.4.refs_4_
  85.6 6.4 %collective-permute-done.3.refs_3_ = bf16[136,512]{1,0:T(8,128)(2,1)S(1)} collective-permute-done((bf16[136,512]{1,0:T(8,128)(2,1)}, bf16[136,512]{1,0:T(8,128)(2,1)S(1)}, u32[]{:S(2)}, u32[]{:S(2)}) %collective-permute-start.3) | collective-permute-done | bytes 139296 | tf_op jit(solution)/shard_map/ppermute | solution.py:782
  92.7 4.9 %outputs.3 = (f32[128,512]{1,0:T(8,128)}, f32[128,512]{1,0:T(8,128)}, bf16[512,512]{1,0:T(8,128)(2,1)}) custom-call(s32[1]{0:T(128)} %bitcast.me_ref, bf16[1024,512]{1,0:T(8,128)(2,1)} %get-tuple-element.57.normed_ref, bf16[1024,512]{1,0:T(8,128)(2,1)} %get-tuple-element.47.x_ref, bf16[1024,128]{1,0:T(8,128)(2,1)} %get-tuple-element.48.b_ref, ...), custom_call_target="tpu_custom_call" | custom-call | flops 50000000 | bytes 150000 | tf_op jit(solution)/shard_map/outputs/pallas_call | solution.py:666
  97.7 1.2 collective-permute-start.8
  98.8 4.3 %outputs.4 = bf16[512,512]{1,0:T(8,128)(2,1)} custom-call(s32[1]{0:T(128)} %bitcast.me_ref, bf16[1024,512]{1,0:T(8,128)(2,1)} %get-tuple-element.57.normed_ref, bf16[1024,512]{1,0:T(8,128)(2,1)} %get-tuple-element.47.x_ref, bf16[1024,128]{1,0:T(8,128)(2,1)} %get-tuple-element.48.b_ref, bf16[1024,128]{1,0:T(8,128)(2,1)} %get-tuple-element.49.c_ref, ...), custom_call_target="tpu_custom_call" | custom-call | flops 50000000 | bytes 150000 | tf_op jit(solution)/shard_map/outputs/pallas_call | solution.py:666
  103.2 1.0 collective-permute-start.9
  104.2 7.4 %outputs.5 = (bf16[512,512]{1,0:T(8,128)(2,1)}, bf16[256,512]{1,0:T(8,128)(2,1)}, bf16[256,512]{1,0:T(8,128)(2,1)}) custom-call(s32[1]{0:T(128)} %bitcast.me_ref, bf16[1024,1024]{1,0:T(8,128)(2,1)} %get-tuple-element.60.normed_ref, bf16[1024,512]{1,0:T(8,128)(2,1)} %get-tuple-element.61.x_ref, bf16[1024,128]{1,0:T(8,128)(2,1)} %get-tuple-element.62.b_ref, ...), custom_call_target="tpu_custom_call" | custom-call | flops 50000000 | bytes 150000 | tf_op jit(solution)/shard_map/outputs/pallas_call | solution.py:666
  112.1 1.2 collective-permute-done.6.refs_1_
  114.6 6.2 %mix_most.1 = (f32[512,1024]{1,0:T(8,128)}, f32[512,128]{1,0:T(8,128)}) custom-call(s32[1]{0:T(128)} %bitcast.me_ref, bf16[512,512]{1,0:T(8,128)(2,1)} %get-tuple-element.69.refs_0_, bf16[256,512]{1,0:T(8,128)(2,1)} %copy-done.1, bf16[256,512]{1,0:T(8,128)(2,1)} %copy-done.2, bf16[512,512]{1,0:T(8,128)(2,1)} %copy-done, bf16[16,128]{1,0:T(8,128)(2,1)} %bitcast.17, ...), custom_call_target="tpu_custom_call" | custom-call | flops 50000000 | bytes 150000 | tf_op jit(solution)/shard_map/mix_most/pallas_call | solution.py:742
  120.8 2.0 %collective-permute-done.9.part_ref = bf16[512,512]{1,0:T(8,128)(2,1)S(1)} collective-permute-done((bf16[512,512]{1,0:T(8,128)(2,1)}, bf16[512,512]{1,0:T(8,128)(2,1)S(1)}, u32[]{:S(2)}, u32[]{:S(2)}) %collective-permute-start.9) | collective-permute-done | bytes 524320 | tf_op jit(solution)/shard_map/ppermute | solution.py:777
  123.6 4.0 %mix_last.1 = bf16[512,1024]{1,0:T(8,128)(2,1)} custom-call(s32[1]{0:T(128)} %bitcast.me_ref, bf16[512,1024]{1,0:T(8,128)(2,1)} %get-tuple-element.44.embed_ref, f32[512,1024]{1,0:T(8,128)} %get-tuple-element.73.mixed_ref, f32[512,128]{1,0:T(8,128)} %get-tuple-element.74.square_ref, bf16[512,512]{1,0:T(8,128)(2,1)} %copy-done.6, bf16[16,128]{1,0:T(8,128)(2,1)} %bitcast.18, ...), custom_call_target="tpu_custom_call" | custom-call | flops 3000000000 | bytes 9000000 | tf_op jit(solution)/shard_map/mix_last/pallas_call | solution.py:759
  (29 shorter events, 5.8 us)
Async XLA Ops:
  44.0 2.6 %collective-permute-start.1 = (bf16[520,384]{1,0:T(8,128)(2,1)}, bf16[520,384]{1,0:T(8,128)(2,1)S(1)}, u32[]{:S(2)}, u32[]{:S(2)}) collective-permute-start(bf16[520,384]{1,0:T(8,128)(2,1)} %order_patches.1.refs_0_.refs_2_.pat_ref), channel_id=1, source_target_pairs={{0,1},{1,0},{2,3},{3,2},{4,5},{5,4},{6,7},{7,6},{8,9},{9,8},{10,11... | collective-permute-start | bytes 1198088 | tf_op jit(solution)/shard_map/ppermute | solution.py:777
  44.9 14.7 %collective-permute-start = (bf16[520,384]{1,0:T(8,128)(2,1)}, bf16[520,384]{1,0:T(8,128)(2,1)S(1)}, u32[]{:S(2)}, u32[]{:S(2)}) collective-permute-start(bf16[520,384]{1,0:T(8,128)(2,1)} %order_patches.1.refs_0_.refs_2_.pat_ref), channel_id=1, source_target_pairs={{0,2},{1,3},{2,0},{3,1},{4,6},{5,7},{6,4},{7,5},{8,10},{9,11},{10,... | collective-permute-start | bytes 1198088 | tf_op jit(solution)/shard_map/ppermute | solution.py:777
  46.5 0.8 copy-start.8
  59.6 1.8 %copy-start.7 = (bf16[520,384]{1,0:T(8,128)(2,1)}, bf16[520,384]{1,0:T(8,128)(2,1)S(1)}, u32[]{:S(2)}) copy-start(bf16[520,384]{1,0:T(8,128)(2,1)S(1)} %collective-permute-done.refs_0_.refs_2_) | copy-start | bytes 1198084
  59.6 1.8 %collective-permute-start.2 = (bf16[520,384]{1,0:T(8,128)(2,1)S(1)}, bf16[520,384]{1,0:T(8,128)(2,1)S(1)}, u32[]{:S(2)}, u32[]{:S(2)}) collective-permute-start(bf16[520,384]{1,0:T(8,128)(2,1)S(1)} %collective-permute-done.refs_0_.refs_2_), channel_id=1, source_target_pairs={{0,1},{1,0},{2,3},{3,2},{4,5},{5,4},{6,7},{7,6},{8,9},{9,8},{10,11... | collective-permute-start | bytes 1198088 | tf_op jit(solution)/shard_map/ppermute | solution.py:777
  61.4 0.8 copy-start.9
  74.7 9.9 %collective-permute-start.5 = (bf16[136,512]{1,0:T(8,128)(2,1)}, bf16[136,512]{1,0:T(8,128)(2,1)S(1)}, u32[]{:S(2)}, u32[]{:S(2)}) collective-permute-start(bf16[136,512]{1,0:T(8,128)(2,1)} %get-tuple-element.55), channel_id=1, source_target_pairs={{0,12},{1,13},{2,14},{3,15},{16,28},{17,29},{18,30},{19,31}} | collective-permute-start | bytes 417800 | tf_op jit(solution)/shard_map/ppermute | solution.py:782
  75.4 10.2 %collective-permute-start.4 = (bf16[136,512]{1,0:T(8,128)(2,1)}, bf16[136,512]{1,0:T(8,128)(2,1)S(1)}, u32[]{:S(2)}, u32[]{:S(2)}) collective-permute-start(bf16[136,512]{1,0:T(8,128)(2,1)} %get-tuple-element.55), channel_id=1, source_target_pairs={{0,8},{4,12},{1,9},{5,13},{2,10},{6,14},{3,11},{7,15},{16,24},{20,... | collective-permute-start | bytes 417800 | tf_op jit(solution)/shard_map/ppermute | solution.py:782
  76.7 15.4 %collective-permute-start.3 = (bf16[136,512]{1,0:T(8,128)(2,1)}, bf16[136,512]{1,0:T(8,128)(2,1)S(1)}, u32[]{:S(2)}, u32[]{:S(2)}) collective-permute-start(bf16[136,512]{1,0:T(8,128)(2,1)} %get-tuple-element.55), channel_id=1, source_target_pairs={{0,4},{4,8},{8,12},{1,5},{5,9},{9,13},{2,6},{6,10},{10,14},{3,7},{... | collective-permute-start | bytes 417800 | tf_op jit(solution)/shard_map/ppermute | solution.py:782
  84.6 7.5 %copy-start.3 = (bf16[136,512]{1,0:T(8,128)(2,1)}, bf16[136,512]{1,0:T(8,128)(2,1)S(1)}, u32[]{:S(2)}) copy-start(bf16[136,512]{1,0:T(8,128)(2,1)S(1)} %collective-permute-done.5.refs_5_) | copy-start | bytes 417796
  85.6 6.4 %copy-start.4 = (bf16[136,512]{1,0:T(8,128)(2,1)}, bf16[136,512]{1,0:T(8,128)(2,1)S(1)}, u32[]{:S(2)}) copy-start(bf16[136,512]{1,0:T(8,128)(2,1)S(1)} %collective-permute-done.4.refs_4_) | copy-start | bytes 417796
  92.1 0.6 copy-start.5
  97.7 16.1 %collective-permute-start.8 = (bf16[512,512]{1,0:T(8,128)(2,1)}, bf16[512,512]{1,0:T(8,128)(2,1)S(1)}, u32[]{:S(2)}, u32[]{:S(2)}) collective-permute-start(bf16[512,512]{1,0:T(8,128)(2,1)} %get-tuple-element.72), channel_id=1, source_target_pairs={{0,2},{1,3},{2,0},{3,1},{4,6},{5,7},{6,4},{7,5},{8,10},{9,11},{10,... | collective-permute-start | bytes 1572872 | tf_op jit(solution)/shard_map/ppermute | solution.py:777
  103.2 19.6 %collective-permute-start.9 = (bf16[512,512]{1,0:T(8,128)(2,1)}, bf16[512,512]{1,0:T(8,128)(2,1)S(1)}, u32[]{:S(2)}, u32[]{:S(2)}) collective-permute-start(bf16[512,512]{1,0:T(8,128)(2,1)} %outputs.4), channel_id=1, source_target_pairs={{0,3},{1,2},{2,1},{3,0},{4,7},{5,6},{6,5},{7,4},{8,11},{9,10},{10,... | collective-permute-start | bytes 1572872 | tf_op jit(solution)/shard_map/ppermute | solution.py:777
  111.6 1.8 %collective-permute-start.6 = (bf16[256,512]{1,0:T(8,128)(2,1)}, bf16[256,512]{1,0:T(8,128)(2,1)S(1)}, u32[]{:S(2)}, u32[]{:S(2)}) collective-permute-start(bf16[256,512]{1,0:T(8,128)(2,1)} %get-tuple-element.70), channel_id=1, source_target_pairs={{0,1},{1,0},{2,3},{3,2},{4,5},{5,4},{6,7},{7,6},{8,9},{9,8},{10,11... | collective-permute-start | bytes 786440 | tf_op jit(solution)/shard_map/ppermute | solution.py:777
  111.6 2.1 %collective-permute-start.7 = (bf16[256,512]{1,0:T(8,128)(2,1)}, bf16[256,512]{1,0:T(8,128)(2,1)S(1)}, u32[]{:S(2)}, u32[]{:S(2)}) collective-permute-start(bf16[256,512]{1,0:T(8,128)(2,1)} %get-tuple-element.71), channel_id=1, source_target_pairs={{0,1},{1,0},{2,3},{3,2},{4,5},{5,4},{6,7},{7,6},{8,9},{9,8},{10,11... | collective-permute-start | bytes 786440 | tf_op jit(solution)/shard_map/ppermute | solution.py:777
  113.3 0.7 copy-start.1
  113.7 0.7 copy-start.2
  113.7 0.9 copy-start
  122.8 0.8 copy-start.6

commit v7 on v6

--- a/solution.py
+++ b/solution.py
@@ -407,7 +407,7 @@
     pats, refs = refs[:2], refs[2:]
     halo, we, nin, wx, wbc, wdt, dtb, alog, cx, cbc, spread = refs[:11]
     earlier, refs = refs[11 : 11 + before], refs[11 + before :]
-    normed_ref, x_ref, b_ref, c_ref, cum_ref, step_ref, local_ref, grown_ref, st_ref = refs[:9]
+    normed_ref, x_ref, b_ref, c_ref, cum_ref, local_ref, grown_ref, st_ref = refs[:8]
     xs, bcs, carried, total, low_tri, dts, rows, tail = refs[-8:]
     block = pl.program_id(0)
     state = wbc.shape[1] // 2
@@ -449,7 +449,6 @@
     xs[...] = mm(joined, wx[...]).astype(BF16).astype(F32)
     step_all = dts[...] + rows[0:1]
     step_all = jnp.maximum(step_all, 0.0) + jnp.log1p(jnp.exp(-jnp.abs(step_all)))
-    step_ref[...] = step_all
 
     def conv(buffer, kernel, at):
         out = kernel[0:1] * buffer[at + 17 - taps : at + 17 - taps + SPAN]
@@ -467,7 +466,9 @@
         packed = one + pltpu.roll(two, heads, 1) + pltpu.roll(three, 2 * heads, 1)
         sums = mm(low_tri[...], packed.astype(BF16))
         cum = sums + pltpu.roll(sums, LANES - heads, 1) + pltpu.roll(sums, LANES - 2 * heads, 1)
-        cum_ref[at : at + SPAN] = cum
+        head_lane = lax.broadcasted_iota(jnp.int32, (SPAN, LANES), 1)
+        packed = jnp.where(head_lane < heads, cum, pltpu.roll(step, heads, 1))
+        cum_ref[at : at + SPAN] = packed
         last = cum[SPAN - 1 : SPAN]
         weights = expand(jnp.exp(last - cum) * step, spread)
         grow = expand(
@@ -492,7 +493,7 @@
         if final:
             everything = [e[...] for e in earlier] + [st_ref[...]]
             count = len(everything)
-            send = refs[9]
+            send = refs[8]
             zero = jnp.zeros((state, xs.shape[1]), F32)
             send[0:state] = fold(everything, count, lax.div(me_ref[0], reps), zero).astype(BF16)
             decay = everything[0][state : state + 8]
@@ -520,7 +521,7 @@
             in_specs=[pl.BlockSpec((span, width), lambda b, me: (b % per, 0))] * len(pats)
             + [pl.BlockSpec((8, width), lambda b, me: (own // 8, 0))]
             + [VMEM] * (len(consts) + len(earlier)),
-            out_specs=[row(model), row(inner), row(state), row(state), row(LANES), row(LANES),
+            out_specs=[row(model), row(inner), row(state), row(state), row(LANES),
                        pl.BlockSpec((subs, state, inner), lambda b, me: (b, 0, 0)),
                        pl.BlockSpec((subs, 8, inner), lambda b, me: (b, 0, 0)), fixed]
             + [fixed] * final,
@@ -537,7 +538,7 @@
         ),
         out_shape=[
             shape(tokens, model, t=BF16), shape(tokens, inner, t=BF16), shape(tokens, state, t=BF16),
-            shape(tokens, state, t=BF16), shape(tokens, LANES), shape(tokens, LANES),
+            shape(tokens, state, t=BF16), shape(tokens, LANES),
             shape(blocks, state, inner), shape(blocks, 8, inner), shape(state + 8, inner),
         ] + [shape(state + 8, inner, t=BF16)] * final,
         compiler_params=PARAMS,
@@ -574,7 +575,7 @@
 
 
 def outputs(
-    heads, chip, chips, seqs, reps, which, gated, opening, me_ref, normed_ref, x_ref, b_ref, c_ref, cum_ref, step_ref, local_ref, grown_ref,
+    heads, chip, chips, seqs, reps, which, gated, opening, me_ref, normed_ref, x_ref, b_ref, c_ref, cum_ref, local_ref, grown_ref,
     *refs,
 ):
     if not gated:
@@ -604,7 +605,7 @@
 
     cum = cum_ref[...]
     log_cum = cum * LOG2E
-    back = (log_cum - jnp.log2(step_ref[...])).T
+    back = (log_cum - jnp.log2(pltpu.roll(cum, LANES - heads, 1))).T
     gram = lax.dot_general(
         c_ref[...], b_ref[...], (((1,), (1,)), ((), ())), preferred_element_type=F32
     )
@@ -631,7 +632,7 @@
     cm = c_ref[...]
     high, low = split(local_ref[0] + grown_ref[0, 0:1] * start[...])
     added = mm(jnp.concatenate([cm, cm], axis=1), jnp.concatenate([high, low], axis=0))
-    value = ((y_acc[...] + expand(jnp.exp(cum), spread) * added) * gate).astype(BF16)
+    value = ((y_acc[...] + expand(jnp.exp(jnp.minimum(cum, 0.0)), spread) * added) * gate).astype(BF16)
     whole = 0
     for n, r in enumerate(which):
         if chip or not r:
@@ -648,7 +649,7 @@
             break
 
 
-def run_outputs(heads, chip, chips, reps, which, me, gate, xc, bm, cm, cum, step, local, grown, wz, spread, enter, own):
+def run_outputs(heads, chip, chips, reps, which, me, gate, xc, bm, cm, cum, local, grown, wz, spread, enter, own):
     tokens, inner = xc.shape
     state = cm.shape[1]
     per = own // SPAN
@@ -668,7 +669,7 @@
         grid_spec=pltpu.PrefetchScalarGridSpec(
             num_scalar_prefetch=1,
             grid=(len(which) * per,),
-            in_specs=[row(a.shape[1]) for a in (gate, xc, bm, cm, cum, step)]
+            in_specs=[row(a.shape[1]) for a in (gate, xc, bm, cm, cum)]
             + [pl.BlockSpec((1, state, inner), block3), pl.BlockSpec((1, 8, inner), block3)]
             + [VMEM] * len(extra),
             out_specs=[fixed(shape) for shape in firsts + shapes],
@@ -679,7 +680,7 @@
         compiler_params=PARAMS,
         cost_estimate=cost(0.05),
         name="outputs",
-    )(me, gate, xc, bm, cm, cum, step, local, grown, *extra)
+    )(me, gate, xc, bm, cm, cum, local, grown, *extra)
 
 
 def pick_gains(norm, index, count):
@@ -817,15 +818,15 @@
         got = run_states(
             me, group, start, consts, heads, inner, state, own, ends, c == chips - 1
         )
-        done.append(got[:8])
-        ends.append(got[8])
-    send = got[9]
+        done.append(got[:7])
+        ends.append(got[7])
+    send = got[8]
     earlier = [shift(send, d) for d in range(1, lax.axis_size("seq"))]
     parts = [None] * share
     gate = None
     enter = (ends, earlier)
     for c in list(range(1, chips)) + [0]:
-        normed, xc, bm, cm, cum, step, local, grown = done[c]
+        normed, xc, bm, cm, cum, local, grown = done[c]
         if gate is not None:
             normed, gate = lax.optimization_barrier((normed, gate))
         ahead = normed
@@ -834,7 +835,7 @@
         values = []
         for which in ([[r] for r in range(reps)] if c else [list(range(reps))]):
             got = run_outputs(
-                heads, c, chips, reps, which, me, ahead, xc, bm, cm, cum, step, local, grown,
+                heads, c, chips, reps, which, me, ahead, xc, bm, cm, cum, local, grown,
                 None if c == 1 else w_z, spread, enter if isinstance(enter, tuple) else enter[c], own,
             )
             if isinstance(enter, tuple):

time: 128 us -> 128 us (level)
  no operation moved by 1% of the time
where the time goes in v7:
time: 128 us
  Pallas kernels  67 us (52%)
  blocking collectives  34.1 us (27%)
  waiting for transfers between devices  13.8 us (11%)
  starting transfers between devices  8.71 us (7%)
  local copies, waits for them, and re-layouts  3.85 us (3%)
    pallas_call x2, Pallas kernels, run_states(): pl.pallas_call(functools.partial(block_states, heads, per, len(pats), len...  24.8 us
    all_to_all x1, blocking collectives, make_patches(): moved = lax.all_to_all(run_second(moved, length), ALL, 0, 0, tiled=True)  17.1 us
    all_to_all x1, blocking collectives, make_patches(): lax.all_to_all(first.reshape(devices, own, pairs, row_block, LANES), ALL,...  17 us
    pallas_call x3, Pallas kernels, run_outputs(): pl.pallas_call(functools.partial(outputs, heads, chip, chips, len(earlier...  17 us
    ppermute x3, waiting for transfers between devices, shift(): return lax.ppermute(value, 'seq', [(i, i + by) for i in range(count - by)])  7.48 us
    ppermute x7, waiting for transfers between devices, swap(): return lax.ppermute(value, HR, [(i, i ^ flip) for i in range(count)])  6.37 us
    pallas_call x1, Pallas kernels, run_mix(): pl.pallas_call(functools.partial(mix_most, sizes, share), grid_spec=pltpu...  6.18 us
    pallas_call x1, Pallas kernels, run_gate(): pl.pallas_call(gate_tokens, grid=(tokens // span,), in_specs=[pl.BlockSpe...  5.15 us
  transfers between devices with their start and end apart: 10, of which 7 were waited for; matrix products, arithmetic and copies ran while one was open for 0% of the time, Pallas kernels for 28%

profile of v7, /device:TPU:17, one launch (start us, length us, event | category | flops | bytes accessed | tf_op | source)
XLA Modules:
  0.0 127.6 jit_solution(16193565117815306119)
XLA Ops:
  0.0 4.5 %first_section.1 = bf16[32,6,8,128]{3,2,1,0:T(8,128)(2,1)} custom-call(s32[1]{0:T(128)} %bitcast.1.pos, f32[3,16]{1,0:T(4,128)} %bitcast.22, f32[16]{0:T(128)} %phase.1, s32[16]{0:T(128)} %mode.1, s32[16]{0:T(128)} %delay.1, s32[2,16]{1,0:T(2,128)} %bitcast.25, f32[2,32]{1,0:T(2,128)} %constant.35.clone.turn_ref, f32[2,3,32,8,128]{4,3,2,1,0:T(8,128)} %bitcast.19, ...), custom_call_target="tpu_custom_call" | custom-call | flops 7000000000 | bytes 21000000 | tf_op jit(solution)/shard_map/first_section/pallas_call | solution.py:219
  4.5 17.0 %all_to_all.10.z_ref = bf16[16,2,6,8,128]{4,3,2,1,0:T(8,128)(2,1)} all-to-all(bf16[16,2,6,8,128]{4,3,2,1,0:T(8,128)(2,1)} %bitcast.16), channel_id=1, replica_groups=mesh['grp'=2,'seq'=4,'head'=2,'rep'=2] {'seq','head','rep'}, dimensions={0} | all-to-all | bytes 786432 | tf_op jit(solution)/shard_map/all_to_all | solution.py:352
  21.6 2.5 %second_section.1 = bf16[16,13,8,128]{3,2,1,0:T(8,128)(2,1)} custom-call(bf16[16,2,6,8,128]{4,3,2,1,0:T(8,128)(2,1)} %all_to_all.10.z_ref, bf16[256,256]{1,0:T(8,128)(2,1)} %constant.40.clone.high_ref, bf16[256,256]{1,0:T(8,128)(2,1)} %constant.41.clone.low_ref), custom_call_target="tpu_custom_call" | custom-call | flops 3000000000 | bytes 9000000 | tf_op jit(solution)/shard_map/second_section/pallas_call | solution.py:277
  24.0 17.1 %all_to_all.11.x_ref = bf16[16,13,8,128]{3,2,1,0:T(8,128)(2,1)} all-to-all(bf16[16,13,8,128]{3,2,1,0:T(8,128)(2,1)} %second_section.1), channel_id=1, replica_groups=mesh['grp'=2,'seq'=4,'head'=2,'rep'=2] {'seq','head','rep'}, dimensions={0} | all-to-all | bytes 851968 | tf_op jit(solution)/shard_map/all_to_all | solution.py:355
  41.1 2.9 %order_patches.1.refs_0_.refs_2_.pat_ref = bf16[520,384]{1,0:T(8,128)(2,1)} custom-call(bf16[16,13,8,128]{3,2,1,0:T(8,128)(2,1)} %all_to_all.11.x_ref, bf16[2,208,384]{2,1,0:T(8,128)(2,1)} %constant.42.clone.perm_ref, bf16[2,192,384]{2,1,0:T(8,128)(2,1)} %constant.43.clone.rim_ref), custom_call_target="tpu_custom_call" | custom-call | flops 3000000000 | bytes 9000000 | tf_op jit(solution)/shard_map/order_patches/pallas_call | solution.py:327
  44.0 1.0 collective-permute-start.1
  45.0 1.6 %collective-permute-done.1.refs_1_ = bf16[520,384]{1,0:T(8,128)(2,1)S(1)} collective-permute-done((bf16[520,384]{1,0:T(8,128)(2,1)}, bf16[520,384]{1,0:T(8,128)(2,1)S(1)}, u32[]{:S(2)}, u32[]{:S(2)}) %collective-permute-start.1) | collective-permute-done | bytes 399392 | tf_op jit(solution)/shard_map/ppermute | solution.py:778
  47.3 12.3 %block_states.2 = (bf16[1024,1024]{1,0:T(8,128)(2,1)}, bf16[1024,512]{1,0:T(8,128)(2,1)}, bf16[1024,128]{1,0:T(8,128)(2,1)}, bf16[1024,128]{1,0:T(8,128)(2,1)}, ...) custom-call(s32[1]{0:T(128)} %bitcast.me_ref, ...), custom_call_target="tpu_custom_call" | custom-call | flops 12999999488 | bytes 39000000 | tf_op jit(solution)/shard_map/block_states/pallas_call | solution.py:516
  60.0 1.4 %collective-permute-done.2.refs_1_ = bf16[520,384]{1,0:T(8,128)(2,1)S(1)} collective-permute-done((bf16[520,384]{1,0:T(8,128)(2,1)S(1)}, bf16[520,384]{1,0:T(8,128)(2,1)S(1)}, u32[]{:S(2)}, u32[]{:S(2)}) %collective-permute-start.2) | collective-permute-done | bytes 399392 | tf_op jit(solution)/shard_map/ppermute | solution.py:778
  62.1 12.5 %block_states.3 = (bf16[1024,1024]{1,0:T(8,128)(2,1)}, bf16[1024,512]{1,0:T(8,128)(2,1)}, bf16[1024,128]{1,0:T(8,128)(2,1)}, bf16[1024,128]{1,0:T(8,128)(2,1)}, ...) custom-call(s32[1]{0:T(128)} %bitcast.me_ref, ...), custom_call_target="tpu_custom_call" | custom-call | flops 12999999488 | bytes 39000000 | tf_op jit(solution)/shard_map/block_states/pallas_call | solution.py:516
  75.3 1.3 %collective-permute-start.4 = (bf16[136,512]{1,0:T(8,128)(2,1)}, bf16[136,512]{1,0:T(8,128)(2,1)S(1)}, u32[]{:S(2)}, u32[]{:S(2)}) collective-permute-start(bf16[136,512]{1,0:T(8,128)(2,1)} %get-tuple-element.52), channel_id=1, source_target_pairs={{0,8},{4,12},{1,9},{5,13},{2,10},{6,14},{3,11},{7,15},{16,24},{20,... | collective-permute-start | bytes 417800 | tf_op jit(solution)/shard_map/ppermute | solution.py:783
  76.6 2.7 %collective-permute-start.3 = (bf16[136,512]{1,0:T(8,128)(2,1)}, bf16[136,512]{1,0:T(8,128)(2,1)S(1)}, u32[]{:S(2)}, u32[]{:S(2)}) collective-permute-start(bf16[136,512]{1,0:T(8,128)(2,1)} %get-tuple-element.52), channel_id=1, source_target_pairs={{0,4},{4,8},{8,12},{1,5},{5,9},{9,13},{2,6},{6,10},{10,14},{3,7},{... | collective-permute-start | bytes 417800 | tf_op jit(solution)/shard_map/ppermute | solution.py:783
  79.4 5.1 %gate_tokens.1 = (bf16[1024,512]{1,0:T(8,128)(2,1)}, bf16[512,1024]{1,0:T(8,128)(2,1)}) custom-call(bf16[1024,1024]{1,0:T(8,128)(2,1)} %get-tuple-element.41.normed_ref, bf16[1024,512]{1,0:T(8,128)(2,1)} %refs_0_.3, bf16[520,384]{1,0:T(8,128)(2,1)} %order_patches.1.refs_0_.refs_2_.pat_ref, bf16[384,1024]{1,0:T(8,128)(2,1)} %we.1), custom_call_target="tpu_custom_call" | custom-call | flops 4000000000 | bytes 12000000 | tf_op jit(solution)/shard_map/gate_tokens/pallas_call | solution.py:562
  84.5 1.1 collective-permute-done.4.refs_4_
  85.6 6.4 %collective-permute-done.3.refs_3_ = bf16[136,512]{1,0:T(8,128)(2,1)S(1)} collective-permute-done((bf16[136,512]{1,0:T(8,128)(2,1)}, bf16[136,512]{1,0:T(8,128)(2,1)S(1)}, u32[]{:S(2)}, u32[]{:S(2)}) %collective-permute-start.3) | collective-permute-done | bytes 139296 | tf_op jit(solution)/shard_map/ppermute | solution.py:783
  92.7 5.0 %outputs.3 = (f32[128,512]{1,0:T(8,128)}, f32[128,512]{1,0:T(8,128)}, bf16[512,512]{1,0:T(8,128)(2,1)}) custom-call(s32[1]{0:T(128)} %bitcast.me_ref, bf16[1024,512]{1,0:T(8,128)(2,1)} %get-tuple-element.54.normed_ref, bf16[1024,512]{1,0:T(8,128)(2,1)} %get-tuple-element.45.x_ref, bf16[1024,128]{1,0:T(8,128)(2,1)} %get-tuple-element.46.b_ref, ...), custom_call_target="tpu_custom_call" | custom-call | flops 50000000 | bytes 150000 | tf_op jit(solution)/shard_map/outputs/pallas_call | solution.py:667
  97.7 1.1 collective-permute-start.8
  98.8 4.5 %outputs.4 = bf16[512,512]{1,0:T(8,128)(2,1)} custom-call(s32[1]{0:T(128)} %bitcast.me_ref, bf16[1024,512]{1,0:T(8,128)(2,1)} %get-tuple-element.54.normed_ref, bf16[1024,512]{1,0:T(8,128)(2,1)} %get-tuple-element.45.x_ref, bf16[1024,128]{1,0:T(8,128)(2,1)} %get-tuple-element.46.b_ref, bf16[1024,128]{1,0:T(8,128)(2,1)} %get-tuple-element.47.c_ref, ...), custom_call_target="tpu_custom_call" | custom-call | flops 50000000 | bytes 150000 | tf_op jit(solution)/shard_map/outputs/pallas_call | solution.py:667
  103.3 1.0 collective-permute-start.9
  104.3 7.5 %outputs.5 = (bf16[512,512]{1,0:T(8,128)(2,1)}, bf16[256,512]{1,0:T(8,128)(2,1)}, bf16[256,512]{1,0:T(8,128)(2,1)}) custom-call(s32[1]{0:T(128)} %bitcast.me_ref, bf16[1024,1024]{1,0:T(8,128)(2,1)} %get-tuple-element.57.normed_ref, bf16[1024,512]{1,0:T(8,128)(2,1)} %get-tuple-element.58.x_ref, bf16[1024,128]{1,0:T(8,128)(2,1)} %get-tuple-element.59.b_ref, ...), custom_call_target="tpu_custom_call" | custom-call | flops 50000000 | bytes 150000 | tf_op jit(solution)/shard_map/outputs/pallas_call | solution.py:667
  112.3 1.2 collective-permute-done.6.refs_1_
  114.8 6.2 %mix_most.1 = (f32[512,1024]{1,0:T(8,128)}, f32[512,128]{1,0:T(8,128)}) custom-call(s32[1]{0:T(128)} %bitcast.me_ref, bf16[512,512]{1,0:T(8,128)(2,1)} %get-tuple-element.65.refs_0_, bf16[256,512]{1,0:T(8,128)(2,1)} %copy-done.1, bf16[256,512]{1,0:T(8,128)(2,1)} %copy-done.2, bf16[512,512]{1,0:T(8,128)(2,1)} %copy-done, bf16[16,128]{1,0:T(8,128)(2,1)} %bitcast.17, ...), custom_call_target="tpu_custom_call" | custom-call | flops 50000000 | bytes 150000 | tf_op jit(solution)/shard_map/mix_most/pallas_call | solution.py:743
  121.0 1.8 %collective-permute-done.9.part_ref = bf16[512,512]{1,0:T(8,128)(2,1)S(1)} collective-permute-done((bf16[512,512]{1,0:T(8,128)(2,1)}, bf16[512,512]{1,0:T(8,128)(2,1)S(1)}, u32[]{:S(2)}, u32[]{:S(2)}) %collective-permute-start.9) | collective-permute-done | bytes 524320 | tf_op jit(solution)/shard_map/ppermute | solution.py:778
  123.6 4.0 %mix_last.1 = bf16[512,1024]{1,0:T(8,128)(2,1)} custom-call(s32[1]{0:T(128)} %bitcast.me_ref, bf16[512,1024]{1,0:T(8,128)(2,1)} %get-tuple-element.42.embed_ref, f32[512,1024]{1,0:T(8,128)} %get-tuple-element.69.mixed_ref, f32[512,128]{1,0:T(8,128)} %get-tuple-element.70.square_ref, bf16[512,512]{1,0:T(8,128)(2,1)} %copy-done.6, bf16[16,128]{1,0:T(8,128)(2,1)} %bitcast.18, ...), custom_call_target="tpu_custom_call" | custom-call | flops 3000000000 | bytes 9000000 | tf_op jit(solution)/shard_map/mix_last/pallas_call | solution.py:760
  (29 shorter events, 5.8 us)
Async XLA Ops:
  44.0 2.6 %collective-permute-start.1 = (bf16[520,384]{1,0:T(8,128)(2,1)}, bf16[520,384]{1,0:T(8,128)(2,1)S(1)}, u32[]{:S(2)}, u32[]{:S(2)}) collective-permute-start(bf16[520,384]{1,0:T(8,128)(2,1)} %order_patches.1.refs_0_.refs_2_.pat_ref), channel_id=1, source_target_pairs={{0,1},{1,0},{2,3},{3,2},{4,5},{5,4},{6,7},{7,6},{8,9},{9,8},{10,11... | collective-permute-start | bytes 1198088 | tf_op jit(solution)/shard_map/ppermute | solution.py:778
  45.0 14.6 %collective-permute-start = (bf16[520,384]{1,0:T(8,128)(2,1)}, bf16[520,384]{1,0:T(8,128)(2,1)S(1)}, u32[]{:S(2)}, u32[]{:S(2)}) collective-permute-start(bf16[520,384]{1,0:T(8,128)(2,1)} %order_patches.1.refs_0_.refs_2_.pat_ref), channel_id=1, source_target_pairs={{0,2},{1,3},{2,0},{3,1},{4,6},{5,7},{6,4},{7,5},{8,10},{9,11},{10,... | collective-permute-start | bytes 1198088 | tf_op jit(solution)/shard_map/ppermute | solution.py:778
  46.5 0.8 copy-start.8
  59.6 1.8 %copy-start.7 = (bf16[520,384]{1,0:T(8,128)(2,1)}, bf16[520,384]{1,0:T(8,128)(2,1)S(1)}, u32[]{:S(2)}) copy-start(bf16[520,384]{1,0:T(8,128)(2,1)S(1)} %collective-permute-done.refs_0_.refs_2_) | copy-start | bytes 1198084
  59.6 1.8 %collective-permute-start.2 = (bf16[520,384]{1,0:T(8,128)(2,1)S(1)}, bf16[520,384]{1,0:T(8,128)(2,1)S(1)}, u32[]{:S(2)}, u32[]{:S(2)}) collective-permute-start(bf16[520,384]{1,0:T(8,128)(2,1)S(1)} %collective-permute-done.refs_0_.refs_2_), channel_id=1, source_target_pairs={{0,1},{1,0},{2,3},{3,2},{4,5},{5,4},{6,7},{7,6},{8,9},{9,8},{10,11... | collective-permute-start | bytes 1198088 | tf_op jit(solution)/shard_map/ppermute | solution.py:778
  61.4 0.8 copy-start.9
  74.7 9.9 %collective-permute-start.5 = (bf16[136,512]{1,0:T(8,128)(2,1)}, bf16[136,512]{1,0:T(8,128)(2,1)S(1)}, u32[]{:S(2)}, u32[]{:S(2)}) collective-permute-start(bf16[136,512]{1,0:T(8,128)(2,1)} %get-tuple-element.52), channel_id=1, source_target_pairs={{0,12},{1,13},{2,14},{3,15},{16,28},{17,29},{18,30},{19,31}} | collective-permute-start | bytes 417800 | tf_op jit(solution)/shard_map/ppermute | solution.py:783
  75.3 10.3 %collective-permute-start.4 = (bf16[136,512]{1,0:T(8,128)(2,1)}, bf16[136,512]{1,0:T(8,128)(2,1)S(1)}, u32[]{:S(2)}, u32[]{:S(2)}) collective-permute-start(bf16[136,512]{1,0:T(8,128)(2,1)} %get-tuple-element.52), channel_id=1, source_target_pairs={{0,8},{4,12},{1,9},{5,13},{2,10},{6,14},{3,11},{7,15},{16,24},{20,... | collective-permute-start | bytes 417800 | tf_op jit(solution)/shard_map/ppermute | solution.py:783
  76.6 15.4 %collective-permute-start.3 = (bf16[136,512]{1,0:T(8,128)(2,1)}, bf16[136,512]{1,0:T(8,128)(2,1)S(1)}, u32[]{:S(2)}, u32[]{:S(2)}) collective-permute-start(bf16[136,512]{1,0:T(8,128)(2,1)} %get-tuple-element.52), channel_id=1, source_target_pairs={{0,4},{4,8},{8,12},{1,5},{5,9},{9,13},{2,6},{6,10},{10,14},{3,7},{... | collective-permute-start | bytes 417800 | tf_op jit(solution)/shard_map/ppermute | solution.py:783
  84.5 7.5 %copy-start.3 = (bf16[136,512]{1,0:T(8,128)(2,1)}, bf16[136,512]{1,0:T(8,128)(2,1)S(1)}, u32[]{:S(2)}) copy-start(bf16[136,512]{1,0:T(8,128)(2,1)S(1)} %collective-permute-done.5.refs_5_) | copy-start | bytes 417796
  85.6 6.4 %copy-start.4 = (bf16[136,512]{1,0:T(8,128)(2,1)}, bf16[136,512]{1,0:T(8,128)(2,1)S(1)}, u32[]{:S(2)}) copy-start(bf16[136,512]{1,0:T(8,128)(2,1)S(1)} %collective-permute-done.4.refs_4_) | copy-start | bytes 417796
  92.0 0.6 copy-start.5
  97.7 16.2 %collective-permute-start.8 = (bf16[512,512]{1,0:T(8,128)(2,1)}, bf16[512,512]{1,0:T(8,128)(2,1)S(1)}, u32[]{:S(2)}, u32[]{:S(2)}) collective-permute-start(bf16[512,512]{1,0:T(8,128)(2,1)} %get-tuple-element.68), channel_id=1, source_target_pairs={{0,2},{1,3},{2,0},{3,1},{4,6},{5,7},{6,4},{7,5},{8,10},{9,11},{10,... | collective-permute-start | bytes 1572872 | tf_op jit(solution)/shard_map/ppermute | solution.py:778
  103.3 19.5 %collective-permute-start.9 = (bf16[512,512]{1,0:T(8,128)(2,1)}, bf16[512,512]{1,0:T(8,128)(2,1)S(1)}, u32[]{:S(2)}, u32[]{:S(2)}) collective-permute-start(bf16[512,512]{1,0:T(8,128)(2,1)} %outputs.4), channel_id=1, source_target_pairs={{0,3},{1,2},{2,1},{3,0},{4,7},{5,6},{6,5},{7,4},{8,11},{9,10},{10,... | collective-permute-start | bytes 1572872 | tf_op jit(solution)/shard_map/ppermute | solution.py:778
  111.8 1.7 %collective-permute-start.6 = (bf16[256,512]{1,0:T(8,128)(2,1)}, bf16[256,512]{1,0:T(8,128)(2,1)S(1)}, u32[]{:S(2)}, u32[]{:S(2)}) collective-permute-start(bf16[256,512]{1,0:T(8,128)(2,1)} %get-tuple-element.66), channel_id=1, source_target_pairs={{0,1},{1,0},{2,3},{3,2},{4,5},{5,4},{6,7},{7,6},{8,9},{9,8},{10,11... | collective-permute-start | bytes 786440 | tf_op jit(solution)/shard_map/ppermute | solution.py:778
  111.8 2.1 %collective-permute-start.7 = (bf16[256,512]{1,0:T(8,128)(2,1)}, bf16[256,512]{1,0:T(8,128)(2,1)S(1)}, u32[]{:S(2)}, u32[]{:S(2)}) collective-permute-start(bf16[256,512]{1,0:T(8,128)(2,1)} %get-tuple-element.67), channel_id=1, source_target_pairs={{0,1},{1,0},{2,3},{3,2},{4,5},{5,4},{6,7},{7,6},{8,9},{9,8},{10,11... | collective-permute-start | bytes 786440 | tf_op jit(solution)/shard_map/ppermute | solution.py:778
  113.5 0.7 copy-start.1
  113.9 0.7 copy-start.2
  113.9 0.9 copy-start
  122.8 0.8 copy-start.6
